TPU v7x, 32 devices: a whole 2x2x4 slice. The times are simulated.
32 devices in a mesh: groups: 2 (over y), neuron: 8 (over z, x), token: 2 (over core).
Axes of the slice: x: 2, y: 2, z: 4, core: 2. Of those that a mesh axis runs over, the one named last changes fastest.
Arguments:
- activations: bfloat16 [8192, 114688], P(('groups', 'token'), 'neuron'), parts along dimension 0, as said below
- basis: float32 [229376, 64], P(('groups', 'neuron')), parts along dimension 0, may hold values from -0.015625 to 0.015625
Outputs:
- embedding: float32 [229376, 64], P(('groups', 'neuron')), parts along dimension 0
There are 2 independent parts, one for each index of `groups`. A program takes and returns all parts, laid end to end along the dimension named above; each array names one. Nothing has to cross between parts.
Inputs may be any that keep to these rules, and one draw needn't show every extreme that they name: Finite real activations whose neurons differ in mean and scale.
All inputs are finite; a program needn't handle non-finite values.
Results may differ from a plain program's by a relative error of at most 0.0043.
Values may be sent and summed in bfloat16 or wider, within the bound.
No kernel may reach another device: no remote copies, remote signals or barrier semaphores. Data moves between devices by JAX's collectives and lax.ppermute only.
A program may use at most 192 MiB of HBM per device.

v0:
```python
import jax
import jax.numpy as jnp
from jax import lax
from jax.sharding import PartitionSpec as P

NEURONS = 114688


def local(activations, basis):
    tok_dev, neu_dev = activations.shape
    tokens = tok_dev * lax.axis_size("token")
    col_sum = jnp.sum(activations.astype(jnp.float32), axis=0)
    col_sq = jnp.sum(jnp.square(activations.astype(jnp.float32)), axis=0)
    col_sum, col_sq = lax.psum((col_sum, col_sq), "token")
    col_mean = col_sum / tokens
    col_scale = lax.rsqrt(col_sq / tokens - col_mean * col_mean + 1e-05)
    scaled = (col_scale[:, None] * basis).astype(jnp.bfloat16)
    offset = jnp.dot(col_mean[None, :], scaled.astype(jnp.float32), precision=lax.Precision.HIGHEST)
    partial_proj = jnp.dot(activations, scaled, preferred_element_type=jnp.float32) - offset
    projection = lax.psum(partial_proj, "neuron").astype(jnp.bfloat16)
    cross = lax.dot_general(
        activations, projection, (((0,), (0,)), ((), ())), preferred_element_type=jnp.float32
    )
    proj_sum = jnp.sum(projection.astype(jnp.float32), axis=0)
    term = cross - col_mean[:, None] * proj_sum[None, :]
    summed = lax.psum(term, "token")
    weighted = summed * col_scale[:, None] / tokens
    gram_part = jnp.einsum("nk,nl->kl", weighted, weighted, precision=lax.Precision.HIGHEST)
    gram = lax.psum(gram_part, "neuron") / NEURONS
    lower = jnp.linalg.cholesky(gram)
    solved = jax.scipy.linalg.solve_triangular(lower, weighted.T, lower=True)
    embedding = solved.T
    return embedding


def solution(mesh):
    placed = (P(("groups", "token"), "neuron"), P(("groups", "neuron"), None))
    return jax.shard_map(
        local, mesh=mesh, in_specs=placed, out_specs=P(("groups", "neuron"), None), check_vma=False
    )
```

profile of v0, /device:TPU:0, one launch (start us, length us, event | category | flops | bytes accessed | tf_op | source)
XLA Modules:
  0.0 235.3 jit_solution(11449491287721878634)
XLA Ops:
  6.5 0.0 all-reduce.7.cloned.1.call-start
  6.5 19.7 %convert_reduce_fusion = (f32[14336]{0:T(1024)}, f32[14336]{0:T(1024)}) fusion(bf16[2048,14336]{1,0:T(8,128)(2,1)} %param.2), kind=kLoop, calls=%fused_computation | loop fusion | flops 117411840 | bytes 58834944 | tf_op jit(solution)/shard_map/reduce_sum | solution.py:12
  26.2 0.0 all-reduce.7.cloned.1.call-update
  26.3 0.0 all-reduce.5.cloned.1.call-start
  26.3 20.7 %all-reduce.7.cloned.1.call-done = (f32[14336]{0:T(1024)}, f32[14336]{0:T(1024)}) async-done(((f32[14336]{0:T(1024)}, f32[14336]{0:T(1024)}), (f32[14336]{0:T(1024)}, f32[14336]{0:T(1024)})) %all-reduce.7.cloned.1.call-update) | async-done | bytes 114704 | tf_op jit(solution)/shard_map/psum | solution.py:14
  47.1 0.9 broadcast_multiply_fusion
  47.9 3.6 %convolution_bitcast_fusion.1 = f32[64]{0:T(128)S(1)} fusion(f32[14336,1]{0,1:T(1,128)S(1)} %bitcast.22, f32[14336,64]{0,1:T(8,128)} %param.3, f32[14336]{0:T(1024)S(1)} %get-tuple-element.10), kind=kOutput, calls=%fused_computation.15 | convolution fusion | flops 12845056 | bytes 3784960 | tf_op jit(solution)/shard_map/dot_general | solution.py:18
  51.5 25.0 %fusion.4 = f32[2048,64]{0,1:T(8,128)S(1)} fusion(bf16[2048,14336]{1,0:T(8,128)(2,1)} %param.2, f32[14336,64]{0,1:T(8,128)} %param.3, f32[14336]{0:T(1024)S(1)} %get-tuple-element.10, f32[64]{0:T(128)S(1)} %convolution_bitcast_fusion.1), kind=kOutput, calls=%fused_computation.10 | convolution fusion | flops 3760062464 | bytes 62972160 | tf_op jit(solution)/shard_map/dot_general | solution.py:19
  76.5 43.5 %all-reduce.8 = bf16[2048,64]{0,1:T(8,128)(2,1)S(1)} all-reduce(f32[2048,64]{0,1:T(8,128)S(1)} %fusion.4), channel_id=1, replica_groups=mesh['groups'=2,'neuron'=8,'token'=2] {'neuron'}, use_global_device_ids=true, to_apply=%region_4.0 | all-reduce | flops 131072 | bytes 786432 | tf_op jit(solution)/shard_map/psum | solution.py:20
  120.0 0.1 convert_reduce_fusion.1
  120.2 22.8 %fusion.1 = f32[14336,64]{0,1:T(8,128)} fusion(bf16[2048,14336]{1,0:T(8,128)(2,1)} %param.2, f32[64]{0:T(128)S(1)} %convert_reduce_fusion.1, f32[14336]{0:T(1024)S(1)} %get-tuple-element.9, bf16[2048,64]{0,1:T(8,128)(2,1)S(1)} %all-reduce.8), kind=kOutput, calls=%fused_computation.4 | convolution fusion | flops 3759931392 | bytes 62710016 | tf_op jit(solution)/shard_map/dot_general | solution.py:21
  143.0 0.0 all-reduce.5.cloned.1.call-update
  143.0 21.6 %all-reduce.5.cloned.1.call-done = f32[14336,64]{0,1:T(8,128)} async-done(((f32[14336,64]{0,1:T(8,128)}), f32[14336,64]{0,1:T(8,128)}) %all-reduce.5.cloned.1.call-update) | async-done | bytes 3670032 | tf_op jit(solution)/shard_map/psum | solution.py:26
  164.6 6.7 %fusion.3 = f32[64,64]{0,1:T(8,128)S(1)} fusion(f32[14336,64]{0,1:T(8,128)} %all-reduce.5.cloned.1.call-done, f32[14336]{0:T(1024)S(1)} %get-tuple-element.10), kind=kOutput, calls=%fused_computation.8 | convolution fusion | flops 706478080 | bytes 3743744 | tf_op jit(solution)/shard_map/nk,nl->kl/dot_general | solution.py:28
  171.3 37.4 %psum.39 = f32[64,64]{0,1:T(8,128)S(1)} all-reduce(f32[64,64]{0,1:T(8,128)S(1)} %fusion.3), channel_id=1, replica_groups=mesh['groups'=2,'neuron'=8,'token'=2] {'neuron'}, use_global_device_ids=true, to_apply=%region_7.0 | all-reduce | flops 4096 | bytes 32768 | tf_op jit(solution)/shard_map/psum | solution.py:29
  208.7 0.1 copy.4
  208.8 5.8 %cholesky.16 = f32[64,64]{1,0:T(8,128)S(1)} custom-call(f32[64,64]{1,0:T(8,128)S(1)} %fusion.12), custom_call_target="Cholesky" | custom-call | tf_op jit(solution)/shard_map/jit(cholesky)/cholesky | solution.py:30
  214.7 0.6 compare_reduce_fusion
  215.3 0.7 fusion.10
  216.0 4.9 %custom-call.7 = f32[1,64,64]{1,2,0:T(8,128)S(1)} custom-call(f32[1,64,64]{2,1,0:T(8,128)S(1)} %fusion.10), custom_call_target="InvertDiagBlocksLowerTriangular" | custom-call | tf_op jit(solution)/shard_map/jit(_solve_triangular)/triangular_solve | solution.py:31
  220.9 7.6 %fusion.2 = f32[14336,64]{0,1:T(8,128)} fusion(f32[14336,64]{0,1:T(8,128)} %all-reduce.5.cloned.1.call-done, f32[14336]{0:T(1024)S(1)} %get-tuple-element.10, f32[1,64,64]{1,2,0:T(8,128)S(1)} %custom-call.7), kind=kOutput, calls=%fused_computation.7 | convolution fusion | flops 706478080 | bytes 7413760 | tf_op jit(solution)/shard_map/jit(_solve_triangular)/triangular_solve | solution.py:31
  (3 shorter events, 0.0 us)
Async XLA Ops:
  6.5 40.5 %all-reduce.7.cloned.1.call-start = ((), (), s32[]{:S(2)}) async-start(), calls=%async_computation.1 | async-start | bytes 229376 | tf_op jit(solution)/shard_map/psum | solution.py:14
  26.3 138.4 %all-reduce.5.cloned.1.call-start = ((), (), s32[]{:S(2)}) async-start(), calls=%async_computation | async-start | bytes 7340032 | tf_op jit(solution)/shard_map/psum | solution.py:26
Sparse Core Ops, SparseCore 0:
  26.4 20.6 all-reduce.6
  143.1 21.4 all-reduce.4
where the time goes:
time: 236 us; the launch traced here: 235 us
  blocking collectives  80.9 us (34%)
  matrix products  65.7 us (28%)
  waiting for transfers between devices  42.4 us (18%)
  other arithmetic  32.8 us (14%)
  between operations  13.5 us (6%)
    psum x1, blocking collectives, local(): projection = lax.psum(partial_proj, 'neuron').astype(jnp.bfloat16)  43.5 us
    psum x1, blocking collectives, local(): gram = lax.psum(gram_part, 'neuron') / NEURONS  37.4 us
    dot_general x1, matrix products, local(): jnp.dot(activations, scaled, preferred_element_type=jnp.float32) - offset  25 us
    dot_general x1, matrix products, local(): lax.dot_general(activations, projection, (((0,), (0,)), ((), ())), prefer...  22.8 us
    psum x1, waiting for transfers between devices, local(): summed = lax.psum(term, 'token')  21.6 us
    psum x1, waiting for transfers between devices, local(): col_sum, col_sq = lax.psum((col_sum, col_sq), 'token')  20.7 us
    reduce_sum x1, other arithmetic, local(): col_sum = jnp.sum(activations.astype(jnp.float32), axis=0)  19.7 us
    another operation x1, matrix products, local(): solved = jax.scipy.linalg.solve_triangular(lower, weighted.T, lower=True)  7.59 us
  transfers between devices with their start and end apart: 2, of which 2 were waited for; matrix products, arithmetic and copies ran while one was open for 0% of the time, Pallas kernels for 0%

commit v1 on v0

v1 whole, which is shorter than its diff:
```python
import jax
import jax.numpy as jnp
from jax import lax
from jax.sharding import PartitionSpec as P

NEURONS = 114688
F32 = jnp.float32
BF16 = jnp.bfloat16
HIGHEST = lax.Precision.HIGHEST


def token_sum(x, m):
    if m == 2:
        return x + lax.ppermute(x, "token", [(0, 1), (1, 0)])
    return lax.psum(x, "token")


def gather_blocks(x, n):
    return lax.all_to_all(jnp.broadcast_to(x[None], (n,) + x.shape), "neuron", 0, 0)


def local(activations, basis):
    tok_dev, neu_dev = activations.shape
    n, m = lax.axis_size("neuron"), lax.axis_size("token")
    tokens = tok_dev * m
    cols = basis.shape[1]
    basis_t = basis.T
    col_sum = jnp.sum(activations.astype(F32), axis=0)
    col_sq = jnp.sum(jnp.square(activations.astype(F32)), axis=0)
    sums = token_sum(jnp.stack([col_sum, col_sq]), m)
    col_mean = sums[0:1] / tokens
    col_scale = lax.rsqrt(sums[1:2] / tokens - col_mean * col_mean + 1e-05)
    scaled = (col_scale * basis_t).astype(BF16)
    offset = jnp.sum(scaled.astype(F32) * col_mean, axis=1, keepdims=True)
    part = lax.dot_general(
        scaled, activations, (((1,), (1,)), ((), ())), preferred_element_type=F32
    ) - offset
    blocks = part.astype(BF16).reshape(cols, n, tok_dev // n).transpose(1, 0, 2)
    blocks = lax.all_to_all(blocks, "neuron", 0, 0)
    own = jnp.sum(blocks.astype(F32), axis=0).astype(BF16)
    proj = gather_blocks(own, n).transpose(1, 0, 2).reshape(cols, tok_dev)
    cross = lax.dot_general(
        proj, activations, (((1,), (0,)), ((), ())), preferred_element_type=F32
    )
    proj_sum = jnp.sum(proj.astype(F32), axis=1, keepdims=True)
    summed = token_sum(cross - proj_sum * col_mean, m)
    weighted = summed * col_scale / tokens
    gram_part = lax.dot_general(
        weighted, weighted, (((1,), (1,)), ((), ())), precision=HIGHEST, preferred_element_type=F32
    )
    gram = jnp.sum(gather_blocks(gram_part, n), axis=0) / NEURONS
    lower = jnp.linalg.cholesky(gram)
    solved = jax.scipy.linalg.solve_triangular(lower, weighted, lower=True)
    return solved.T


def solution(mesh):
    placed = (P(("groups", "token"), "neuron"), P(("groups", "neuron"), None))
    return jax.shard_map(
        local, mesh=mesh, in_specs=placed, out_specs=P(("groups", "neuron"), None), check_vma=False
    )
```

time: 236 us -> 140 us (0.59)
  blocking collectives: 80.9 us -> 38.9 us
  waiting for transfers between devices: 42.4 us -> 7.36 us
  between operations: 13.5 us -> 0.17 us
  matrix products: 65.7 us -> 58.6 us
    psum x2 -> x0, blocking collectives: 80.9 us -> none  [the longest x1 43.5 us: local(): projection = lax.psum(partial_proj, 'neuron').astype(jnp.bfloat16)]
    psum x2 -> x0, waiting for transfers between devices: 42.4 us -> none  [the longest x1 21.6 us: local(): summed = lax.psum(term, 'token')]
    all_to_all x0 -> x3, blocking collectives: none -> 38.9 us  [the longest x2 22.7 us: gather_blocks(): lax.all_to_all(jnp.broadcast_to(x[None], (n,) + x.shape), 'neuron', 0, 0)]
    dot_general x4 -> x3, matrix products: 58.1 us -> 49.7 us  [the longest x1 25 us: local(): lax.dot_general(scaled, activations, (((1,), (1,)), ((), ())), preferred_...]
    ppermute x0 -> x2, waiting for transfers between devices: none -> 7.36 us  [token_sum(): return x + lax.ppermute(x, 'token', [(0, 1), (1, 0)])]
    another operation x2 -> x3, other arithmetic: 5.55 us -> 5.66 us  [the longest x2 5.55 us: local(): solved = jax.scipy.linalg.solve_triangular(lower, weighted, lower=True)]
    reduce_sum x2 -> x5, other arithmetic: 19.8 us -> 19.9 us  [the longest x1 19.2 us: local(): col_sum = jnp.sum(activations.astype(F32), axis=0)]
where the time goes in v1:
time: 140 us
  matrix products  58.6 us (42%)
  blocking collectives  38.9 us (28%)
  other arithmetic  33.3 us (24%)
  waiting for transfers between devices  7.36 us (5%)
    dot_general x1, matrix products, local(): lax.dot_general(scaled, activations, (((1,), (1,)), ((), ())), preferred_...  25 us
    all_to_all x2, blocking collectives, gather_blocks(): lax.all_to_all(jnp.broadcast_to(x[None], (n,) + x.shape), 'neuron', 0, 0)  22.7 us
    dot_general x1, matrix products, local(): lax.dot_general(proj, activations, (((1,), (0,)), ((), ())), preferred_el...  21.5 us
    reduce_sum x1, other arithmetic, local(): col_sum = jnp.sum(activations.astype(F32), axis=0)  19.2 us
    all_to_all x1, blocking collectives, local(): blocks = lax.all_to_all(blocks, 'neuron', 0, 0)  16.2 us
    another operation x1, matrix products, local(): solved = jax.scipy.linalg.solve_triangular(lower, weighted, lower=True)  8.85 us
    ppermute x2, waiting for transfers between devices, token_sum(): return x + lax.ppermute(x, 'token', [(0, 1), (1, 0)])  7.36 us
    another operation x3, other arithmetic, local(): lower = jnp.linalg.cholesky(gram)  6.52 us
  transfers between devices with their start and end apart: 2, of which 2 were waited for; matrix products, arithmetic and copies ran while one was open for 0% of the time, Pallas kernels for 0%

profile of v1, /device:TPU:0, one launch (start us, length us, event | category | flops | bytes accessed | tf_op | source)
XLA Modules:
  0.0 139.9 jit_solution(18050009954585647598)
XLA Ops:
  0.0 19.2 %convert_reduce_fusion = (f32[14336]{0:T(1024)S(1)}, f32[14336]{0:T(1024)S(1)}) fusion(bf16[2048,14336]{1,0:T(8,128)(2,1)} %param.2), kind=kLoop, calls=%fused_computation.1 | loop fusion | flops 117411840 | bytes 58834944 | tf_op jit(solution)/shard_map/reduce_sum | solution.py:28
  19.2 0.1 pad_maximum_fusion
  19.3 0.5 collective-permute-start
  19.9 1.0 collective-permute-done
  20.8 0.1 fusion.10
  21.0 0.1 slice_multiply_fusion
  21.1 0.5 multiply_reduce_fusion
  21.6 25.0 %fusion.1 = bf16[64,2048]{1,0:T(8,128)(2,1)S(1)} fusion(bf16[2048,14336]{1,0:T(8,128)(2,1)} %param.2, f32[14336,64]{0,1:T(8,128)} %param.3, f32[14336]{0:T(1024)S(1)} %bitcast.29, f32[64]{0:T(128)S(1)} %multiply_reduce_fusion), kind=kOutput, calls=%fused_computation.8 | convolution fusion | flops 3760193536 | bytes 62710016 | tf_op jit(solution)/shard_map/dot_general | solution.py:35
  46.6 16.2 %all_to_all.15 = bf16[8,64,256]{2,1,0:T(8,128)(2,1)S(1)} all-to-all(bf16[8,64,256]{2,1,0:T(8,128)(2,1)S(1)} %bitcast.34), channel_id=1, replica_groups=mesh['groups'=2,'neuron'=8,'token'=2] {'neuron'}, dimensions={0} | all-to-all | bytes 524288 | tf_op jit(solution)/shard_map/all_to_all | solution.py:39
  62.9 12.0 %all_to_all.16 = bf16[8,64,256]{2,1,0:T(8,128)(2,1)S(1)} all-to-all(bf16[8,64,256]{2,1,0:T(8,128)(2,1)S(1)} %broadcast_in_dim.5), channel_id=1, replica_groups=mesh['groups'=2,'neuron'=8,'token'=2] {'neuron'}, dimensions={0} | all-to-all | bytes 524288 | tf_op jit(solution)/shard_map/all_to_all | solution.py:19
  74.9 0.1 convert_reduce_fusion.1
  75.0 21.5 %convolution_subtract_fusion = f32[64,14336]{1,0:T(8,128)S(1)} fusion(bf16[64,2048]{1,0:T(8,128)(2,1)S(1)} %bitcast.32, bf16[2048,14336]{1,0:T(8,128)(2,1)} %param.2, f32[14336]{0:T(1024)S(1)} %bitcast.40, f32[64]{0:T(128)S(1)} %convert_reduce_fusion.1), kind=kOutput, calls=%fused_computation.3 | convolution fusion | flops 3759931392 | bytes 62710016 | tf_op jit(solution)/shard_map/dot_general | solution.py:42
  96.6 6.4 %collective-permute-done.1 = f32[64,14336]{1,0:T(8,128)S(1)} collective-permute-done((f32[64,14336]{1,0:T(8,128)S(1)}, f32[64,14336]{1,0:T(8,128)S(1)}, u32[]{:S(2)}, u32[]{:S(2)}) %collective-permute-start.1) | collective-permute-done | bytes 3670048 | tf_op jit(solution)/shard_map/ppermute | solution.py:14
  103.0 3.2 %fusion.3 = f32[64,64]{1,0:T(8,128)S(1)} fusion(f32[64,14336]{1,0:T(8,128)S(1)} %convolution_subtract_fusion, f32[64,14336]{1,0:T(8,128)S(1)} %collective-permute-done.1, f32[14336]{0:T(1024)S(1)} %bitcast.30), kind=kOutput, calls=%fused_computation.10 | convolution fusion | flops 707395584 | bytes 7413760 | tf_op jit(solution)/shard_map/dot_general | solution.py:48
  106.3 0.2 reshape.22
  106.5 10.7 %all_to_all.17 = f32[8,1,4096]{2,1,0:T(1,128)S(1)} all-to-all(f32[8,1,4096]{2,1,0:T(1,128)S(1)} %reshape.22), channel_id=1, replica_groups=mesh['groups'=2,'neuron'=8,'token'=2] {'neuron'}, dimensions={0} | all-to-all | bytes 262144 | tf_op jit(solution)/shard_map/all_to_all | solution.py:19
  117.2 0.5 broadcast.74
  117.7 1.0 reduce.9
  118.7 0.1 reshape.23
  119.0 5.8 %cholesky.16 = f32[64,64]{1,0:T(8,128)S(1)} custom-call(f32[64,64]{1,0:T(8,128)S(1)} %fusion.7), custom_call_target="Cholesky" | custom-call | tf_op jit(solution)/shard_map/jit(cholesky)/cholesky | solution.py:52
  124.9 0.6 compare_reduce_fusion
  125.5 0.7 fusion.5
  126.2 4.9 %custom-call.7 = f32[1,64,64]{1,2,0:T(8,128)S(1)} custom-call(f32[1,64,64]{2,1,0:T(8,128)S(1)} %fusion.5), custom_call_target="InvertDiagBlocksLowerTriangular" | custom-call | tf_op jit(solution)/shard_map/jit(_solve_triangular)/triangular_solve | solution.py:53
  131.1 8.8 %fusion.2 = f32[14336,64]{0,1:T(8,128)} fusion(f32[64,14336]{1,0:T(8,128)} %copy-done, f32[64,14336]{1,0:T(8,128)} %copy-done.2, f32[14336]{0:T(1024)S(1)} %bitcast.31, f32[1,64,64]{1,2,0:T(8,128)S(1)} %custom-call.7), kind=kOutput, calls=%fused_computation.9 | convolution fusion | flops 707395584 | bytes 11083776 | tf_op jit(solution)/shard_map/jit(_solve_triangular)/triangular_solve | solution.py:53
  (18 shorter events, 0.4 us)
Async XLA Ops:
  0.0 21.1 %copy-start.1 = (f32[14336,64]{0,1:T(8,128)S(1)}, f32[14336,64]{0,1:T(8,128)}, u32[]{:S(2)}) copy-start(f32[14336,64]{0,1:T(8,128)} %param.3) | copy-start | bytes 11010052
  19.3 1.5 %collective-permute-start = (f32[2,14336]{1,0:T(2,128)S(1)}, f32[2,14336]{1,0:T(2,128)S(1)}, u32[]{:S(2)}, u32[]{:S(2)}) collective-permute-start(f32[2,14336]{1,0:T(2,128)S(1)} %pad_maximum_fusion), channel_id=1, source_target_pairs={{0,1},{1,0},{2,3},{3,2},{4,5},{5,4},{6,7},{7,6},{8,9},{9,8},{10,11... | collective-permute-start | bytes 344072 | tf_op jit(solution)/shard_map/ppermute | solution.py:14
  96.5 9.7 %copy-start = (f32[64,14336]{1,0:T(8,128)}, f32[64,14336]{1,0:T(8,128)S(1)}, u32[]{:S(2)}) copy-start(f32[64,14336]{1,0:T(8,128)S(1)} %convolution_subtract_fusion) | copy-start | bytes 11010052
  96.5 6.5 %collective-permute-start.1 = (f32[64,14336]{1,0:T(8,128)S(1)}, f32[64,14336]{1,0:T(8,128)S(1)}, u32[]{:S(2)}, u32[]{:S(2)}) collective-permute-start(f32[64,14336]{1,0:T(8,128)S(1)} %convolution_subtract_fusion), channel_id=1, source_target_pairs={{0,1},{1,0},{2,3},{3,2},{4,5},{5,4},{6,7},{7,6},{8,9},{9,8},{10,11... | collective-permute-start | bytes 11010056 | tf_op jit(solution)/shard_map/ppermute | solution.py:14
  103.0 3.2 %copy-start.2 = (f32[64,14336]{1,0:T(8,128)}, f32[64,14336]{1,0:T(8,128)S(1)}, u32[]{:S(2)}) copy-start(f32[64,14336]{1,0:T(8,128)S(1)} %collective-permute-done.1) | copy-start | bytes 11010052

commit v2 on v1

v2 whole, which is shorter than its diff:
```python
import functools

import jax
import jax.numpy as jnp
from jax import lax
from jax.experimental import pallas as pl
from jax.experimental.pallas import tpu as pltpu
from jax.sharding import PartitionSpec as P

NEURONS = 114688
F32 = jnp.float32
BF16 = jnp.bfloat16
MIB = 1 << 20
NT = (((1,), (1,)), ((), ()))


def block_of(size, most):
    return max(b for b in range(128, most + 1, 128) if size % b == 0)


def swap_tokens(x):
    return lax.ppermute(x, "token", [(0, 1), (1, 0)])


def token_sum(x, m):
    return x + swap_tokens(x) if m == 2 else lax.psum(x, "token")


def halves(x):
    head = x.astype(BF16)
    return head, (x - head.astype(F32)).astype(BF16)


def cross_kernel(blocks, proj_ref, act_ref, mean_ref, out_ref, sum_ref):
    j = pl.program_id(0)
    proj = proj_ref[0]
    part = jnp.sum(proj.astype(F32), axis=1, keepdims=True)
    prod = jnp.dot(proj, act_ref[...], preferred_element_type=F32)

    @pl.when(j == 0)
    def _():
        out_ref[...] = prod
        sum_ref[:, 0:1] = part

    @pl.when(j > 0)
    def _():
        out_ref[...] += prod
        sum_ref[:, 0:1] += part

    @pl.when(j == blocks - 1)
    def _():
        out_ref[...] -= sum_ref[:, 0:1] * mean_ref[...]


def cross_slab(proj, act, mean, slab, width):
    blocks, cols, tb = proj.shape
    return pl.pallas_call(
        functools.partial(cross_kernel, blocks),
        grid=(blocks,),
        in_specs=[
            pl.BlockSpec((1, cols, tb), lambda j: (j, 0, 0)),
            pl.BlockSpec((tb, width), lambda j: (j, slab)),
            pl.BlockSpec((1, width), lambda j: (0, slab)),
        ],
        out_specs=pl.BlockSpec((cols, width), lambda j: (0, 0)),
        out_shape=jax.ShapeDtypeStruct((cols, width), F32),
        scratch_shapes=[pltpu.VMEM((cols, 128), F32)],
        compiler_params=pltpu.CompilerParams(vmem_limit_bytes=32 * MIB),
        cost_estimate=pl.CostEstimate(
            flops=2 * blocks * tb * cols * width,
            bytes_accessed=2 * blocks * tb * width,
            transcendentals=0,
        ),
        name="cross",
    )(proj, act, mean)


def combine_kernel(steps, last, tokens, own_ref, got_ref, scale_ref, *refs):
    i = pl.program_id(0)
    if last:
        prev_ref, _, out_ref, gram_ref, acc_ref = refs
    else:
        out_ref, gram_ref, acc_ref = refs
    cols = own_ref.shape[0]
    weighted = (own_ref[...] + got_ref[...]) * scale_ref[...] / tokens
    out_ref[...] = weighted
    both = jnp.concatenate(halves(weighted), axis=0)
    square = lax.dot_general(both, both, NT, preferred_element_type=F32)

    @pl.when(i == 0)
    def _():
        acc_ref[...] = square

    @pl.when(i > 0)
    def _():
        acc_ref[...] += square

    @pl.when(i == steps - 1)
    def _():
        full = acc_ref[...]
        gram = (full[:cols, :cols] + full[cols:, cols:]) + (full[:cols, cols:] + full[cols:, :cols])
        packed = jnp.concatenate([gram[: cols // 2], gram[cols // 2 :]], axis=1)
        if last:
            packed = packed + prev_ref[...]
            for r in range(gram_ref.shape[0]):
                gram_ref[r] = packed
        else:
            gram_ref[...] = packed


def combine_slab(own, got, scale, slab, slabs, tokens, n, prev, buffer):
    cols, width = own.shape
    last = slab == slabs - 1
    nb = block_of(width, 2048)
    steps = width // nb
    here = pl.BlockSpec((cols, nb), lambda i: (0, i))
    there = pl.BlockSpec((cols, nb), lambda i: (0, i + slab * steps))
    packed = (n, cols // 2, 2 * cols) if last else (cols // 2, 2 * cols)
    in_specs = [here, here, pl.BlockSpec((1, nb), lambda i: (0, i + slab * steps))]
    args = [own, got, scale]
    aliases = {}
    if last:
        in_specs += [pl.BlockSpec((cols // 2, 2 * cols), lambda i: (0, 0)), pl.BlockSpec(memory_space=pl.ANY)]
        args += [prev, buffer]
        aliases = {4: 0}
    return pl.pallas_call(
        functools.partial(combine_kernel, steps, last, tokens),
        grid=(steps,),
        in_specs=in_specs,
        out_specs=[there, pl.BlockSpec(packed, lambda i: (0,) * len(packed))],
        out_shape=[
            jax.ShapeDtypeStruct((cols, width * slabs), F32),
            jax.ShapeDtypeStruct(packed, F32),
        ],
        scratch_shapes=[pltpu.VMEM((2 * cols, 2 * cols), F32)],
        input_output_aliases=aliases,
        compiler_params=pltpu.CompilerParams(vmem_limit_bytes=32 * MIB),
        cost_estimate=pl.CostEstimate(
            flops=8 * cols * cols * width, bytes_accessed=12 * cols * width, transcendentals=0
        ),
        name="combine",
    )(*args)


def finish_kernel(gram_ref, weighted_ref, out_ref, inv_ref):
    cols = weighted_ref.shape[0]

    @pl.when(pl.program_id(0) == 0)
    def _():
        packed = jnp.sum(gram_ref[...], axis=0) / NEURONS
        gram = jnp.concatenate([packed[:, :cols], packed[:, cols:]], axis=0)
        row = lax.broadcasted_iota(jnp.int32, (cols, cols), 0)
        lane = lax.broadcasted_iota(jnp.int32, (cols, cols), 1)
        wide = jnp.concatenate([gram, (row == lane).astype(F32)], axis=1)
        tall = [wide[8 * b : 8 * b + 8] for b in range(cols // 8)]
        within = lax.broadcasted_iota(jnp.int32, (8, 1), 0)
        for k in range(cols):
            at, inner = divmod(k, 8)
            pivot_row = tall[at][inner : inner + 1]
            pivot_row = pivot_row / pivot_row[:, k : k + 1]
            for b in range(at, cols // 8):
                factor = tall[b][:, k : k + 1]
                if b == at:
                    factor = jnp.where(within > inner, factor, 0.0)
                tall[b] = tall[b] - factor * pivot_row
        wide = jnp.concatenate(tall, axis=0)
        diag = jnp.sum(jnp.where(row == lane, wide[:, :cols], 0.0), axis=1, keepdims=True)
        head, rest = halves(wide[:, cols:] * lax.rsqrt(diag))
        inv_ref[...] = jnp.concatenate([head, head, rest], axis=1)

    head, rest = halves(weighted_ref[...])
    out_ref[...] = jnp.dot(
        inv_ref[...], jnp.concatenate([head, rest, head], axis=0), preferred_element_type=F32
    )


def finish(grams, weighted):
    cols, width = weighted.shape
    nb = block_of(width, 3584)
    return pl.pallas_call(
        finish_kernel,
        grid=(width // nb,),
        in_specs=[
            pl.BlockSpec(grams.shape, lambda i: (0, 0, 0)),
            pl.BlockSpec((cols, nb), lambda i: (0, i)),
        ],
        out_specs=pl.BlockSpec((cols, nb), lambda i: (0, i)),
        out_shape=jax.ShapeDtypeStruct((cols, width), F32),
        scratch_shapes=[pltpu.VMEM((cols, 3 * cols), BF16)],
        compiler_params=pltpu.CompilerParams(vmem_limit_bytes=32 * MIB),
        name="finish",
    )(grams, weighted)


def local(activations, basis):
    tok_dev, neu_dev = activations.shape
    n, m = lax.axis_size("neuron"), lax.axis_size("token")
    tokens = tok_dev * m
    cols = basis.shape[1]
    basis_t = basis.T
    col_sum = jnp.sum(activations.astype(F32), axis=0)
    col_sq = jnp.sum(jnp.square(activations.astype(F32)), axis=0)
    sums = token_sum(jnp.stack([col_sum, col_sq]), m)
    col_mean = sums[0:1] / tokens
    col_scale = lax.rsqrt(sums[1:2] / tokens - col_mean * col_mean + 1e-05)
    scaled = (col_scale * basis_t).astype(BF16)
    offset = jnp.sum(scaled.astype(F32) * col_mean, axis=1, keepdims=True)
    part = lax.dot_general(scaled, activations, NT, preferred_element_type=F32) - offset
    blocks = part.astype(BF16).reshape(cols, n, tok_dev // n).transpose(1, 0, 2)
    blocks = lax.all_to_all(blocks, "neuron", 0, 0)
    own = jnp.sum(blocks.astype(F32), axis=0).astype(BF16)
    proj = lax.all_to_all(jnp.broadcast_to(own[None], blocks.shape), "neuron", 0, 0)

    slabs = 2
    width = neu_dev // slabs
    terms, swapped = [], []
    for slab in range(slabs):
        terms.append(cross_slab(proj, activations, col_mean, slab, width))
        swapped.append(swap_tokens(terms[-1]))
    weighted = gram = None
    for slab in range(slabs):
        weighted, gram = combine_slab(
            terms[slab], swapped[slab], col_scale, slab, slabs, tokens, n, gram, weighted
        )
    grams = lax.all_to_all(gram, "neuron", 0, 0)
    return finish(grams, weighted).T


def solution(mesh):
    placed = (P(("groups", "token"), "neuron"), P(("groups", "neuron"), None))
    return jax.shard_map(
        local, mesh=mesh, in_specs=placed, out_specs=P(("groups", "neuron"), None), check_vma=False
    )
```

time: 140 us -> 129 us (0.921)
  Pallas kernels: 0 us -> 40.6 us
  matrix products: 58.6 us -> 25 us
  other arithmetic: 33.3 us -> 20.1 us
  waiting for transfers between devices: 7.36 us -> 2.43 us
    pallas_call x0 -> x5, Pallas kernels: none -> 40.6 us  [the longest x2 28 us: cross_slab(): pl.pallas_call(functools.partial(cross_kernel, blocks), grid=(blocks,), i...]
    dot_general x3 -> x1, matrix products: 49.7 us -> 25 us  [local(): lax.dot_general(scaled, activations, NT, preferred_element_type=F32)]
    another operation x5 -> x0, other arithmetic: 12.1 us -> none  [the longest x3 6.52 us: local(): lower = jnp.linalg.cholesky(gram)]
    another operation x1 -> x0, matrix products: 8.85 us -> none  [local(): solved = jax.scipy.linalg.solve_triangular(lower, weighted, lower=True)]
    ppermute x2 -> x3, waiting for transfers between devices: 7.36 us -> 2.43 us  [swap_tokens(): return lax.ppermute(x, 'token', [(0, 1), (1, 0)])]
  transfers between devices with their start and end apart: 2 -> 3, of which waited for: 2 -> 2; matrix products, arithmetic and copies ran while one was open for 0% -> 0% of each run, Pallas kernels for 0% -> 12%
where the time goes in v2:
time: 129 us
  Pallas kernels  40.6 us (31%)
  blocking collectives  39 us (30%)
  matrix products  25 us (19%)
  other arithmetic  20.1 us (16%)
  waiting for transfers between devices  2.43 us (2%)
    pallas_call x2, Pallas kernels, cross_slab(): pl.pallas_call(functools.partial(cross_kernel, blocks), grid=(blocks,), i...  28 us
    dot_general x1, matrix products, local(): lax.dot_general(scaled, activations, NT, preferred_element_type=F32)  25 us
    reduce_sum x1, other arithmetic, local(): col_sum = jnp.sum(activations.astype(F32), axis=0)  19.2 us
    all_to_all x1, blocking collectives, local(): blocks = lax.all_to_all(blocks, 'neuron', 0, 0)  16.2 us
    all_to_all x1, blocking collectives, local(): lax.all_to_all(jnp.broadcast_to(own[None], blocks.shape), 'neuron', 0, 0)  12 us
    all_to_all x1, blocking collectives, local(): grams = lax.all_to_all(gram, 'neuron', 0, 0)  10.9 us
    pallas_call x1, Pallas kernels, finish(): pl.pallas_call(finish_kernel, grid=(width // nb,), in_specs=[pl.BlockSpec...  8.7 us
    pallas_call x2, Pallas kernels, combine_slab(): pl.pallas_call(functools.partial(combine_kernel, steps, last, tokens), gr...  3.94 us
  transfers between devices with their start and end apart: 3, of which 2 were waited for; matrix products, arithmetic and copies ran while one was open for 0% of the time, Pallas kernels for 12%

profile of v2, /device:TPU:0, one launch (start us, length us, event | category | flops | bytes accessed | tf_op | source)
XLA Modules:
  0.0 128.5 jit_solution(3294022482143334028)
XLA Ops:
  0.0 0.0 copy-start
  0.0 19.2 %convert_reduce_fusion = (f32[14336]{0:T(1024)S(1)}, f32[14336]{0:T(1024)S(1)}) fusion(bf16[2048,14336]{1,0:T(8,128)(2,1)} %act_ref.3), kind=kLoop, calls=%fused_computation.1 | loop fusion | flops 117411840 | bytes 58834944 | tf_op jit(solution)/shard_map/reduce_sum | solution.py:201
  19.2 0.1 pad_maximum_fusion
  19.3 0.5 collective-permute-start
  19.9 1.0 collective-permute-done
  20.8 0.1 fusion.3
  21.0 0.1 slice_multiply_fusion
  21.1 0.0 copy-done
  21.1 0.5 multiply_reduce_fusion
  21.6 25.0 %fusion.1 = bf16[64,2048]{1,0:T(8,128)(2,1)S(1)} fusion(bf16[2048,14336]{1,0:T(8,128)(2,1)} %act_ref.3, f32[14336,64]{0,1:T(8,128)} %param.3, f32[14336]{0:T(1024)S(1)} %bitcast.14, f32[64]{0:T(128)S(1)} %multiply_reduce_fusion), kind=kOutput, calls=%fused_computation.6 | convolution fusion | flops 3760193536 | bytes 62710016 | tf_op jit(solution)/shard_map/dot_general | solution.py:208
  46.6 16.2 %all_to_all.15 = bf16[8,64,256]{2,1,0:T(8,128)(2,1)S(1)} all-to-all(bf16[8,64,256]{2,1,0:T(8,128)(2,1)S(1)} %bitcast.17), channel_id=1, replica_groups=mesh['groups'=2,'neuron'=8,'token'=2] {'neuron'}, dimensions={0} | all-to-all | bytes 524288 | tf_op jit(solution)/shard_map/all_to_all | solution.py:210
  62.9 12.0 %all_to_all.16.proj_ref = bf16[8,64,256]{2,1,0:T(8,128)(2,1)S(1)} all-to-all(bf16[8,64,256]{2,1,0:T(8,128)(2,1)S(1)} %broadcast_in_dim.2), channel_id=1, replica_groups=mesh['groups'=2,'neuron'=8,'token'=2] {'neuron'}, dimensions={0} | all-to-all | bytes 524288 | tf_op jit(solution)/shard_map/all_to_all | solution.py:212
  74.8 14.0 %cross.3.own_ref = f32[64,7168]{1,0:T(8,128)S(1)} custom-call(bf16[8,64,256]{2,1,0:T(8,128)(2,1)S(1)} %all_to_all.16.proj_ref, bf16[2048,14336]{1,0:T(8,128)(2,1)} %act_ref.3, f32[1,14336]{1,0:T(1,128)S(1)} %get-tuple-element.15.mean_ref), custom_call_target="tpu_custom_call" | custom-call | flops 1879048192 | bytes 29360128 | tf_op jit(solution)/shard_map/cross/pallas_call | solution.py:57
  88.8 0.1 collective-permute-start.2
  88.9 14.0 %cross.2.own_ref = f32[64,7168]{1,0:T(8,128)S(1)} custom-call(bf16[8,64,256]{2,1,0:T(8,128)(2,1)S(1)} %all_to_all.16.proj_ref, bf16[2048,14336]{1,0:T(8,128)(2,1)} %act_ref.3, f32[1,14336]{1,0:T(1,128)S(1)} %get-tuple-element.15.mean_ref), custom_call_target="tpu_custom_call" | custom-call | flops 1879048192 | bytes 29360128 | tf_op jit(solution)/shard_map/cross/pallas_call | solution.py:57
  102.9 0.5 collective-permute-start.1
  103.5 0.0 collective-permute-done.2.got_ref
  103.5 1.9 %combine.2 = (f32[64,14336]{1,0:T(8,128)S(1)}, f32[32,128]{1,0:T(8,128)S(1)}) custom-call(f32[64,7168]{1,0:T(8,128)S(1)} %cross.3.own_ref, f32[64,7168]{1,0:T(8,128)S(1)} %collective-permute-done.2.got_ref, f32[1,14336]{1,0:T(1,128)S(1)} %get-tuple-element.16.scale_ref), custom_call_target="tpu_custom_call" | custom-call | flops 234881024 | bytes 5505024 | tf_op jit(solution)/shard_map/combine/pallas_call | solution.py:126
  105.4 1.5 %collective-permute-done.1.got_ref = f32[64,7168]{1,0:T(8,128)S(1)} collective-permute-done((f32[64,7168]{1,0:T(8,128)S(1)}, f32[64,7168]{1,0:T(8,128)S(1)}, u32[]{:S(2)}, u32[]{:S(2)}) %collective-permute-start.1) | collective-permute-done | bytes 1835040 | tf_op jit(solution)/shard_map/ppermute | solution.py:22
  106.9 2.0 %combine.3 = (f32[64,14336]{1,0:T(8,128)S(1)}, f32[8,32,128]{2,1,0:T(8,128)S(1)}) custom-call(f32[64,7168]{1,0:T(8,128)S(1)} %cross.2.own_ref, f32[64,7168]{1,0:T(8,128)S(1)} %collective-permute-done.1.got_ref, f32[1,14336]{1,0:T(1,128)S(1)} %get-tuple-element.16.scale_ref, f32[32,128]{1,0:T(8,128)S(1)} %get-tuple-element.9.refs_0_, ...), custom_call_target="tpu_custom_call", output_to_operand_aliasing={{0}: (4, {})} | custom-call | flops 234881024 | bytes 5505024 | tf_op jit(solution)/shard_map/combine/pallas_call | solution.py:126
  108.9 10.9 %all_to_all.17.gram_ref = f32[8,32,128]{2,1,0:T(8,128)S(1)} all-to-all(f32[8,32,128]{2,1,0:T(8,128)S(1)} %get-tuple-element.11), channel_id=1, replica_groups=mesh['groups'=2,'neuron'=8,'token'=2] {'neuron'}, dimensions={0} | all-to-all | bytes 262144 | tf_op jit(solution)/shard_map/all_to_all | solution.py:225
  119.8 8.7 %finish.1 = f32[64,14336]{1,0:T(8,128)} custom-call(f32[8,32,128]{2,1,0:T(8,128)S(1)} %all_to_all.17.gram_ref, f32[64,14336]{1,0:T(8,128)S(1)} %get-tuple-element.12.weighted_ref), custom_call_target="tpu_custom_call" | custom-call | tf_op jit(solution)/shard_map/finish/pallas_call | solution.py:180
  (3 shorter events, 0.1 us)
Async XLA Ops:
  0.0 21.1 %copy-start = (f32[14336,64]{0,1:T(8,128)S(1)}, f32[14336,64]{0,1:T(8,128)}, u32[]{:S(2)}) copy-start(f32[14336,64]{0,1:T(8,128)} %param.3) | copy-start | bytes 11010052
  19.3 1.5 %collective-permute-start = (f32[2,14336]{1,0:T(2,128)S(1)}, f32[2,14336]{1,0:T(2,128)S(1)}, u32[]{:S(2)}, u32[]{:S(2)}) collective-permute-start(f32[2,14336]{1,0:T(2,128)S(1)} %pad_maximum_fusion), channel_id=1, source_target_pairs={{0,1},{1,0},{2,3},{3,2},{4,5},{5,4},{6,7},{7,6},{8,9},{9,8},{10,11... | collective-permute-start | bytes 344072 | tf_op jit(solution)/shard_map/ppermute | solution.py:22
  88.8 14.6 %collective-permute-start.2 = (f32[64,7168]{1,0:T(8,128)S(1)}, f32[64,7168]{1,0:T(8,128)S(1)}, u32[]{:S(2)}, u32[]{:S(2)}) collective-permute-start(f32[64,7168]{1,0:T(8,128)S(1)} %cross.3.own_ref), channel_id=1, source_target_pairs={{0,1},{1,0},{2,3},{3,2},{4,5},{5,4},{6,7},{7,6},{8,9},{9,8},{10,11... | collective-permute-start | bytes 5505032 | tf_op jit(solution)/shard_map/ppermute | solution.py:22
  102.9 4.0 %collective-permute-start.1 = (f32[64,7168]{1,0:T(8,128)S(1)}, f32[64,7168]{1,0:T(8,128)S(1)}, u32[]{:S(2)}, u32[]{:S(2)}) collective-permute-start(f32[64,7168]{1,0:T(8,128)S(1)} %cross.2.own_ref), channel_id=1, source_target_pairs={{0,1},{1,0},{2,3},{3,2},{4,5},{5,4},{6,7},{7,6},{8,9},{9,8},{10,11... | collective-permute-start | bytes 5505032 | tf_op jit(solution)/shard_map/ppermute | solution.py:22

commit v3 on v2

v3 whole, which is shorter than its diff:
```python
import functools

import jax
import jax.numpy as jnp
from jax import lax
from jax.experimental import pallas as pl
from jax.experimental.pallas import tpu as pltpu
from jax.sharding import PartitionSpec as P

NEURONS = 114688
F32 = jnp.float32
BF16 = jnp.bfloat16
MIB = 1 << 20
NT = (((1,), (1,)), ((), ()))
ROWS = 256
CHUNKS = 4
KEEP = 2
DEPTH = 4
DELAY = 1
SCOPED = 6 * MIB


def block_of(size, most):
    return max(b for b in range(128, most + 1, 128) if size % b == 0)


def swap_tokens(x):
    return lax.ppermute(x, "token", [(0, 1), (1, 0)])


def halves(x):
    head = x.astype(BF16)
    return head, (x - head.astype(F32)).astype(BF16)


def stream_kernel(tokens, chunk, loads, at_chunk, starts, *refs):
    projects = at_chunk is not None
    refs = list(refs)
    take = refs.pop
    if loads is not None:
        act_ref = take(0)
    if loads != 0:
        buf_ref = take(0)
    if projects:
        own_ref, got_ref, basis_ref = take(0), take(0), take(0)
        if not starts:
            part_ref = take(0)
    if loads is not None:
        buf_ref, sums_ref = take(0), take(0)
    slots, tok_dev, _ = buf_ref.shape
    rows = tok_dev // ROWS
    if projects:
        proj_ref, stat_ref = take(0), take(0)
    if loads is not None:
        acc_ref, sem = take(0), take(0)
        into = loads % slots
        copies = [
            pltpu.make_async_copy(
                act_ref.at[pl.ds(j * ROWS, ROWS), pl.ds(loads * chunk, chunk)],
                buf_ref.at[into, pl.ds(j * ROWS, ROWS)],
                sem.at[j],
            )
            for j in range(rows)
        ]
        for copy in copies:
            copy.start()
    if projects:
        scaled_ref = take(0)
        held = at_chunk % slots
        sums = own_ref[...] + got_ref[...]
        mean = sums[0:1] / tokens
        scale = lax.rsqrt(sums[1:2] / tokens - mean * mean + 1e-05)
        stat_ref[0:1] = mean
        stat_ref[1:2] = scale
        scaled = (scale * basis_ref[:, at_chunk * chunk : at_chunk * chunk + chunk]).astype(BF16)
        scaled_ref[...] = scaled
        offset = jnp.sum(scaled.astype(F32) * mean, axis=1, keepdims=True)
    for j in range(rows):
        at = slice(j * ROWS, j * ROWS + ROWS)
        if loads is not None:
            copies[j].wait()
            x = buf_ref[into, at, :].astype(F32)
            total = jnp.sum(x.reshape(ROWS // 8, 8, chunk), axis=0)
            square = jnp.sum((x * x).reshape(ROWS // 8, 8, chunk), axis=0)
            if j == 0:
                acc_ref[0:8] = total
                acc_ref[8:16] = square
            else:
                acc_ref[0:8] += total
                acc_ref[8:16] += square
        if projects:
            part = lax.dot_general(
                scaled_ref[...], buf_ref[held, at, :], NT, preferred_element_type=F32
            ) - offset
            if not starts:
                part = part + part_ref[:, at]
            if len(proj_ref.shape) == 3:
                proj_ref[j] = part.astype(BF16)
            else:
                proj_ref[:, at] = part.astype(proj_ref.dtype)
    if loads is not None:
        sums_ref[0:1] = jnp.sum(acc_ref[0:8], axis=0, keepdims=True)
        sums_ref[1:2] = jnp.sum(acc_ref[8:16], axis=0, keepdims=True)


def stream(tokens, n, chunk, act, loads, buf, at, own, got, basis_t, part, last):
    rows, cols = act.shape[0], basis_t.shape[0]
    vmem = pl.BlockSpec(memory_space=pltpu.VMEM)
    args, in_specs, outs, scratch, aliases = [], [], [], [], {}
    if loads is not None:
        args.append(act)
        in_specs.append(pl.BlockSpec(memory_space=pl.ANY))
        outs += [pltpu.VMEM((KEEP, rows, chunk), BF16), jax.ShapeDtypeStruct((2, chunk), F32)]
        scratch += [pltpu.VMEM((16, chunk), F32), pltpu.SemaphoreType.DMA((rows // ROWS,))]
    if loads != 0:
        if loads is not None:
            aliases = {len(args): 0}
        args.append(buf)
        in_specs.append(vmem)
    if at is not None:
        args += [own, got, basis_t]
        in_specs += [vmem] * 3
        if part is not None:
            args.append(part)
            in_specs.append(vmem)
        blocks = last and rows // n == ROWS
        outs += [
            jax.ShapeDtypeStruct((n, cols, ROWS) if blocks else (cols, rows), BF16 if last else F32),
            jax.ShapeDtypeStruct((2, chunk), F32),
        ]
        scratch.append(pltpu.VMEM((cols, chunk), BF16))
    return list(pl.pallas_call(
        functools.partial(stream_kernel, tokens, chunk, loads, at, part is None),
        in_specs=in_specs,
        out_specs=[vmem] * len(outs),
        out_shape=outs,
        scratch_shapes=scratch,
        input_output_aliases=aliases,
        compiler_params=pltpu.CompilerParams(vmem_limit_bytes=SCOPED),
        cost_estimate=pl.CostEstimate(
            flops=8 * rows * chunk * cols, bytes_accessed=2 * rows * chunk, transcendentals=0
        ),
        name="stream",
    )(*args))


def spread_kernel(blocks_ref, out_ref):
    total = jnp.sum(blocks_ref[...].astype(F32), axis=0).astype(BF16)
    for r in range(out_ref.shape[0]):
        out_ref[r] = total


def spread(blocks):
    return pl.pallas_call(
        spread_kernel,
        out_shape=jax.ShapeDtypeStruct(blocks.shape, BF16),
        compiler_params=pltpu.CompilerParams(vmem_limit_bytes=SCOPED),
        name="spread",
    )(blocks)


def cross_kernel(start, sub, proj_ref, act_ref, stats_ref, out_ref, buf_ref, sem):
    depth = buf_ref.shape[0]
    blocks = out_ref.shape[1] // sub
    copies = [
        pltpu.make_async_copy(
            act_ref.at[:, pl.ds(start + s * sub, sub)], buf_ref.at[s % depth], sem.at[s % depth]
        )
        for s in range(blocks)
    ]
    for copy in copies[:depth]:
        copy.start()
    proj = jnp.concatenate([proj_ref[r] for r in range(proj_ref.shape[0])], axis=1)
    total = jnp.sum(proj.astype(F32), axis=1, keepdims=True)
    for s, copy in enumerate(copies):
        here = slice(s * sub, s * sub + sub)
        copy.wait()
        prod = jnp.dot(proj, buf_ref[s % depth], preferred_element_type=F32)
        if s + depth < blocks:
            copies[s + depth].start()
        out_ref[:, here] = prod - total * stats_ref[0:1, here]


def cross(proj, act, stats, start):
    cols, rows = proj.shape[1], act.shape[0]
    width = stats.shape[1]
    sub = block_of(width, 512)
    vmem = pl.BlockSpec(memory_space=pltpu.VMEM)
    return pl.pallas_call(
        functools.partial(cross_kernel, start, sub),
        in_specs=[vmem, pl.BlockSpec(memory_space=pl.ANY), vmem],
        out_specs=vmem,
        out_shape=jax.ShapeDtypeStruct((cols, width), F32),
        scratch_shapes=[pltpu.VMEM((DEPTH, rows, sub), BF16), pltpu.SemaphoreType.DMA((DEPTH,))],
        compiler_params=pltpu.CompilerParams(vmem_limit_bytes=24 * MIB),
        cost_estimate=pl.CostEstimate(
            flops=8 * rows * cols * width, bytes_accessed=2 * rows * width, transcendentals=0
        ),
        name="cross",
    )(proj, act, stats)


def combine_kernel(pieces, first, last, tokens, own_ref, got_ref, stat_ref, *refs):
    i = pl.program_id(0)
    if not first:
        prev_ref, _, *refs = refs
    out_ref, gram_ref, acc_ref = refs
    cols = own_ref.shape[0]
    weighted = (own_ref[...] + got_ref[...]) * stat_ref[1:2] / tokens
    out_ref[...] = weighted
    both = jnp.concatenate(halves(weighted), axis=0)
    square = lax.dot_general(both, both, NT, preferred_element_type=F32)

    @pl.when(i == 0)
    def _():
        acc_ref[...] = square

    @pl.when(i > 0)
    def _():
        acc_ref[...] += square

    @pl.when(i == pieces - 1)
    def _():
        full = acc_ref[...]
        gram = (full[:cols, :cols] + full[cols:, cols:]) + (full[:cols, cols:] + full[cols:, :cols])
        packed = jnp.concatenate([gram[: cols // 2], gram[cols // 2 :]], axis=1)
        if not first:
            packed = packed + prev_ref[...]
        if last:
            for r in range(gram_ref.shape[0]):
                gram_ref[r] = packed
        else:
            gram_ref[...] = packed


def combine(own, got, stats, start, chunk, whole, tokens, n, prev, buffer, last):
    cols = own.shape[0]
    pieces = own.shape[1] // chunk
    first = prev is None
    here = pl.BlockSpec((cols, chunk), lambda i: (0, i))
    there = pl.BlockSpec((cols, chunk), lambda i: (0, i + start // chunk))
    packed = (n, cols // 2, 2 * cols) if last else (cols // 2, 2 * cols)
    in_specs = [here, here, pl.BlockSpec((2, chunk), lambda i: (0, i))]
    args, aliases = [own, got, stats], {}
    if not first:
        in_specs += [pl.BlockSpec((cols // 2, 2 * cols), lambda i: (0, 0)), pl.BlockSpec(memory_space=pl.ANY)]
        args += [prev, buffer]
        aliases = {4: 0}
    return pl.pallas_call(
        functools.partial(combine_kernel, pieces, first, last, tokens),
        grid=(pieces,),
        in_specs=in_specs,
        out_specs=[there, pl.BlockSpec(packed, lambda i: (0,) * len(packed))],
        out_shape=[
            jax.ShapeDtypeStruct((cols, whole), F32),
            jax.ShapeDtypeStruct(packed, F32),
        ],
        scratch_shapes=[pltpu.VMEM((2 * cols, 2 * cols), F32)],
        input_output_aliases=aliases,
        compiler_params=pltpu.CompilerParams(vmem_limit_bytes=12 * MIB),
        cost_estimate=pl.CostEstimate(
            flops=8 * cols * cols * own.shape[1], bytes_accessed=12 * cols * own.shape[1], transcendentals=0
        ),
        name="combine",
    )(*args)


def finish_kernel(gram_ref, weighted_ref, out_ref, inv_ref):
    cols = weighted_ref.shape[0]

    @pl.when(pl.program_id(0) == 0)
    def _():
        packed = jnp.sum(gram_ref[...], axis=0) / NEURONS
        gram = jnp.concatenate([packed[:, :cols], packed[:, cols:]], axis=0)
        row = lax.broadcasted_iota(jnp.int32, (cols, cols), 0)
        lane = lax.broadcasted_iota(jnp.int32, (cols, cols), 1)
        wide = jnp.concatenate([gram, (row == lane).astype(F32)], axis=1)
        tall = [wide[8 * b : 8 * b + 8] for b in range(cols // 8)]
        within = lax.broadcasted_iota(jnp.int32, (8, 1), 0)
        for k in range(cols):
            at, inner = divmod(k, 8)
            pivot_row = tall[at][inner : inner + 1]
            pivot_row = pivot_row / pivot_row[:, k : k + 1]
            for b in range(at, cols // 8):
                factor = tall[b][:, k : k + 1]
                if b == at:
                    factor = jnp.where(within > inner, factor, 0.0)
                tall[b] = tall[b] - factor * pivot_row
        wide = jnp.concatenate(tall, axis=0)
        diag = jnp.sum(jnp.where(row == lane, wide[:, :cols], 0.0), axis=1, keepdims=True)
        head, rest = halves(wide[:, cols:] * lax.rsqrt(diag))
        inv_ref[...] = jnp.concatenate([head, head, rest], axis=1)

    head, rest = halves(weighted_ref[...])
    out_ref[...] = jnp.dot(
        inv_ref[...], jnp.concatenate([head, rest, head], axis=0), preferred_element_type=F32
    )


def finish(grams, weighted):
    cols, width = weighted.shape
    nb = block_of(width, 2048)
    return pl.pallas_call(
        finish_kernel,
        grid=(width // nb,),
        in_specs=[
            pl.BlockSpec(grams.shape, lambda i: (0, 0, 0)),
            pl.BlockSpec((cols, nb), lambda i: (0, i)),
        ],
        out_specs=pl.BlockSpec((cols, nb), lambda i: (0, i)),
        out_shape=jax.ShapeDtypeStruct((cols, width), F32),
        scratch_shapes=[pltpu.VMEM((cols, 3 * cols), BF16)],
        compiler_params=pltpu.CompilerParams(vmem_limit_bytes=8 * MIB),
        name="finish",
    )(grams, weighted)


def local(activations, basis):
    tok_dev, neu_dev = activations.shape
    n, m = lax.axis_size("neuron"), lax.axis_size("token")
    tokens = tok_dev * m
    cols = basis.shape[1]
    basis_t = basis.T
    chunks = next(c for c in (CHUNKS, 7, 2, 1) if neu_dev % (128 * c) == 0)
    chunk = neu_dev // chunks

    own, got, stats = [], [], []
    part = buf = None
    for step in range(chunks + DELAY):
        loads = step if step < chunks else None
        at = step - DELAY if step >= DELAY else None
        sums = (None, None) if at is None else (own[at], got[at])
        results = stream(
            tokens, n, chunk, activations, loads, buf, at, *sums, basis_t, part, at == chunks - 1
        )
        if loads is not None:
            buf = results.pop(0)
            own.append(results.pop(0))
            got.append(swap_tokens(own[-1]))
        if at is not None:
            part = results.pop(0)
            stats.append(results.pop(0))

    blocks = part if part.ndim == 3 else part.reshape(cols, n, tok_dev // n).transpose(1, 0, 2)
    blocks = spread(lax.all_to_all(blocks, "neuron", 0, 0))
    proj = lax.all_to_all(blocks, "neuron", 0, 0)
    if proj.shape[2] % 128:
        proj = proj.transpose(1, 0, 2).reshape(1, cols, tok_dev)

    split = chunks - max(1, chunks // 4)
    spans = [(0, split), (split, chunks)] if split else [(0, chunks)]
    stats = [jnp.concatenate(stats[lo:hi], axis=1) for lo, hi in spans]
    terms = [cross(proj, activations, stat, lo * chunk) for stat, (lo, _) in zip(stats, spans)]
    swapped = [swap_tokens(term) for term in terms]
    weighted = gram = None
    for term, got, stat, (lo, hi) in zip(terms, swapped, stats, spans):
        weighted, gram = combine(
            term, got, stat, lo * chunk, chunk, neu_dev, tokens, n, gram, weighted, hi == chunks
        )
    grams = lax.all_to_all(gram, "neuron", 0, 0)
    return finish(grams, weighted).T


def solution(mesh):
    placed = (P(("groups", "token"), "neuron"), P(("groups", "neuron"), None))
    return jax.shard_map(
        local, mesh=mesh, in_specs=placed, out_specs=P(("groups", "neuron"), None), check_vma=False
    )
```

time: 129 us -> 125 us (0.969)
  Pallas kernels: 40.6 us -> 79.4 us
  blocking collectives: 39 us -> 10.7 us
  matrix products: 25 us -> 0 us
  other arithmetic: 20.1 us -> 0 us
  waiting for transfers between devices: 2.43 us -> 21.2 us
  starting transfers between devices: 1.14 us -> 13.1 us
    pallas_call x4 -> x10, Pallas kernels: 31.9 us -> 69.5 us  [the longest x5 45 us: stream(): pl.pallas_call(functools.partial(stream_kernel, tokens, chunk, loads, at,...]
    all_to_all x2 -> x0, blocking collectives: 28.1 us -> none  [the longest x1 16.2 us: local(): blocks = lax.all_to_all(blocks, 'neuron', 0, 0)]
    dot_general x1 -> x0, matrix products: 25 us -> none  [local(): lax.dot_general(scaled, activations, NT, preferred_element_type=F32)]
    reduce_sum x3 -> x0, other arithmetic: 19.7 us -> none  [the longest x1 19.2 us: local(): col_sum = jnp.sum(activations.astype(F32), axis=0)]
    all_to_all x0 -> x2, waiting for transfers between devices: none -> 17.7 us  [the longest x1 9.24 us: local(): blocks = spread(lax.all_to_all(blocks, 'neuron', 0, 0))]
    all_to_all x0 -> x2, starting transfers between devices: none -> 10.8 us  [the longest x1 7.15 us: local(): blocks = spread(lax.all_to_all(blocks, 'neuron', 0, 0))]
    ppermute x3 -> x6, waiting for transfers between devices: 2.43 us -> 3.44 us  [swap_tokens(): return lax.ppermute(x, 'token', [(0, 1), (1, 0)])]
  transfers between devices with their start and end apart: 3 -> 8, of which waited for: 2 -> 6; matrix products, arithmetic and copies ran while one was open for 0% -> 0% of each run, Pallas kernels for 12% -> 7%
where the time goes in v3:
time: 125 us
  Pallas kernels  79.4 us (64%)
  waiting for transfers between devices  21.2 us (17%)
  starting transfers between devices  13.1 us (10%)
  blocking collectives  10.7 us (9%)
    pallas_call x5, Pallas kernels, stream(): pl.pallas_call(functools.partial(stream_kernel, tokens, chunk, loads, at,...  45 us
    pallas_call x2, Pallas kernels, cross(): pl.pallas_call(functools.partial(cross_kernel, start, sub), in_specs=[vme...  20.8 us
    all_to_all x1, blocking collectives, local(): grams = lax.all_to_all(gram, 'neuron', 0, 0)  10.7 us
    pallas_call x1, Pallas kernels, finish(): pl.pallas_call(finish_kernel, grid=(width // nb,), in_specs=[pl.BlockSpec...  9.9 us
    all_to_all x1, waiting for transfers between devices, local(): blocks = spread(lax.all_to_all(blocks, 'neuron', 0, 0))  9.24 us
    all_to_all x1, waiting for transfers between devices, local(): proj = lax.all_to_all(blocks, 'neuron', 0, 0)  8.48 us
    all_to_all x1, starting transfers between devices, local(): blocks = spread(lax.all_to_all(blocks, 'neuron', 0, 0))  7.15 us
    all_to_all x1, starting transfers between devices, local(): proj = lax.all_to_all(blocks, 'neuron', 0, 0)  3.63 us
  transfers between devices with their start and end apart: 8, of which 6 were waited for; matrix products, arithmetic and copies ran while one was open for 0% of the time, Pallas kernels for 7%

profile of v3, /device:TPU:0, one launch (start us, length us, event | category | flops | bytes accessed | tf_op | source)
XLA Modules:
  0.0 124.6 jit_solution(9572370880021055905)
XLA Ops:
  0.0 5.8 %stream.5 = (bf16[2,2048,3584]{2,1,0:T(8,128)(2,1)S(1)}, f32[2,3584]{1,0:T(2,128)S(1)}) custom-call(bf16[2048,14336]{1,0:T(8,128)(2,1)} %act_ref.3), custom_call_target="tpu_custom_call" | custom-call | flops 3758096384 | bytes 14680064 | tf_op jit(solution)/shard_map/stream/pallas_call | solution.py:132
  5.8 0.5 collective-permute-start
  6.4 0.9 collective-permute-done.refs_3_
  7.2 11.2 %stream.6 = (bf16[2,2048,3584]{2,1,0:T(8,128)(2,1)S(1)}, f32[2,3584]{1,0:T(2,128)S(1)}, f32[64,2048]{1,0:T(8,128)S(1)}, f32[2,3584]{1,0:T(2,128)S(1)}) custom-call(bf16[2048,14336]{1,0:T(8,128)(2,1)} %act_ref.3, bf16[2,2048,3584]{2,1,0:T(8,128)(2,1)S(1)} %get-tuple-element.25.refs_1_, ...), custom_call_target="tpu_custom_call", output_to_operand_aliasing={{0}: (1, {})} | custom-call | flops 3758096384 | bytes 14680064 | tf_op jit(solution)/shard_map/stream/pallas_call | solution.py:132
  18.5 0.4 collective-permute-start.1
  18.9 0.9 collective-permute-done.1.refs_3_
  19.7 11.5 %stream.7 = (bf16[2,2048,3584]{2,1,0:T(8,128)(2,1)S(1)}, f32[2,3584]{1,0:T(2,128)S(1)}, f32[64,2048]{1,0:T(8,128)S(1)}, f32[2,3584]{1,0:T(2,128)S(1)}) custom-call(bf16[2048,14336]{1,0:T(8,128)(2,1)} %act_ref.3, bf16[2,2048,3584]{2,1,0:T(8,128)(2,1)S(1)} %get-tuple-element.27.refs_1_, ...), custom_call_target="tpu_custom_call", output_to_operand_aliasing={{0}: (1, {})} | custom-call | flops 3758096384 | bytes 14680064 | tf_op jit(solution)/shard_map/stream/pallas_call | solution.py:132
  31.2 0.4 collective-permute-start.2
  31.6 0.9 collective-permute-done.2.refs_3_
  32.5 11.3 %stream.8 = (bf16[2,2048,3584]{2,1,0:T(8,128)(2,1)S(1)}, f32[2,3584]{1,0:T(2,128)S(1)}, f32[64,2048]{1,0:T(8,128)S(1)}, f32[2,3584]{1,0:T(2,128)S(1)}) custom-call(bf16[2048,14336]{1,0:T(8,128)(2,1)} %act_ref.3, bf16[2,2048,3584]{2,1,0:T(8,128)(2,1)S(1)} %get-tuple-element.30.refs_1_, ...), custom_call_target="tpu_custom_call", output_to_operand_aliasing={{0}: (1, {})} | custom-call | flops 3758096384 | bytes 14680064 | tf_op jit(solution)/shard_map/stream/pallas_call | solution.py:132
  44.2 0.9 collective-permute-done.3.refs_2_
  45.0 5.2 %stream.9 = (bf16[8,64,256]{2,1,0:T(8,128)(2,1)}, f32[2,3584]{1,0:T(2,128)S(1)}) custom-call(bf16[2,2048,3584]{2,1,0:T(8,128)(2,1)S(1)} %get-tuple-element.33.refs_0_, f32[2,3584]{1,0:T(2,128)S(1)} %get-tuple-element.34.refs_1_, f32[2,3584]{1,0:T(2,128)S(1)} %collective-permute-done.3.refs_2_, f32[64,14336]{1,0:T(8,128)S(1)} %bitcast.5, ...), custom_call_target="tpu_custom_call" | custom-call | flops 3758096384 | bytes 14680064 | tf_op jit(solution)/shard_map/stream/pallas_call | solution.py:132
  50.2 7.1 %all-to-all-start = ((bf16[8,64,256]{2,1,0:T(8,128)(2,1)}), bf16[8,64,256]{2,1,0:T(8,128)(2,1)S(1)}, u32[]{:S(2)}, u32[]{:S(2)}) async-start(bf16[8,64,256]{2,1,0:T(8,128)(2,1)} %get-tuple-element.36), calls=%async_computation | async-start | bytes 524288 | tf_op jit(solution)/shard_map/all_to_all | solution.py:345
  57.4 9.2 %all-to-all-done.blocks_ref = bf16[8,64,256]{2,1,0:T(8,128)(2,1)S(1)} async-done(((bf16[8,64,256]{2,1,0:T(8,128)(2,1)}), bf16[8,64,256]{2,1,0:T(8,128)(2,1)S(1)}, u32[]{:S(2)}, u32[]{:S(2)}) %all-to-all-start) | async-done | bytes 262176 | tf_op jit(solution)/shard_map/all_to_all | solution.py:345
  66.6 0.7 spread.1
  67.4 3.6 %all-to-all-start.1 = ((bf16[8,64,256]{2,1,0:T(8,128)(2,1)}), bf16[8,64,256]{2,1,0:T(8,128)(2,1)S(1)}, u32[]{:S(2)}, u32[]{:S(2)}) async-start(bf16[8,64,256]{2,1,0:T(8,128)(2,1)} %spread.1), calls=%async_computation.1 | async-start | bytes 524288 | tf_op jit(solution)/shard_map/all_to_all | solution.py:346
  71.0 8.5 %all-to-all-done.1.proj_ref = bf16[8,64,256]{2,1,0:T(8,128)(2,1)S(1)} async-done(((bf16[8,64,256]{2,1,0:T(8,128)(2,1)}), bf16[8,64,256]{2,1,0:T(8,128)(2,1)S(1)}, u32[]{:S(2)}, u32[]{:S(2)}) %all-to-all-start.1) | async-done | bytes 262176 | tf_op jit(solution)/shard_map/all_to_all | solution.py:346
  79.5 14.7 %cross.3.own_ref = f32[64,10752]{1,0:T(8,128)S(1)} custom-call(bf16[8,64,256]{2,1,0:T(8,128)(2,1)S(1)} %all-to-all-done.1.proj_ref, bf16[2048,14336]{1,0:T(8,128)(2,1)} %act_ref.3, f32[2,10752]{1,0:T(2,128)S(1)} %constant_dynamic-update-slice_fusion.stats_ref.stat_ref), custom_call_target="tpu_custom_call" | custom-call | flops 11274289152 | bytes 44040192 | tf_op jit(solution)/shard_map/cross/pallas_call | solution.py:189
  94.3 6.1 %cross.2.own_ref = f32[64,3584]{1,0:T(8,128)S(1)} custom-call(bf16[8,64,256]{2,1,0:T(8,128)(2,1)S(1)} %all-to-all-done.1.proj_ref, bf16[2048,14336]{1,0:T(8,128)(2,1)} %act_ref.3, f32[2,3584]{1,0:T(2,128)S(1)} %get-tuple-element.37.stats_ref.stat_ref), custom_call_target="tpu_custom_call" | custom-call | flops 3758096384 | bytes 14680064 | tf_op jit(solution)/shard_map/cross/pallas_call | solution.py:189
  100.4 0.6 collective-permute-start.4
  100.9 2.2 %combine.2 = (f32[64,14336]{1,0:T(8,128)S(1)}, f32[32,128]{1,0:T(8,128)S(1)}) custom-call(f32[64,10752]{1,0:T(8,128)S(1)} %cross.3.own_ref, f32[64,10752]{1,0:T(8,128)S(1)} %collective-permute-done.5.got_ref, f32[2,10752]{1,0:T(2,128)S(1)} %constant_dynamic-update-slice_fusion.stats_ref.stat_ref), custom_call_target="tpu_custom_call" | custom-call | flops 352321536 | bytes 8257536 | tf_op jit(solution)/shard_map/combine/pallas_call | solution.py:249
  103.2 0.7 combine.3
  103.9 10.7 %all_to_all.15.gram_ref = f32[8,32,128]{2,1,0:T(8,128)S(1)} all-to-all(f32[8,32,128]{2,1,0:T(8,128)S(1)} %get-tuple-element.43), channel_id=1, replica_groups=mesh['groups'=2,'neuron'=8,'token'=2] {'neuron'}, dimensions={0} | all-to-all | bytes 262144 | tf_op jit(solution)/shard_map/all_to_all | solution.py:360
  114.7 9.9 %finish.1 = f32[64,14336]{1,0:T(8,128)} custom-call(f32[8,32,128]{2,1,0:T(8,128)S(1)} %all_to_all.15.gram_ref, f32[64,14336]{1,0:T(8,128)S(1)} %get-tuple-element.44.weighted_ref), custom_call_target="tpu_custom_call" | custom-call | tf_op jit(solution)/shard_map/finish/pallas_call | solution.py:303
  (9 shorter events, 0.5 us)
Async XLA Ops:
  0.0 7.2 %copy-start = (f32[14336,64]{0,1:T(8,128)S(1)}, f32[14336,64]{0,1:T(8,128)}, u32[]{:S(2)}) copy-start(f32[14336,64]{0,1:T(8,128)} %param.3) | copy-start | bytes 11010052
  5.8 1.4 %collective-permute-start = (f32[2,3584]{1,0:T(2,128)S(1)}, f32[2,3584]{1,0:T(2,128)S(1)}, u32[]{:S(2)}, u32[]{:S(2)}) collective-permute-start(f32[2,3584]{1,0:T(2,128)S(1)} %get-tuple-element.26.refs_2_), channel_id=1, source_target_pairs={{0,1},{1,0},{2,3},{3,2},{4,5},{5,4},{6,7},{7,6},{8,9},{9,8},{10,11... | collective-permute-start | bytes 86024 | tf_op jit(solution)/shard_map/ppermute | solution.py:28
  18.5 1.3 %collective-permute-start.1 = (f32[2,3584]{1,0:T(2,128)S(1)}, f32[2,3584]{1,0:T(2,128)S(1)}, u32[]{:S(2)}, u32[]{:S(2)}) collective-permute-start(f32[2,3584]{1,0:T(2,128)S(1)} %get-tuple-element.28.refs_2_), channel_id=1, source_target_pairs={{0,1},{1,0},{2,3},{3,2},{4,5},{5,4},{6,7},{7,6},{8,9},{9,8},{10,11... | collective-permute-start | bytes 86024 | tf_op jit(solution)/shard_map/ppermute | solution.py:28
  31.2 1.3 %collective-permute-start.2 = (f32[2,3584]{1,0:T(2,128)S(1)}, f32[2,3584]{1,0:T(2,128)S(1)}, u32[]{:S(2)}, u32[]{:S(2)}) collective-permute-start(f32[2,3584]{1,0:T(2,128)S(1)} %get-tuple-element.31.refs_2_), channel_id=1, source_target_pairs={{0,1},{1,0},{2,3},{3,2},{4,5},{5,4},{6,7},{7,6},{8,9},{9,8},{10,11... | collective-permute-start | bytes 86024 | tf_op jit(solution)/shard_map/ppermute | solution.py:28
  43.7 1.3 %collective-permute-start.3 = (f32[2,3584]{1,0:T(2,128)S(1)}, f32[2,3584]{1,0:T(2,128)S(1)}, u32[]{:S(2)}, u32[]{:S(2)}) collective-permute-start(f32[2,3584]{1,0:T(2,128)S(1)} %get-tuple-element.34.refs_1_), channel_id=1, source_target_pairs={{0,1},{1,0},{2,3},{3,2},{4,5},{5,4},{6,7},{7,6},{8,9},{9,8},{10,11... | collective-permute-start | bytes 86024 | tf_op jit(solution)/shard_map/ppermute | solution.py:28
  50.2 16.4 %all-to-all-start = ((bf16[8,64,256]{2,1,0:T(8,128)(2,1)}), bf16[8,64,256]{2,1,0:T(8,128)(2,1)S(1)}, u32[]{:S(2)}, u32[]{:S(2)}) async-start(bf16[8,64,256]{2,1,0:T(8,128)(2,1)} %get-tuple-element.36), calls=%async_computation | async-start | bytes 524288 | tf_op jit(solution)/shard_map/all_to_all | solution.py:345
  67.4 12.2 %all-to-all-start.1 = ((bf16[8,64,256]{2,1,0:T(8,128)(2,1)}), bf16[8,64,256]{2,1,0:T(8,128)(2,1)S(1)}, u32[]{:S(2)}, u32[]{:S(2)}) async-start(bf16[8,64,256]{2,1,0:T(8,128)(2,1)} %spread.1), calls=%async_computation.1 | async-start | bytes 524288 | tf_op jit(solution)/shard_map/all_to_all | solution.py:346
  94.2 6.7 %collective-permute-start.5 = (f32[64,10752]{1,0:T(8,128)S(1)}, f32[64,10752]{1,0:T(8,128)S(1)}, u32[]{:S(2)}, u32[]{:S(2)}) collective-permute-start(f32[64,10752]{1,0:T(8,128)S(1)} %cross.3.own_ref), channel_id=1, source_target_pairs={{0,1},{1,0},{2,3},{3,2},{4,5},{5,4},{6,7},{7,6},{8,9},{9,8},{10,11... | collective-permute-start | bytes 8257544 | tf_op jit(solution)/shard_map/ppermute | solution.py:28
  100.4 2.8 %collective-permute-start.4 = (f32[64,3584]{1,0:T(8,128)S(1)}, f32[64,3584]{1,0:T(8,128)S(1)}, u32[]{:S(2)}, u32[]{:S(2)}) collective-permute-start(f32[64,3584]{1,0:T(8,128)S(1)} %cross.2.own_ref), channel_id=1, source_target_pairs={{0,1},{1,0},{2,3},{3,2},{4,5},{5,4},{6,7},{7,6},{8,9},{9,8},{10,11... | collective-permute-start | bytes 2752520 | tf_op jit(solution)/shard_map/ppermute | solution.py:28

commit v4 on v3

--- a/solution.py
+++ b/solution.py
@@ -16,6 +16,7 @@
 CHUNKS = 4
 KEEP = 2
 DEPTH = 4
+LANES = 512
 DELAY = 1
 SCOPED = 6 * MIB
 
@@ -75,35 +76,58 @@
         scaled = (scale * basis_ref[:, at_chunk * chunk : at_chunk * chunk + chunk]).astype(BF16)
         scaled_ref[...] = scaled
         offset = jnp.sum(scaled.astype(F32) * mean, axis=1, keepdims=True)
-    for j in range(rows):
-        at = slice(j * ROWS, j * ROWS + ROWS)
-        if loads is not None:
-            copies[j].wait()
-            x = buf_ref[into, at, :].astype(F32)
-            total = jnp.sum(x.reshape(ROWS // 8, 8, chunk), axis=0)
-            square = jnp.sum((x * x).reshape(ROWS // 8, 8, chunk), axis=0)
-            if j == 0:
-                acc_ref[0:8] = total
-                acc_ref[8:16] = square
-            else:
-                acc_ref[0:8] += total
-                acc_ref[8:16] += square
-        if projects:
-            part = lax.dot_general(
-                scaled_ref[...], buf_ref[held, at, :], NT, preferred_element_type=F32
-            ) - offset
-            if not starts:
-                part = part + part_ref[:, at]
-            if len(proj_ref.shape) == 3:
-                proj_ref[j] = part.astype(BF16)
-            else:
-                proj_ref[:, at] = part.astype(proj_ref.dtype)
+
+    def gather(j):
+        pltpu.make_async_copy(
+            act_ref.at[pl.ds(0, ROWS), pl.ds(0, chunk)], buf_ref.at[into, pl.ds(0, ROWS)], sem.at[j]
+        ).wait()
+
+    def add_sums(j):
+        at = pl.ds(pl.multiple_of(j * ROWS, ROWS), ROWS)
+        for lo in range(0, chunk, LANES):
+            here = slice(lo, min(lo + LANES, chunk))
+            x = buf_ref[into, at, here].astype(F32)
+            wide = (ROWS // 8, 8, x.shape[1])
+            acc_ref[0:8, here] += jnp.sum(x.reshape(wide), axis=0)
+            acc_ref[8:16, here] += jnp.sum((x * x).reshape(wide), axis=0)
+
+    def project(j):
+        at = pl.ds(pl.multiple_of(j * ROWS, ROWS), ROWS)
+        part_here = lax.dot_general(
+            scaled_ref[...], buf_ref[held, at, :], NT, preferred_element_type=F32
+        ) - offset
+        if not starts:
+            part_here = part_here + part_ref[j]
+        proj_ref[j] = part_here.astype(proj_ref.dtype)
+
+    if loads is not None:
+        acc_ref[...] = jnp.zeros_like(acc_ref)
+    if loads is None:
+        pl.loop(0, rows)(project)
+    elif not projects:
+
+        @pl.loop(0, rows)
+        def _(j):
+            gather(j)
+            add_sums(j)
+
+    else:
+        project(0)
+
+        @pl.loop(1, rows)
+        def _(j):
+            gather(j - 1)
+            add_sums(j - 1)
+            project(j)
+
+        gather(rows - 1)
+        add_sums(rows - 1)
     if loads is not None:
         sums_ref[0:1] = jnp.sum(acc_ref[0:8], axis=0, keepdims=True)
         sums_ref[1:2] = jnp.sum(acc_ref[8:16], axis=0, keepdims=True)
 
 
-def stream(tokens, n, chunk, act, loads, buf, at, own, got, basis_t, part, last):
+def stream(tokens, chunk, act, loads, buf, at, own, got, basis_t, part, last):
     rows, cols = act.shape[0], basis_t.shape[0]
     vmem = pl.BlockSpec(memory_space=pltpu.VMEM)
     args, in_specs, outs, scratch, aliases = [], [], [], [], {}
@@ -123,9 +147,8 @@
         if part is not None:
             args.append(part)
             in_specs.append(vmem)
-        blocks = last and rows // n == ROWS
         outs += [
-            jax.ShapeDtypeStruct((n, cols, ROWS) if blocks else (cols, rows), BF16 if last else F32),
+            jax.ShapeDtypeStruct((rows // ROWS, cols, ROWS), BF16 if last else F32),
             jax.ShapeDtypeStruct((2, chunk), F32),
         ]
         scratch.append(pltpu.VMEM((cols, chunk), BF16))
@@ -299,7 +322,7 @@
 
 def finish(grams, weighted):
     cols, width = weighted.shape
-    nb = block_of(width, 2048)
+    nb = block_of(width, 3584)
     return pl.pallas_call(
         finish_kernel,
         grid=(width // nb,),
@@ -310,7 +333,7 @@
         out_specs=pl.BlockSpec((cols, nb), lambda i: (0, i)),
         out_shape=jax.ShapeDtypeStruct((cols, width), F32),
         scratch_shapes=[pltpu.VMEM((cols, 3 * cols), BF16)],
-        compiler_params=pltpu.CompilerParams(vmem_limit_bytes=8 * MIB),
+        compiler_params=pltpu.CompilerParams(vmem_limit_bytes=16 * MIB),
         name="finish",
     )(grams, weighted)
 
@@ -331,7 +354,7 @@
         at = step - DELAY if step >= DELAY else None
         sums = (None, None) if at is None else (own[at], got[at])
         results = stream(
-            tokens, n, chunk, activations, loads, buf, at, *sums, basis_t, part, at == chunks - 1
+            tokens, chunk, activations, loads, buf, at, *sums, basis_t, part, at == chunks - 1
         )
         if loads is not None:
             buf = results.pop(0)
@@ -341,7 +364,9 @@
             part = results.pop(0)
             stats.append(results.pop(0))
 
-    blocks = part if part.ndim == 3 else part.reshape(cols, n, tok_dev // n).transpose(1, 0, 2)
+    blocks = part
+    if tok_dev // n != ROWS:
+        blocks = part.transpose(1, 0, 2).reshape(cols, n, tok_dev // n).transpose(1, 0, 2)
     blocks = spread(lax.all_to_all(blocks, "neuron", 0, 0))
     proj = lax.all_to_all(blocks, "neuron", 0, 0)
     if proj.shape[2] % 128:

time: 125 us -> 114 us (0.912)
  Pallas kernels: 79.4 us -> 68.3 us
    pallas_call x5, Pallas kernels: 45 us -> 35.1 us  [stream(): pl.pallas_call(functools.partial(stream_kernel, tokens, chunk, loads, at,...]
where the time goes in v4:
time: 114 us; the launch traced here: 113 us
  Pallas kernels  68.3 us (60%)
  waiting for transfers between devices  21.2 us (19%)
  starting transfers between devices  13.1 us (11%)
  blocking collectives  10.7 us (9%)
    pallas_call x5, Pallas kernels, stream(): pl.pallas_call(functools.partial(stream_kernel, tokens, chunk, loads, at,...  35.1 us
    pallas_call x2, Pallas kernels, cross(): pl.pallas_call(functools.partial(cross_kernel, start, sub), in_specs=[vme...  20.8 us
    all_to_all x1, blocking collectives, local(): grams = lax.all_to_all(gram, 'neuron', 0, 0)  10.7 us
    all_to_all x1, waiting for transfers between devices, local(): blocks = spread(lax.all_to_all(blocks, 'neuron', 0, 0))  9.24 us
    pallas_call x1, Pallas kernels, finish(): pl.pallas_call(finish_kernel, grid=(width // nb,), in_specs=[pl.BlockSpec...  8.7 us
    all_to_all x1, waiting for transfers between devices, local(): proj = lax.all_to_all(blocks, 'neuron', 0, 0)  8.52 us
    all_to_all x1, starting transfers between devices, local(): blocks = spread(lax.all_to_all(blocks, 'neuron', 0, 0))  7.15 us
    all_to_all x1, starting transfers between devices, local(): proj = lax.all_to_all(blocks, 'neuron', 0, 0)  3.59 us
  transfers between devices with their start and end apart: 8, of which 6 were waited for; matrix products, arithmetic and copies ran while one was open for 0% of the time, Pallas kernels for 7%

profile of v4, /device:TPU:0, one launch (start us, length us, event | category | flops | bytes accessed | tf_op | source)
XLA Modules:
  0.0 113.5 jit_solution(5605315266231971889)
XLA Ops:
  0.0 5.8 %stream.5 = (bf16[2,2048,3584]{2,1,0:T(8,128)(2,1)S(1)}, f32[2,3584]{1,0:T(2,128)S(1)}) custom-call(bf16[2048,14336]{1,0:T(8,128)(2,1)} %act_ref.3), custom_call_target="tpu_custom_call" | custom-call | flops 3758096384 | bytes 14680064 | tf_op jit(solution)/shard_map/stream/pallas_call | solution.py:155
  5.8 0.5 collective-permute-start
  6.4 0.9 collective-permute-done.refs_3_
  7.2 7.6 %stream.6 = (bf16[2,2048,3584]{2,1,0:T(8,128)(2,1)S(1)}, f32[2,3584]{1,0:T(2,128)S(1)}, f32[8,64,256]{2,1,0:T(8,128)S(1)}, f32[2,3584]{1,0:T(2,128)S(1)}) custom-call(bf16[2048,14336]{1,0:T(8,128)(2,1)} %act_ref.3, bf16[2,2048,3584]{2,1,0:T(8,128)(2,1)S(1)} %get-tuple-element.25.refs_1_, ...), custom_call_target="tpu_custom_call", output_to_operand_aliasing={{0}: (1, {})} | custom-call | flops 3758096384 | bytes 14680064 | tf_op jit(solution)/shard_map/stream/pallas_call | solution.py:155
  15.3 0.9 collective-permute-done.1.refs_3_
  16.1 7.7 %stream.7 = (bf16[2,2048,3584]{2,1,0:T(8,128)(2,1)S(1)}, f32[2,3584]{1,0:T(2,128)S(1)}, f32[8,64,256]{2,1,0:T(8,128)S(1)}, f32[2,3584]{1,0:T(2,128)S(1)}) custom-call(bf16[2048,14336]{1,0:T(8,128)(2,1)} %act_ref.3, bf16[2,2048,3584]{2,1,0:T(8,128)(2,1)S(1)} %get-tuple-element.27.refs_1_, ...), custom_call_target="tpu_custom_call", output_to_operand_aliasing={{0}: (1, {})} | custom-call | flops 3758096384 | bytes 14680064 | tf_op jit(solution)/shard_map/stream/pallas_call | solution.py:155
  23.8 0.4 collective-permute-start.2
  24.2 0.9 collective-permute-done.2.refs_3_
  25.1 7.7 %stream.8 = (bf16[2,2048,3584]{2,1,0:T(8,128)(2,1)S(1)}, f32[2,3584]{1,0:T(2,128)S(1)}, f32[8,64,256]{2,1,0:T(8,128)S(1)}, f32[2,3584]{1,0:T(2,128)S(1)}) custom-call(bf16[2048,14336]{1,0:T(8,128)(2,1)} %act_ref.3, bf16[2,2048,3584]{2,1,0:T(8,128)(2,1)S(1)} %get-tuple-element.30.refs_1_, ...), custom_call_target="tpu_custom_call", output_to_operand_aliasing={{0}: (1, {})} | custom-call | flops 3758096384 | bytes 14680064 | tf_op jit(solution)/shard_map/stream/pallas_call | solution.py:155
  32.7 0.4 collective-permute-start.3
  33.1 0.9 collective-permute-done.3.refs_2_
  34.0 6.4 %stream.9 = (bf16[8,64,256]{2,1,0:T(8,128)(2,1)}, f32[2,3584]{1,0:T(2,128)S(1)}) custom-call(bf16[2,2048,3584]{2,1,0:T(8,128)(2,1)S(1)} %get-tuple-element.33.refs_0_, f32[2,3584]{1,0:T(2,128)S(1)} %get-tuple-element.34.refs_1_, f32[2,3584]{1,0:T(2,128)S(1)} %collective-permute-done.3.refs_2_, f32[64,14336]{1,0:T(8,128)S(1)} %bitcast.5, ...), custom_call_target="tpu_custom_call" | custom-call | flops 3758096384 | bytes 14680064 | tf_op jit(solution)/shard_map/stream/pallas_call | solution.py:155
  40.4 7.2 %all-to-all-start = ((bf16[8,64,256]{2,1,0:T(8,128)(2,1)}), bf16[8,64,256]{2,1,0:T(8,128)(2,1)S(1)}, u32[]{:S(2)}, u32[]{:S(2)}) async-start(bf16[8,64,256]{2,1,0:T(8,128)(2,1)} %get-tuple-element.36), calls=%async_computation | async-start | bytes 524288 | tf_op jit(solution)/shard_map/all_to_all | solution.py:370
  47.5 9.2 %all-to-all-done.blocks_ref = bf16[8,64,256]{2,1,0:T(8,128)(2,1)S(1)} async-done(((bf16[8,64,256]{2,1,0:T(8,128)(2,1)}), bf16[8,64,256]{2,1,0:T(8,128)(2,1)S(1)}, u32[]{:S(2)}, u32[]{:S(2)}) %all-to-all-start) | async-done | bytes 262176 | tf_op jit(solution)/shard_map/all_to_all | solution.py:370
  56.8 0.7 spread.1
  57.5 3.6 %all-to-all-start.1 = ((bf16[8,64,256]{2,1,0:T(8,128)(2,1)}), bf16[8,64,256]{2,1,0:T(8,128)(2,1)S(1)}, u32[]{:S(2)}, u32[]{:S(2)}) async-start(bf16[8,64,256]{2,1,0:T(8,128)(2,1)} %spread.1), calls=%async_computation.1 | async-start | bytes 524288 | tf_op jit(solution)/shard_map/all_to_all | solution.py:371
  61.1 8.5 %all-to-all-done.1.proj_ref = bf16[8,64,256]{2,1,0:T(8,128)(2,1)S(1)} async-done(((bf16[8,64,256]{2,1,0:T(8,128)(2,1)}), bf16[8,64,256]{2,1,0:T(8,128)(2,1)S(1)}, u32[]{:S(2)}, u32[]{:S(2)}) %all-to-all-start.1) | async-done | bytes 262176 | tf_op jit(solution)/shard_map/all_to_all | solution.py:371
  69.7 14.7 %cross.3.own_ref = f32[64,10752]{1,0:T(8,128)S(1)} custom-call(bf16[8,64,256]{2,1,0:T(8,128)(2,1)S(1)} %all-to-all-done.1.proj_ref, bf16[2048,14336]{1,0:T(8,128)(2,1)} %act_ref.3, f32[2,10752]{1,0:T(2,128)S(1)} %constant_dynamic-update-slice_fusion.stats_ref.stat_ref), custom_call_target="tpu_custom_call" | custom-call | flops 11274289152 | bytes 44040192 | tf_op jit(solution)/shard_map/cross/pallas_call | solution.py:212
  84.5 6.1 %cross.2.own_ref = f32[64,3584]{1,0:T(8,128)S(1)} custom-call(bf16[8,64,256]{2,1,0:T(8,128)(2,1)S(1)} %all-to-all-done.1.proj_ref, bf16[2048,14336]{1,0:T(8,128)(2,1)} %act_ref.3, f32[2,3584]{1,0:T(2,128)S(1)} %get-tuple-element.37.stats_ref.stat_ref), custom_call_target="tpu_custom_call" | custom-call | flops 3758096384 | bytes 14680064 | tf_op jit(solution)/shard_map/cross/pallas_call | solution.py:212
  90.5 0.6 collective-permute-start.4
  91.1 2.2 %combine.2 = (f32[64,14336]{1,0:T(8,128)S(1)}, f32[32,128]{1,0:T(8,128)S(1)}) custom-call(f32[64,10752]{1,0:T(8,128)S(1)} %cross.3.own_ref, f32[64,10752]{1,0:T(8,128)S(1)} %collective-permute-done.5.got_ref, f32[2,10752]{1,0:T(2,128)S(1)} %constant_dynamic-update-slice_fusion.stats_ref.stat_ref), custom_call_target="tpu_custom_call" | custom-call | flops 352321536 | bytes 8257536 | tf_op jit(solution)/shard_map/combine/pallas_call | solution.py:272
  93.3 0.7 combine.3
  94.0 10.7 %all_to_all.15.gram_ref = f32[8,32,128]{2,1,0:T(8,128)S(1)} all-to-all(f32[8,32,128]{2,1,0:T(8,128)S(1)} %get-tuple-element.43), channel_id=1, replica_groups=mesh['groups'=2,'neuron'=8,'token'=2] {'neuron'}, dimensions={0} | all-to-all | bytes 262144 | tf_op jit(solution)/shard_map/all_to_all | solution.py:385
  104.8 8.7 %finish.1 = f32[64,14336]{1,0:T(8,128)} custom-call(f32[8,32,128]{2,1,0:T(8,128)S(1)} %all_to_all.15.gram_ref, f32[64,14336]{1,0:T(8,128)S(1)} %get-tuple-element.44.weighted_ref), custom_call_target="tpu_custom_call" | custom-call | tf_op jit(solution)/shard_map/finish/pallas_call | solution.py:326
  (9 shorter events, 0.5 us)
Async XLA Ops:
  0.0 7.2 %copy-start = (f32[14336,64]{0,1:T(8,128)S(1)}, f32[14336,64]{0,1:T(8,128)}, u32[]{:S(2)}) copy-start(f32[14336,64]{0,1:T(8,128)} %param.3) | copy-start | bytes 11010052
  5.8 1.4 %collective-permute-start = (f32[2,3584]{1,0:T(2,128)S(1)}, f32[2,3584]{1,0:T(2,128)S(1)}, u32[]{:S(2)}, u32[]{:S(2)}) collective-permute-start(f32[2,3584]{1,0:T(2,128)S(1)} %get-tuple-element.26.refs_2_), channel_id=1, source_target_pairs={{0,1},{1,0},{2,3},{3,2},{4,5},{5,4},{6,7},{7,6},{8,9},{9,8},{10,11... | collective-permute-start | bytes 86024 | tf_op jit(solution)/shard_map/ppermute | solution.py:29
  14.9 1.3 %collective-permute-start.1 = (f32[2,3584]{1,0:T(2,128)S(1)}, f32[2,3584]{1,0:T(2,128)S(1)}, u32[]{:S(2)}, u32[]{:S(2)}) collective-permute-start(f32[2,3584]{1,0:T(2,128)S(1)} %get-tuple-element.28.refs_2_), channel_id=1, source_target_pairs={{0,1},{1,0},{2,3},{3,2},{4,5},{5,4},{6,7},{7,6},{8,9},{9,8},{10,11... | collective-permute-start | bytes 86024 | tf_op jit(solution)/shard_map/ppermute | solution.py:29
  23.8 1.3 %collective-permute-start.2 = (f32[2,3584]{1,0:T(2,128)S(1)}, f32[2,3584]{1,0:T(2,128)S(1)}, u32[]{:S(2)}, u32[]{:S(2)}) collective-permute-start(f32[2,3584]{1,0:T(2,128)S(1)} %get-tuple-element.31.refs_2_), channel_id=1, source_target_pairs={{0,1},{1,0},{2,3},{3,2},{4,5},{5,4},{6,7},{7,6},{8,9},{9,8},{10,11... | collective-permute-start | bytes 86024 | tf_op jit(solution)/shard_map/ppermute | solution.py:29
  32.7 1.3 %collective-permute-start.3 = (f32[2,3584]{1,0:T(2,128)S(1)}, f32[2,3584]{1,0:T(2,128)S(1)}, u32[]{:S(2)}, u32[]{:S(2)}) collective-permute-start(f32[2,3584]{1,0:T(2,128)S(1)} %get-tuple-element.34.refs_1_), channel_id=1, source_target_pairs={{0,1},{1,0},{2,3},{3,2},{4,5},{5,4},{6,7},{7,6},{8,9},{9,8},{10,11... | collective-permute-start | bytes 86024 | tf_op jit(solution)/shard_map/ppermute | solution.py:29
  40.4 16.4 %all-to-all-start = ((bf16[8,64,256]{2,1,0:T(8,128)(2,1)}), bf16[8,64,256]{2,1,0:T(8,128)(2,1)S(1)}, u32[]{:S(2)}, u32[]{:S(2)}) async-start(bf16[8,64,256]{2,1,0:T(8,128)(2,1)} %get-tuple-element.36), calls=%async_computation | async-start | bytes 524288 | tf_op jit(solution)/shard_map/all_to_all | solution.py:370
  57.5 12.2 %all-to-all-start.1 = ((bf16[8,64,256]{2,1,0:T(8,128)(2,1)}), bf16[8,64,256]{2,1,0:T(8,128)(2,1)S(1)}, u32[]{:S(2)}, u32[]{:S(2)}) async-start(bf16[8,64,256]{2,1,0:T(8,128)(2,1)} %spread.1), calls=%async_computation.1 | async-start | bytes 524288 | tf_op jit(solution)/shard_map/all_to_all | solution.py:371
  84.4 6.7 %collective-permute-start.5 = (f32[64,10752]{1,0:T(8,128)S(1)}, f32[64,10752]{1,0:T(8,128)S(1)}, u32[]{:S(2)}, u32[]{:S(2)}) collective-permute-start(f32[64,10752]{1,0:T(8,128)S(1)} %cross.3.own_ref), channel_id=1, source_target_pairs={{0,1},{1,0},{2,3},{3,2},{4,5},{5,4},{6,7},{7,6},{8,9},{9,8},{10,11... | collective-permute-start | bytes 8257544 | tf_op jit(solution)/shard_map/ppermute | solution.py:29
  90.5 2.8 %collective-permute-start.4 = (f32[64,3584]{1,0:T(8,128)S(1)}, f32[64,3584]{1,0:T(8,128)S(1)}, u32[]{:S(2)}, u32[]{:S(2)}) collective-permute-start(f32[64,3584]{1,0:T(8,128)S(1)} %cross.2.own_ref), channel_id=1, source_target_pairs={{0,1},{1,0},{2,3},{3,2},{4,5},{5,4},{6,7},{7,6},{8,9},{9,8},{10,11... | collective-permute-start | bytes 2752520 | tf_op jit(solution)/shard_map/ppermute | solution.py:29

commit v5 on v4

--- a/solution.py
+++ b/solution.py
@@ -14,10 +14,11 @@
 NT = (((1,), (1,)), ((), ()))
 ROWS = 256
 CHUNKS = 4
-KEEP = 2
+KEEP = 3
 DEPTH = 4
+SUB = 512
 LANES = 512
-DELAY = 1
+DELAY = 2
 SCOPED = 6 * MIB
 
 
@@ -32,6 +33,10 @@
 def halves(x):
     head = x.astype(BF16)
     return head, (x - head.astype(F32)).astype(BF16)
+
+
+def rows_at(j):
+    return pl.ds(j * ROWS if isinstance(j, int) else pl.multiple_of(j * ROWS, ROWS), ROWS)
 
 
 def stream_kernel(tokens, chunk, loads, at_chunk, starts, *refs):
@@ -83,7 +88,7 @@
         ).wait()
 
     def add_sums(j):
-        at = pl.ds(pl.multiple_of(j * ROWS, ROWS), ROWS)
+        at = rows_at(j)
         for lo in range(0, chunk, LANES):
             here = slice(lo, min(lo + LANES, chunk))
             x = buf_ref[into, at, here].astype(F32)
@@ -92,7 +97,7 @@
             acc_ref[8:16, here] += jnp.sum((x * x).reshape(wide), axis=0)
 
     def project(j):
-        at = pl.ds(pl.multiple_of(j * ROWS, ROWS), ROWS)
+        at = rows_at(j)
         part_here = lax.dot_general(
             scaled_ref[...], buf_ref[held, at, :], NT, preferred_element_type=F32
         ) - offset
@@ -103,7 +108,8 @@
     if loads is not None:
         acc_ref[...] = jnp.zeros_like(acc_ref)
     if loads is None:
-        pl.loop(0, rows)(project)
+        for j in range(rows):
+            project(j)
     elif not projects:
 
         @pl.loop(0, rows)
@@ -167,21 +173,6 @@
     )(*args))
 
 
-def spread_kernel(blocks_ref, out_ref):
-    total = jnp.sum(blocks_ref[...].astype(F32), axis=0).astype(BF16)
-    for r in range(out_ref.shape[0]):
-        out_ref[r] = total
-
-
-def spread(blocks):
-    return pl.pallas_call(
-        spread_kernel,
-        out_shape=jax.ShapeDtypeStruct(blocks.shape, BF16),
-        compiler_params=pltpu.CompilerParams(vmem_limit_bytes=SCOPED),
-        name="spread",
-    )(blocks)
-
-
 def cross_kernel(start, sub, proj_ref, act_ref, stats_ref, out_ref, buf_ref, sem):
     depth = buf_ref.shape[0]
     blocks = out_ref.shape[1] // sub
@@ -207,7 +198,7 @@
 def cross(proj, act, stats, start):
     cols, rows = proj.shape[1], act.shape[0]
     width = stats.shape[1]
-    sub = block_of(width, 512)
+    sub = block_of(width, SUB)
     vmem = pl.BlockSpec(memory_space=pltpu.VMEM)
     return pl.pallas_call(
         functools.partial(cross_kernel, start, sub),
@@ -215,7 +206,7 @@
         out_specs=vmem,
         out_shape=jax.ShapeDtypeStruct((cols, width), F32),
         scratch_shapes=[pltpu.VMEM((DEPTH, rows, sub), BF16), pltpu.SemaphoreType.DMA((DEPTH,))],
-        compiler_params=pltpu.CompilerParams(vmem_limit_bytes=24 * MIB),
+        compiler_params=pltpu.CompilerParams(vmem_limit_bytes=40 * MIB),
         cost_estimate=pl.CostEstimate(
             flops=8 * rows * cols * width, bytes_accessed=2 * rows * width, transcendentals=0
         ),
@@ -288,6 +279,53 @@
     )(*args)
 
 
+def inverse_factor(gram):
+    cols = gram.shape[0]
+    row = lax.broadcasted_iota(jnp.int32, (cols, cols), 0)
+    lane = lax.broadcasted_iota(jnp.int32, (cols, cols), 1)
+    diag = jnp.where(row == lane, gram, 0.0)
+    down = lax.rsqrt(jnp.sum(diag, axis=1, keepdims=True))
+    along = lax.rsqrt(jnp.sum(diag, axis=0, keepdims=True))
+    gram = gram * down * along
+    wide = jnp.concatenate([gram, (row == lane).astype(F32)], axis=1)
+    tall = [wide[8 * b : 8 * b + 8] for b in range(cols // 8)]
+    tile = tall[0].shape
+    within = lax.broadcasted_iota(jnp.int32, tile, 0)
+
+    def column(x, k):
+        return jnp.broadcast_to(x[:, k : k + 1], tile)
+
+    def line(x, i):
+        return jnp.broadcast_to(x[i : i + 1], tile)
+
+    for k in range(0, cols, 2):
+        at, inner = divmod(k, 8)
+        first, second = line(tall[at], inner), line(tall[at], inner + 1)
+        left, right = column(tall[at], k), column(tall[at], k + 1)
+        a, b, c = line(left, inner), line(right, inner), line(right, inner + 1)
+        over = 1.0 / (a * c - b * b)
+        a, b, c = a * over, b * over, c * over
+        for t in range(at, cols // 8):
+            if t > at:
+                left, right = column(tall[t], k), column(tall[t], k + 1)
+            by_first, by_second = c * left - b * right, a * right - b * left
+            if t == at:
+                if inner == 6:
+                    continue
+                below = within > inner + 1
+                by_first, by_second = jnp.where(below, by_first, 0.0), jnp.where(below, by_second, 0.0)
+            tall[t] = tall[t] - (by_first * first + by_second * second)
+    wide = jnp.concatenate(tall, axis=0)
+    diag = jnp.sum(jnp.where(row == lane, wide[:, :cols], 0.0), axis=1, keepdims=True)
+    odd = row % 2 == 1
+    beside = jnp.sum(jnp.where((row == lane + 1) & odd, wide[:, :cols], 0.0), axis=1, keepdims=True)
+    above = pltpu.roll(wide, 1, 0)[:, cols:]
+    diag_above = pltpu.roll(jnp.broadcast_to(diag, wide.shape), 1, 0)[:, 0:1]
+    ratio = jnp.where(odd[:, 0:1], beside / diag_above, 0.0)
+    unit = wide[:, cols:] - ratio * above
+    return unit * lax.rsqrt(diag - ratio * beside) * along
+
+
 def finish_kernel(gram_ref, weighted_ref, out_ref, inv_ref):
     cols = weighted_ref.shape[0]
 
@@ -295,23 +333,7 @@
     def _():
         packed = jnp.sum(gram_ref[...], axis=0) / NEURONS
         gram = jnp.concatenate([packed[:, :cols], packed[:, cols:]], axis=0)
-        row = lax.broadcasted_iota(jnp.int32, (cols, cols), 0)
-        lane = lax.broadcasted_iota(jnp.int32, (cols, cols), 1)
-        wide = jnp.concatenate([gram, (row == lane).astype(F32)], axis=1)
-        tall = [wide[8 * b : 8 * b + 8] for b in range(cols // 8)]
-        within = lax.broadcasted_iota(jnp.int32, (8, 1), 0)
-        for k in range(cols):
-            at, inner = divmod(k, 8)
-            pivot_row = tall[at][inner : inner + 1]
-            pivot_row = pivot_row / pivot_row[:, k : k + 1]
-            for b in range(at, cols // 8):
-                factor = tall[b][:, k : k + 1]
-                if b == at:
-                    factor = jnp.where(within > inner, factor, 0.0)
-                tall[b] = tall[b] - factor * pivot_row
-        wide = jnp.concatenate(tall, axis=0)
-        diag = jnp.sum(jnp.where(row == lane, wide[:, :cols], 0.0), axis=1, keepdims=True)
-        head, rest = halves(wide[:, cols:] * lax.rsqrt(diag))
+        head, rest = halves(inverse_factor(gram))
         inv_ref[...] = jnp.concatenate([head, head, rest], axis=1)
 
     head, rest = halves(weighted_ref[...])
@@ -367,7 +389,9 @@
     blocks = part
     if tok_dev // n != ROWS:
         blocks = part.transpose(1, 0, 2).reshape(cols, n, tok_dev // n).transpose(1, 0, 2)
-    blocks = spread(lax.all_to_all(blocks, "neuron", 0, 0))
+    blocks = lax.all_to_all(blocks, "neuron", 0, 0)
+    block = sum(blocks[r].astype(F32) for r in range(n)).astype(BF16)
+    blocks = jnp.broadcast_to(block[None], blocks.shape)
     proj = lax.all_to_all(blocks, "neuron", 0, 0)
     if proj.shape[2] % 128:
         proj = proj.transpose(1, 0, 2).reshape(1, cols, tok_dev)

time: 114 us -> 111 us (0.974)
  waiting for transfers between devices: 21.2 us -> 18.4 us
    ppermute x6, waiting for transfers between devices: 3.42 us -> 0.02 us  [swap_tokens(): return lax.ppermute(x, 'token', [(0, 1), (1, 0)])]
    pallas_call x5 -> x6, Pallas kernels: 35.1 us -> 36.5 us  [stream(): pl.pallas_call(functools.partial(stream_kernel, tokens, chunk, loads, at,...]
  transfers between devices with their start and end apart: 8 -> 8, of which waited for: 6 -> 2; matrix products, arithmetic and copies ran while one was open for 0% -> 0% of each run, Pallas kernels for 7% -> 31%
where the time goes in v5:
time: 111 us
  Pallas kernels  68.1 us (61%)
  waiting for transfers between devices  18.4 us (17%)
  starting transfers between devices  12.5 us (11%)
  blocking collectives  10.7 us (10%)
    pallas_call x6, Pallas kernels, stream(): pl.pallas_call(functools.partial(stream_kernel, tokens, chunk, loads, at,...  36.5 us
    pallas_call x2, Pallas kernels, cross(): pl.pallas_call(functools.partial(cross_kernel, start, sub), in_specs=[vme...  20.8 us
    all_to_all x1, blocking collectives, local(): grams = lax.all_to_all(gram, 'neuron', 0, 0)  10.7 us
    all_to_all x1, waiting for transfers between devices, local(): blocks = lax.all_to_all(blocks, 'neuron', 0, 0)  9.44 us
    all_to_all x1, waiting for transfers between devices, local(): proj = lax.all_to_all(blocks, 'neuron', 0, 0)  8.97 us
    pallas_call x1, Pallas kernels, finish(): pl.pallas_call(finish_kernel, grid=(width // nb,), in_specs=[pl.BlockSpec...  7.83 us
    all_to_all x1, starting transfers between devices, local(): blocks = lax.all_to_all(blocks, 'neuron', 0, 0)  6.95 us
    all_to_all x1, starting transfers between devices, local(): proj = lax.all_to_all(blocks, 'neuron', 0, 0)  3.59 us
  transfers between devices with their start and end apart: 8, of which 2 were waited for; matrix products, arithmetic and copies ran while one was open for 0% of the time, Pallas kernels for 31%

profile of v5, /device:TPU:0, one launch (start us, length us, event | category | flops | bytes accessed | tf_op | source)
XLA Modules:
  0.0 110.9 jit_solution(5410955402865192416)
XLA Ops:
  0.0 5.7 %stream.6 = (bf16[3,2048,3584]{2,1,0:T(8,128)(2,1)S(1)}, f32[2,3584]{1,0:T(2,128)S(1)}) custom-call(bf16[2048,14336]{1,0:T(8,128)(2,1)} %act_ref.3), custom_call_target="tpu_custom_call" | custom-call | flops 3758096384 | bytes 14680064 | tf_op jit(solution)/shard_map/stream/pallas_call | solution.py:161
  5.7 0.5 collective-permute-start
  6.2 5.8 %stream.7 = (bf16[3,2048,3584]{2,1,0:T(8,128)(2,1)S(1)}, f32[2,3584]{1,0:T(2,128)S(1)}) custom-call(bf16[2048,14336]{1,0:T(8,128)(2,1)} %act_ref.3, bf16[3,2048,3584]{2,1,0:T(8,128)(2,1)S(1)} %get-tuple-element.25.refs_1_), custom_call_target="tpu_custom_call", output_to_operand_aliasing={{0}: (1, {})} | custom-call | flops 3758096384 | bytes 14680064 | tf_op jit(solution)/shard_map/stream/pallas_call | solution.py:161
  12.0 0.1 collective-permute-start.1
  12.2 0.3 copy-done
  12.5 7.6 %stream.8 = (bf16[3,2048,3584]{2,1,0:T(8,128)(2,1)S(1)}, f32[2,3584]{1,0:T(2,128)S(1)}, f32[8,64,256]{2,1,0:T(8,128)S(1)}, f32[2,3584]{1,0:T(2,128)S(1)}) custom-call(bf16[2048,14336]{1,0:T(8,128)(2,1)} %act_ref.3, bf16[3,2048,3584]{2,1,0:T(8,128)(2,1)S(1)} %get-tuple-element.26.refs_1_, ...), custom_call_target="tpu_custom_call", output_to_operand_aliasing={{0}: (1, {})} | custom-call | flops 3758096384 | bytes 14680064 | tf_op jit(solution)/shard_map/stream/pallas_call | solution.py:161
  20.1 0.2 collective-permute-start.3
  20.3 7.7 %stream.9 = (bf16[3,2048,3584]{2,1,0:T(8,128)(2,1)S(1)}, f32[2,3584]{1,0:T(2,128)S(1)}, f32[8,64,256]{2,1,0:T(8,128)S(1)}, f32[2,3584]{1,0:T(2,128)S(1)}) custom-call(bf16[2048,14336]{1,0:T(8,128)(2,1)} %act_ref.3, bf16[3,2048,3584]{2,1,0:T(8,128)(2,1)S(1)} %get-tuple-element.28.refs_1_, ...), custom_call_target="tpu_custom_call", output_to_operand_aliasing={{0}: (1, {})} | custom-call | flops 3758096384 | bytes 14680064 | tf_op jit(solution)/shard_map/stream/pallas_call | solution.py:161
  28.0 0.4 collective-permute-start.2
  28.5 4.5 %stream.10 = (f32[8,64,256]{2,1,0:T(8,128)S(1)}, f32[2,3584]{1,0:T(2,128)S(1)}) custom-call(bf16[3,2048,3584]{2,1,0:T(8,128)(2,1)S(1)} %get-tuple-element.31.refs_0_, f32[2,3584]{1,0:T(2,128)S(1)} %get-tuple-element.33.refs_1_, f32[2,3584]{1,0:T(2,128)S(1)} %collective-permute-done.3.refs_2_, f32[64,14336]{1,0:T(8,128)S(1)} %bitcast.6, ...), custom_call_target="tpu_custom_call" | custom-call | flops 3758096384 | bytes 14680064 | tf_op jit(solution)/shard_map/stream/pallas_call | solution.py:161
  33.0 5.2 %stream.11 = (bf16[8,64,256]{2,1,0:T(8,128)(2,1)}, f32[2,3584]{1,0:T(2,128)S(1)}) custom-call(bf16[3,2048,3584]{2,1,0:T(8,128)(2,1)S(1)} %get-tuple-element.31.refs_0_, f32[2,3584]{1,0:T(2,128)S(1)} %get-tuple-element.32.refs_1_, f32[2,3584]{1,0:T(2,128)S(1)} %collective-permute-done.2.refs_2_, f32[64,14336]{1,0:T(8,128)S(1)} %bitcast.7, ...), custom_call_target="tpu_custom_call" | custom-call | flops 3758096384 | bytes 14680064 | tf_op jit(solution)/shard_map/stream/pallas_call | solution.py:161
  38.2 6.9 %all-to-all-start = ((bf16[8,64,256]{2,1,0:T(8,128)(2,1)}), bf16[8,64,256]{2,1,0:T(8,128)(2,1)S(1)}, u32[]{:S(2)}, u32[]{:S(2)}) async-start(bf16[8,64,256]{2,1,0:T(8,128)(2,1)} %get-tuple-element.36), calls=%async_computation | async-start | bytes 524288 | tf_op jit(solution)/shard_map/all_to_all | solution.py:392
  45.1 9.4 %all-to-all-done = bf16[8,64,256]{2,1,0:T(8,128)(2,1)S(1)} async-done(((bf16[8,64,256]{2,1,0:T(8,128)(2,1)}), bf16[8,64,256]{2,1,0:T(8,128)(2,1)S(1)}, u32[]{:S(2)}, u32[]{:S(2)}) %all-to-all-start) | async-done | bytes 262176 | tf_op jit(solution)/shard_map/all_to_all | solution.py:392
  54.6 0.7 broadcast_in_dim.9
  55.3 3.6 %all-to-all-start.1 = ((bf16[8,64,256]{2,1,0:T(8,128)(2,1)}), bf16[8,64,256]{2,1,0:T(8,128)(2,1)S(1)}, u32[]{:S(2)}, u32[]{:S(2)}) async-start(bf16[8,64,256]{2,1,0:T(8,128)(2,1)} %broadcast_in_dim.9), calls=%async_computation.1 | async-start | bytes 524288 | tf_op jit(solution)/shard_map/all_to_all | solution.py:395
  59.0 9.0 %all-to-all-done.1.proj_ref = bf16[8,64,256]{2,1,0:T(8,128)(2,1)S(1)} async-done(((bf16[8,64,256]{2,1,0:T(8,128)(2,1)}), bf16[8,64,256]{2,1,0:T(8,128)(2,1)S(1)}, u32[]{:S(2)}, u32[]{:S(2)}) %all-to-all-start.1) | async-done | bytes 262176 | tf_op jit(solution)/shard_map/all_to_all | solution.py:395
  67.9 14.7 %cross.3.own_ref = f32[64,10752]{1,0:T(8,128)S(1)} custom-call(bf16[8,64,256]{2,1,0:T(8,128)(2,1)S(1)} %all-to-all-done.1.proj_ref, bf16[2048,14336]{1,0:T(8,128)(2,1)} %act_ref.3, f32[2,10752]{1,0:T(2,128)S(1)} %constant_dynamic-update-slice_fusion.stats_ref.stat_ref), custom_call_target="tpu_custom_call" | custom-call | flops 11274289152 | bytes 44040192 | tf_op jit(solution)/shard_map/cross/pallas_call | solution.py:203
  82.7 0.1 collective-permute-start.5
  82.7 6.1 %cross.2.own_ref = f32[64,3584]{1,0:T(8,128)S(1)} custom-call(bf16[8,64,256]{2,1,0:T(8,128)(2,1)S(1)} %all-to-all-done.1.proj_ref, bf16[2048,14336]{1,0:T(8,128)(2,1)} %act_ref.3, f32[2,3584]{1,0:T(2,128)S(1)} %get-tuple-element.37.stats_ref.stat_ref), custom_call_target="tpu_custom_call" | custom-call | flops 3758096384 | bytes 14680064 | tf_op jit(solution)/shard_map/cross/pallas_call | solution.py:203
  88.8 0.6 collective-permute-start.4
  89.4 2.2 %combine.2 = (f32[64,14336]{1,0:T(8,128)S(1)}, f32[32,128]{1,0:T(8,128)S(1)}) custom-call(f32[64,10752]{1,0:T(8,128)S(1)} %cross.3.own_ref, f32[64,10752]{1,0:T(8,128)S(1)} %collective-permute-done.5.got_ref, f32[2,10752]{1,0:T(2,128)S(1)} %constant_dynamic-update-slice_fusion.stats_ref.stat_ref), custom_call_target="tpu_custom_call" | custom-call | flops 352321536 | bytes 8257536 | tf_op jit(solution)/shard_map/combine/pallas_call | solution.py:263
  91.6 0.7 combine.3
  92.3 10.7 %all_to_all.15.gram_ref = f32[8,32,128]{2,1,0:T(8,128)S(1)} all-to-all(f32[8,32,128]{2,1,0:T(8,128)S(1)} %get-tuple-element.43), channel_id=1, replica_groups=mesh['groups'=2,'neuron'=8,'token'=2] {'neuron'}, dimensions={0} | all-to-all | bytes 262144 | tf_op jit(solution)/shard_map/all_to_all | solution.py:409
  103.1 7.8 %finish.1 = f32[64,14336]{1,0:T(8,128)} custom-call(f32[8,32,128]{2,1,0:T(8,128)S(1)} %all_to_all.15.gram_ref, f32[64,14336]{1,0:T(8,128)S(1)} %get-tuple-element.44.weighted_ref), custom_call_target="tpu_custom_call" | custom-call | tf_op jit(solution)/shard_map/finish/pallas_call | solution.py:348
  (11 shorter events, 0.1 us)
Async XLA Ops:
  5.7 6.5 %collective-permute-start = (f32[2,3584]{1,0:T(2,128)S(1)}, f32[2,3584]{1,0:T(2,128)S(1)}, u32[]{:S(2)}, u32[]{:S(2)}) collective-permute-start(f32[2,3584]{1,0:T(2,128)S(1)} %get-tuple-element.27.refs_2_), channel_id=1, source_target_pairs={{0,1},{1,0},{2,3},{3,2},{4,5},{5,4},{6,7},{7,6},{8,9},{9,8},{10,11... | collective-permute-start | bytes 86024 | tf_op jit(solution)/shard_map/ppermute | solution.py:30
  6.2 6.3 %copy-start = (f32[14336,64]{0,1:T(8,128)S(1)}, f32[14336,64]{0,1:T(8,128)}, u32[]{:S(2)}) copy-start(f32[14336,64]{0,1:T(8,128)} %param.3) | copy-start | bytes 11010052
  12.0 8.3 %collective-permute-start.1 = (f32[2,3584]{1,0:T(2,128)S(1)}, f32[2,3584]{1,0:T(2,128)S(1)}, u32[]{:S(2)}, u32[]{:S(2)}) collective-permute-start(f32[2,3584]{1,0:T(2,128)S(1)} %get-tuple-element.29.refs_2_), channel_id=1, source_target_pairs={{0,1},{1,0},{2,3},{3,2},{4,5},{5,4},{6,7},{7,6},{8,9},{9,8},{10,11... | collective-permute-start | bytes 86024 | tf_op jit(solution)/shard_map/ppermute | solution.py:30
  20.1 8.3 %collective-permute-start.3 = (f32[2,3584]{1,0:T(2,128)S(1)}, f32[2,3584]{1,0:T(2,128)S(1)}, u32[]{:S(2)}, u32[]{:S(2)}) collective-permute-start(f32[2,3584]{1,0:T(2,128)S(1)} %get-tuple-element.33.refs_1_), channel_id=1, source_target_pairs={{0,1},{1,0},{2,3},{3,2},{4,5},{5,4},{6,7},{7,6},{8,9},{9,8},{10,11... | collective-permute-start | bytes 86024 | tf_op jit(solution)/shard_map/ppermute | solution.py:30
  28.0 5.0 %collective-permute-start.2 = (f32[2,3584]{1,0:T(2,128)S(1)}, f32[2,3584]{1,0:T(2,128)S(1)}, u32[]{:S(2)}, u32[]{:S(2)}) collective-permute-start(f32[2,3584]{1,0:T(2,128)S(1)} %get-tuple-element.32.refs_1_), channel_id=1, source_target_pairs={{0,1},{1,0},{2,3},{3,2},{4,5},{5,4},{6,7},{7,6},{8,9},{9,8},{10,11... | collective-permute-start | bytes 86024 | tf_op jit(solution)/shard_map/ppermute | solution.py:30
  38.2 16.4 %all-to-all-start = ((bf16[8,64,256]{2,1,0:T(8,128)(2,1)}), bf16[8,64,256]{2,1,0:T(8,128)(2,1)S(1)}, u32[]{:S(2)}, u32[]{:S(2)}) async-start(bf16[8,64,256]{2,1,0:T(8,128)(2,1)} %get-tuple-element.36), calls=%async_computation | async-start | bytes 524288 | tf_op jit(solution)/shard_map/all_to_all | solution.py:392
  55.3 12.6 %all-to-all-start.1 = ((bf16[8,64,256]{2,1,0:T(8,128)(2,1)}), bf16[8,64,256]{2,1,0:T(8,128)(2,1)S(1)}, u32[]{:S(2)}, u32[]{:S(2)}) async-start(bf16[8,64,256]{2,1,0:T(8,128)(2,1)} %broadcast_in_dim.9), calls=%async_computation.1 | async-start | bytes 524288 | tf_op jit(solution)/shard_map/all_to_all | solution.py:395
  82.7 6.7 %collective-permute-start.5 = (f32[64,10752]{1,0:T(8,128)S(1)}, f32[64,10752]{1,0:T(8,128)S(1)}, u32[]{:S(2)}, u32[]{:S(2)}) collective-permute-start(f32[64,10752]{1,0:T(8,128)S(1)} %cross.3.own_ref), channel_id=1, source_target_pairs={{0,1},{1,0},{2,3},{3,2},{4,5},{5,4},{6,7},{7,6},{8,9},{9,8},{10,11... | collective-permute-start | bytes 8257544 | tf_op jit(solution)/shard_map/ppermute | solution.py:30
  88.8 2.8 %collective-permute-start.4 = (f32[64,3584]{1,0:T(8,128)S(1)}, f32[64,3584]{1,0:T(8,128)S(1)}, u32[]{:S(2)}, u32[]{:S(2)}) collective-permute-start(f32[64,3584]{1,0:T(8,128)S(1)} %cross.2.own_ref), channel_id=1, source_target_pairs={{0,1},{1,0},{2,3},{3,2},{4,5},{5,4},{6,7},{7,6},{8,9},{9,8},{10,11... | collective-permute-start | bytes 2752520 | tf_op jit(solution)/shard_map/ppermute | solution.py:30

commit v6 on v5

--- a/solution.py
+++ b/solution.py
@@ -17,6 +17,7 @@
 KEEP = 3
 DEPTH = 4
 SUB = 512
+FINAL = 2048
 LANES = 512
 DELAY = 2
 SCOPED = 6 * MIB
@@ -173,8 +174,10 @@
     )(*args))
 
 
-def cross_kernel(start, sub, proj_ref, act_ref, stats_ref, out_ref, buf_ref, sem):
+def cross_kernel(start, sub, proj_ref, act_ref, *refs):
+    *stat_refs, out_ref, buf_ref, sem = refs
     depth = buf_ref.shape[0]
+    chunk = stat_refs[0].shape[1]
     blocks = out_ref.shape[1] // sub
     copies = [
         pltpu.make_async_copy(
@@ -187,22 +190,24 @@
     proj = jnp.concatenate([proj_ref[r] for r in range(proj_ref.shape[0])], axis=1)
     total = jnp.sum(proj.astype(F32), axis=1, keepdims=True)
     for s, copy in enumerate(copies):
-        here = slice(s * sub, s * sub + sub)
+        piece, at = divmod(s * sub, chunk)
+        mean = stat_refs[piece][0:1, at : at + sub]
         copy.wait()
         prod = jnp.dot(proj, buf_ref[s % depth], preferred_element_type=F32)
         if s + depth < blocks:
             copies[s + depth].start()
-        out_ref[:, here] = prod - total * stats_ref[0:1, here]
+        out_ref[:, s * sub : s * sub + sub] = prod - total * mean
 
 
 def cross(proj, act, stats, start):
     cols, rows = proj.shape[1], act.shape[0]
-    width = stats.shape[1]
-    sub = block_of(width, SUB)
+    chunk = stats[0].shape[1]
+    width = chunk * len(stats)
+    sub = block_of(chunk, SUB)
     vmem = pl.BlockSpec(memory_space=pltpu.VMEM)
     return pl.pallas_call(
         functools.partial(cross_kernel, start, sub),
-        in_specs=[vmem, pl.BlockSpec(memory_space=pl.ANY), vmem],
+        in_specs=[vmem, pl.BlockSpec(memory_space=pl.ANY)] + [vmem] * len(stats),
         out_specs=vmem,
         out_shape=jax.ShapeDtypeStruct((cols, width), F32),
         scratch_shapes=[pltpu.VMEM((DEPTH, rows, sub), BF16), pltpu.SemaphoreType.DMA((DEPTH,))],
@@ -211,69 +216,55 @@
             flops=8 * rows * cols * width, bytes_accessed=2 * rows * width, transcendentals=0
         ),
         name="cross",
-    )(proj, act, stats)
-
-
-def combine_kernel(pieces, first, last, tokens, own_ref, got_ref, stat_ref, *refs):
-    i = pl.program_id(0)
-    if not first:
-        prev_ref, _, *refs = refs
-    out_ref, gram_ref, acc_ref = refs
+    )(proj, act, *stats)
+
+
+def combine_kernel(start, pieces, last, tokens, own_ref, got_ref, *refs):
+    stat_refs, refs = refs[:pieces], refs[pieces:]
+    if start:
+        _, prev_ref, *refs = refs
+    out_ref, gram_ref = refs
     cols = own_ref.shape[0]
-    weighted = (own_ref[...] + got_ref[...]) * stat_ref[1:2] / tokens
-    out_ref[...] = weighted
-    both = jnp.concatenate(halves(weighted), axis=0)
-    square = lax.dot_general(both, both, NT, preferred_element_type=F32)
-
-    @pl.when(i == 0)
-    def _():
-        acc_ref[...] = square
-
-    @pl.when(i > 0)
-    def _():
-        acc_ref[...] += square
-
-    @pl.when(i == pieces - 1)
-    def _():
-        full = acc_ref[...]
-        gram = (full[:cols, :cols] + full[cols:, cols:]) + (full[:cols, cols:] + full[cols:, :cols])
-        packed = jnp.concatenate([gram[: cols // 2], gram[cols // 2 :]], axis=1)
-        if not first:
-            packed = packed + prev_ref[...]
-        if last:
-            for r in range(gram_ref.shape[0]):
-                gram_ref[r] = packed
-        else:
-            gram_ref[...] = packed
-
-
-def combine(own, got, stats, start, chunk, whole, tokens, n, prev, buffer, last):
-    cols = own.shape[0]
-    pieces = own.shape[1] // chunk
-    first = prev is None
-    here = pl.BlockSpec((cols, chunk), lambda i: (0, i))
-    there = pl.BlockSpec((cols, chunk), lambda i: (0, i + start // chunk))
+    chunk = stat_refs[0].shape[1]
+    nb = block_of(chunk, 1792)
+    full = None
+    for at in range(0, own_ref.shape[1], nb):
+        piece, within = divmod(at, chunk)
+        scale = stat_refs[piece][1:2, within : within + nb] * (1.0 / tokens)
+        weighted = (own_ref[:, at : at + nb] + got_ref[:, at : at + nb]) * scale
+        both = jnp.concatenate(halves(weighted), axis=0)
+        out_ref[:, start + at : start + at + nb] = both
+        square = lax.dot_general(both, both, NT, preferred_element_type=F32)
+        full = square if full is None else full + square
+    gram = (full[:cols, :cols] + full[cols:, cols:]) + (full[:cols, cols:] + full[cols:, :cols])
+    packed = jnp.concatenate([gram[: cols // 2], gram[cols // 2 :]], axis=1)
+    if start:
+        packed = packed + prev_ref[...]
+    if last:
+        for r in range(gram_ref.shape[0]):
+            gram_ref[r] = packed
+    else:
+        gram_ref[...] = packed
+
+
+def combine(own, got, stats, start, whole, tokens, n, buffer, prev):
+    cols, width = own.shape
+    last = start + width == whole
     packed = (n, cols // 2, 2 * cols) if last else (cols // 2, 2 * cols)
-    in_specs = [here, here, pl.BlockSpec((2, chunk), lambda i: (0, i))]
-    args, aliases = [own, got, stats], {}
-    if not first:
-        in_specs += [pl.BlockSpec((cols // 2, 2 * cols), lambda i: (0, 0)), pl.BlockSpec(memory_space=pl.ANY)]
-        args += [prev, buffer]
-        aliases = {4: 0}
+    args = [own, got, *stats] + ([buffer, prev] if start else [])
+    vmem = pl.BlockSpec(memory_space=pltpu.VMEM)
     return pl.pallas_call(
-        functools.partial(combine_kernel, pieces, first, last, tokens),
-        grid=(pieces,),
-        in_specs=in_specs,
-        out_specs=[there, pl.BlockSpec(packed, lambda i: (0,) * len(packed))],
+        functools.partial(combine_kernel, start, len(stats), last, tokens),
+        in_specs=[vmem] * len(args),
+        out_specs=[vmem, vmem],
         out_shape=[
-            jax.ShapeDtypeStruct((cols, whole), F32),
+            jax.ShapeDtypeStruct((2 * cols, whole), BF16),
             jax.ShapeDtypeStruct(packed, F32),
         ],
-        scratch_shapes=[pltpu.VMEM((2 * cols, 2 * cols), F32)],
-        input_output_aliases=aliases,
-        compiler_params=pltpu.CompilerParams(vmem_limit_bytes=12 * MIB),
+        input_output_aliases={len(args) - 2: 0} if start else {},
+        compiler_params=pltpu.CompilerParams(vmem_limit_bytes=16 * MIB),
         cost_estimate=pl.CostEstimate(
-            flops=8 * cols * cols * own.shape[1], bytes_accessed=12 * cols * own.shape[1], transcendentals=0
+            flops=8 * cols * cols * width, bytes_accessed=12 * cols * width, transcendentals=0
         ),
         name="combine",
     )(*args)
@@ -326,38 +317,41 @@
     return unit * lax.rsqrt(diag - ratio * beside) * along
 
 
-def finish_kernel(gram_ref, weighted_ref, out_ref, inv_ref):
-    cols = weighted_ref.shape[0]
-
-    @pl.when(pl.program_id(0) == 0)
-    def _():
-        packed = jnp.sum(gram_ref[...], axis=0) / NEURONS
-        gram = jnp.concatenate([packed[:, :cols], packed[:, cols:]], axis=0)
-        head, rest = halves(inverse_factor(gram))
-        inv_ref[...] = jnp.concatenate([head, head, rest], axis=1)
-
-    head, rest = halves(weighted_ref[...])
-    out_ref[...] = jnp.dot(
-        inv_ref[...], jnp.concatenate([head, rest, head], axis=0), preferred_element_type=F32
-    )
-
-
-def finish(grams, weighted):
-    cols, width = weighted.shape
-    nb = block_of(width, 3584)
+def finish_kernel(nb, gram_ref, both_ref, out_ref, stage_ref, sem):
+    cols = out_ref.shape[0]
+    packed = jnp.sum(gram_ref[...], axis=0) / NEURONS
+    gram = jnp.concatenate([packed[:, :cols], packed[:, cols:]], axis=0)
+    head, rest = halves(inverse_factor(gram))
+    twice = jnp.concatenate([head, head], axis=1)
+    copies = []
+    for s, at in enumerate(range(0, out_ref.shape[1], nb)):
+        both = both_ref[:, at : at + nb]
+        stage_ref[:, at : at + nb] = jnp.dot(twice, both, preferred_element_type=F32) + jnp.dot(
+            rest, both[:cols], preferred_element_type=F32
+        )
+        copies.append(
+            pltpu.make_async_copy(
+                stage_ref.at[:, pl.ds(at, nb)], out_ref.at[:, pl.ds(at, nb)], sem.at[s]
+            )
+        )
+        copies[-1].start()
+    for copy in copies:
+        copy.wait()
+
+
+def finish(grams, both):
+    cols, width = both.shape[0] // 2, both.shape[1]
+    nb = block_of(width, FINAL)
+    vmem = pl.BlockSpec(memory_space=pltpu.VMEM)
     return pl.pallas_call(
-        finish_kernel,
-        grid=(width // nb,),
-        in_specs=[
-            pl.BlockSpec(grams.shape, lambda i: (0, 0, 0)),
-            pl.BlockSpec((cols, nb), lambda i: (0, i)),
-        ],
-        out_specs=pl.BlockSpec((cols, nb), lambda i: (0, i)),
+        functools.partial(finish_kernel, nb),
+        in_specs=[vmem, vmem],
+        out_specs=pl.BlockSpec(memory_space=pl.ANY),
         out_shape=jax.ShapeDtypeStruct((cols, width), F32),
-        scratch_shapes=[pltpu.VMEM((cols, 3 * cols), BF16)],
+        scratch_shapes=[pltpu.VMEM((cols, width), F32), pltpu.SemaphoreType.DMA((width // nb,))],
         compiler_params=pltpu.CompilerParams(vmem_limit_bytes=16 * MIB),
         name="finish",
-    )(grams, weighted)
+    )(grams, both)
 
 
 def local(activations, basis):
@@ -398,16 +392,14 @@
 
     split = chunks - max(1, chunks // 4)
     spans = [(0, split), (split, chunks)] if split else [(0, chunks)]
-    stats = [jnp.concatenate(stats[lo:hi], axis=1) for lo, hi in spans]
-    terms = [cross(proj, activations, stat, lo * chunk) for stat, (lo, _) in zip(stats, spans)]
+    spans = [(lo * chunk, stats[lo:hi]) for lo, hi in spans]
+    terms = [cross(proj, activations, stat, start) for start, stat in spans]
     swapped = [swap_tokens(term) for term in terms]
-    weighted = gram = None
-    for term, got, stat, (lo, hi) in zip(terms, swapped, stats, spans):
-        weighted, gram = combine(
-            term, got, stat, lo * chunk, chunk, neu_dev, tokens, n, gram, weighted, hi == chunks
-        )
+    both = gram = None
+    for term, got, (start, stat) in zip(terms, swapped, spans):
+        both, gram = combine(term, got, stat, start, neu_dev, tokens, n, both, gram)
     grams = lax.all_to_all(gram, "neuron", 0, 0)
-    return finish(grams, weighted).T
+    return finish(grams, both).T
 
 
 def solution(mesh):

time: 111 us -> 108 us (0.973)
  blocking collectives: 10.7 us -> 39.5 us
  waiting for transfers between devices: 18.4 us -> 0.82 us
  starting transfers between devices: 12.5 us -> 1.91 us
  Pallas kernels: 68.1 us -> 65.3 us
    all_to_all x0 -> x2, blocking collectives: none -> 28.6 us  [the longest x1 16.2 us: local(): blocks = lax.all_to_all(blocks, 'neuron', 0, 0)]
    all_to_all x2 -> x0, waiting for transfers between devices: 18.4 us -> none  [the longest x1 9.44 us: local(): blocks = lax.all_to_all(blocks, 'neuron', 0, 0)]
    all_to_all x2 -> x0, starting transfers between devices: 10.5 us -> none  [the longest x1 6.95 us: local(): blocks = lax.all_to_all(blocks, 'neuron', 0, 0)]
    pallas_call x3, Pallas kernels: 10.8 us -> 8.75 us  [the longest x1 6.8 us: finish(): pl.pallas_call(functools.partial(finish_kernel, nb), in_specs=[vmem, vmem...]
  transfers between devices with their start and end apart: 8 -> 6, of which waited for: 2 -> 1; matrix products, arithmetic and copies ran while one was open for 0% -> 0% of each run, Pallas kernels for 31% -> 30%
where the time goes in v6:
time: 108 us
  Pallas kernels  65.3 us (60%)
  blocking collectives  39.5 us (37%)
  starting transfers between devices  1.91 us (2%)
    pallas_call x6, Pallas kernels, stream(): pl.pallas_call(functools.partial(stream_kernel, tokens, chunk, loads, at,...  35.8 us
    pallas_call x2, Pallas kernels, cross(): pl.pallas_call(functools.partial(cross_kernel, start, sub), in_specs=[vme...  20.8 us
    all_to_all x1, blocking collectives, local(): blocks = lax.all_to_all(blocks, 'neuron', 0, 0)  16.2 us
    all_to_all x1, blocking collectives, local(): proj = lax.all_to_all(blocks, 'neuron', 0, 0)  12.4 us
    all_to_all x1, blocking collectives, local(): grams = lax.all_to_all(gram, 'neuron', 0, 0)  10.9 us
    pallas_call x1, Pallas kernels, finish(): pl.pallas_call(functools.partial(finish_kernel, nb), in_specs=[vmem, vmem...  6.8 us
  transfers between devices with their start and end apart: 6, of which 1 were waited for; matrix products, arithmetic and copies ran while one was open for 0% of the time, Pallas kernels for 30%

profile of v6, /device:TPU:0, one launch (start us, length us, event | category | flops | bytes accessed | tf_op | source)
XLA Modules:
  0.0 108.2 jit_solution(17554016126047675620)
XLA Ops:
  0.0 5.7 %stream.6 = (bf16[3,2048,3584]{2,1,0:T(8,128)(2,1)S(1)}, f32[2,3584]{1,0:T(2,128)S(1)}) custom-call(bf16[2048,14336]{1,0:T(8,128)(2,1)} %act_ref.3), custom_call_target="tpu_custom_call" | custom-call | flops 3758096384 | bytes 14680064 | tf_op jit(solution)/shard_map/stream/pallas_call | solution.py:162
  5.7 0.5 collective-permute-start
  6.2 5.8 %stream.7 = (bf16[3,2048,3584]{2,1,0:T(8,128)(2,1)S(1)}, f32[2,3584]{1,0:T(2,128)S(1)}) custom-call(bf16[2048,14336]{1,0:T(8,128)(2,1)} %act_ref.3, bf16[3,2048,3584]{2,1,0:T(8,128)(2,1)S(1)} %get-tuple-element.25.refs_1_), custom_call_target="tpu_custom_call", output_to_operand_aliasing={{0}: (1, {})} | custom-call | flops 3758096384 | bytes 14680064 | tf_op jit(solution)/shard_map/stream/pallas_call | solution.py:162
  12.0 0.1 collective-permute-start.1
  12.2 0.0 collective-permute-done.refs_3_
  12.2 0.3 copy-done
  12.5 7.6 %stream.8 = (bf16[3,2048,3584]{2,1,0:T(8,128)(2,1)S(1)}, f32[2,3584]{1,0:T(2,128)S(1)}, f32[8,64,256]{2,1,0:T(8,128)S(1)}, f32[2,3584]{1,0:T(2,128)S(1)}) custom-call(bf16[2048,14336]{1,0:T(8,128)(2,1)} %act_ref.3, bf16[3,2048,3584]{2,1,0:T(8,128)(2,1)S(1)} %get-tuple-element.26.refs_1_, ...), custom_call_target="tpu_custom_call", output_to_operand_aliasing={{0}: (1, {})} | custom-call | flops 3758096384 | bytes 14680064 | tf_op jit(solution)/shard_map/stream/pallas_call | solution.py:162
  20.1 0.2 collective-permute-start.3
  20.3 0.0 collective-permute-done.1.refs_3_
  20.3 7.7 %stream.9 = (bf16[3,2048,3584]{2,1,0:T(8,128)(2,1)S(1)}, f32[2,3584]{1,0:T(2,128)S(1)}, f32[8,64,256]{2,1,0:T(8,128)S(1)}, f32[2,3584]{1,0:T(2,128)S(1)}) custom-call(bf16[2048,14336]{1,0:T(8,128)(2,1)} %act_ref.3, bf16[3,2048,3584]{2,1,0:T(8,128)(2,1)S(1)} %get-tuple-element.28.refs_1_, ...), custom_call_target="tpu_custom_call", output_to_operand_aliasing={{0}: (1, {})} | custom-call | flops 3758096384 | bytes 14680064 | tf_op jit(solution)/shard_map/stream/pallas_call | solution.py:162
  28.0 0.4 collective-permute-start.2
  28.5 4.5 %stream.10 = (f32[8,64,256]{2,1,0:T(8,128)S(1)}, f32[2,3584]{1,0:T(2,128)S(1)}) custom-call(bf16[3,2048,3584]{2,1,0:T(8,128)(2,1)S(1)} %get-tuple-element.31.refs_0_, f32[2,3584]{1,0:T(2,128)S(1)} %get-tuple-element.33.refs_1_, f32[2,3584]{1,0:T(2,128)S(1)} %collective-permute-done.3.refs_2_, f32[64,14336]{1,0:T(8,128)S(1)} %bitcast.6, ...), custom_call_target="tpu_custom_call" | custom-call | flops 3758096384 | bytes 14680064 | tf_op jit(solution)/shard_map/stream/pallas_call | solution.py:162
  33.0 4.5 %stream.11 = (bf16[8,64,256]{2,1,0:T(8,128)(2,1)S(1)}, f32[2,3584]{1,0:T(2,128)S(1)}) custom-call(bf16[3,2048,3584]{2,1,0:T(8,128)(2,1)S(1)} %get-tuple-element.31.refs_0_, f32[2,3584]{1,0:T(2,128)S(1)} %get-tuple-element.32.refs_1_, f32[2,3584]{1,0:T(2,128)S(1)} %collective-permute-done.2.refs_2_, f32[64,14336]{1,0:T(8,128)S(1)} %bitcast.7, ...), custom_call_target="tpu_custom_call" | custom-call | flops 3758096384 | bytes 14680064 | tf_op jit(solution)/shard_map/stream/pallas_call | solution.py:162
  37.5 16.2 %all_to_all.15 = bf16[8,64,256]{2,1,0:T(8,128)(2,1)S(1)} all-to-all(bf16[8,64,256]{2,1,0:T(8,128)(2,1)S(1)} %get-tuple-element.36), channel_id=1, replica_groups=mesh['groups'=2,'neuron'=8,'token'=2] {'neuron'}, dimensions={0} | all-to-all | bytes 524288 | tf_op jit(solution)/shard_map/all_to_all | solution.py:386
  53.8 12.4 %all_to_all.16.proj_ref = bf16[8,64,256]{2,1,0:T(8,128)(2,1)S(1)} all-to-all(bf16[8,64,256]{2,1,0:T(8,128)(2,1)S(1)} %broadcast_in_dim.9), channel_id=1, replica_groups=mesh['groups'=2,'neuron'=8,'token'=2] {'neuron'}, dimensions={0} | all-to-all | bytes 524288 | tf_op jit(solution)/shard_map/all_to_all | solution.py:389
  66.2 14.7 %cross.3.own_ref = f32[64,10752]{1,0:T(8,128)S(1)} custom-call(bf16[8,64,256]{2,1,0:T(8,128)(2,1)S(1)} %all_to_all.16.proj_ref, bf16[2048,14336]{1,0:T(8,128)(2,1)} %act_ref.3, f32[2,3584]{1,0:T(2,128)S(1)} %get-tuple-element.38.refs_0_, f32[2,3584]{1,0:T(2,128)S(1)} %get-tuple-element.39.refs_1_, f32[2,3584]{1,0:T(2,128)S(1)} %get-tuple-element.40.refs_2_), custom_call_target="tpu_custom_call" | custom-call | flops 11274289152 | bytes 44040192 | tf_op jit(solution)/shard_map/cross/pallas_call | solution.py:208
  80.9 0.1 collective-permute-start.5
  80.9 6.1 %cross.2.own_ref = f32[64,3584]{1,0:T(8,128)S(1)} custom-call(bf16[8,64,256]{2,1,0:T(8,128)(2,1)S(1)} %all_to_all.16.proj_ref, bf16[2048,14336]{1,0:T(8,128)(2,1)} %act_ref.3, f32[2,3584]{1,0:T(2,128)S(1)} %get-tuple-element.37.refs_0_), custom_call_target="tpu_custom_call" | custom-call | flops 3758096384 | bytes 14680064 | tf_op jit(solution)/shard_map/cross/pallas_call | solution.py:208
  87.0 0.6 collective-permute-start.4
  87.6 1.3 %combine.2 = (bf16[128,14336]{1,0:T(8,128)(2,1)S(1)}, f32[32,128]{1,0:T(8,128)S(1)}) custom-call(f32[64,10752]{1,0:T(8,128)S(1)} %cross.3.own_ref, f32[64,10752]{1,0:T(8,128)S(1)} %collective-permute-done.5.got_ref, f32[2,3584]{1,0:T(2,128)S(1)} %get-tuple-element.38.refs_0_, f32[2,3584]{1,0:T(2,128)S(1)} %get-tuple-element.39.refs_1_, ...), custom_call_target="tpu_custom_call" | custom-call | flops 352321536 | bytes 8257536 | tf_op jit(solution)/shard_map/combine/pallas_call | solution.py:256
  88.9 0.8 collective-permute-done.4.got_ref
  89.7 0.7 combine.3
  90.3 10.9 %all_to_all.17.gram_ref = f32[8,32,128]{2,1,0:T(8,128)S(1)} all-to-all(f32[8,32,128]{2,1,0:T(8,128)S(1)} %get-tuple-element.43), channel_id=1, replica_groups=mesh['groups'=2,'neuron'=8,'token'=2] {'neuron'}, dimensions={0} | all-to-all | bytes 262144 | tf_op jit(solution)/shard_map/all_to_all | solution.py:401
  101.3 6.8 %finish.1 = f32[64,14336]{1,0:T(8,128)} custom-call(f32[8,32,128]{2,1,0:T(8,128)S(1)} %all_to_all.17.gram_ref, bf16[128,14336]{1,0:T(8,128)(2,1)S(1)} %get-tuple-element.44.both_ref), custom_call_target="tpu_custom_call" | custom-call | tf_op jit(solution)/shard_map/finish/pallas_call | solution.py:346
  (6 shorter events, 0.1 us)
Async XLA Ops:
  5.7 6.5 %collective-permute-start = (f32[2,3584]{1,0:T(2,128)S(1)}, f32[2,3584]{1,0:T(2,128)S(1)}, u32[]{:S(2)}, u32[]{:S(2)}) collective-permute-start(f32[2,3584]{1,0:T(2,128)S(1)} %get-tuple-element.27.refs_2_), channel_id=1, source_target_pairs={{0,1},{1,0},{2,3},{3,2},{4,5},{5,4},{6,7},{7,6},{8,9},{9,8},{10,11... | collective-permute-start | bytes 86024 | tf_op jit(solution)/shard_map/ppermute | solution.py:31
  6.2 6.3 %copy-start = (f32[14336,64]{0,1:T(8,128)S(1)}, f32[14336,64]{0,1:T(8,128)}, u32[]{:S(2)}) copy-start(f32[14336,64]{0,1:T(8,128)} %param.3) | copy-start | bytes 11010052
  12.0 8.3 %collective-permute-start.1 = (f32[2,3584]{1,0:T(2,128)S(1)}, f32[2,3584]{1,0:T(2,128)S(1)}, u32[]{:S(2)}, u32[]{:S(2)}) collective-permute-start(f32[2,3584]{1,0:T(2,128)S(1)} %get-tuple-element.29.refs_2_), channel_id=1, source_target_pairs={{0,1},{1,0},{2,3},{3,2},{4,5},{5,4},{6,7},{7,6},{8,9},{9,8},{10,11... | collective-permute-start | bytes 86024 | tf_op jit(solution)/shard_map/ppermute | solution.py:31
  20.1 8.3 %collective-permute-start.3 = (f32[2,3584]{1,0:T(2,128)S(1)}, f32[2,3584]{1,0:T(2,128)S(1)}, u32[]{:S(2)}, u32[]{:S(2)}) collective-permute-start(f32[2,3584]{1,0:T(2,128)S(1)} %get-tuple-element.33.refs_1_), channel_id=1, source_target_pairs={{0,1},{1,0},{2,3},{3,2},{4,5},{5,4},{6,7},{7,6},{8,9},{9,8},{10,11... | collective-permute-start | bytes 86024 | tf_op jit(solution)/shard_map/ppermute | solution.py:31
  28.0 5.0 %collective-permute-start.2 = (f32[2,3584]{1,0:T(2,128)S(1)}, f32[2,3584]{1,0:T(2,128)S(1)}, u32[]{:S(2)}, u32[]{:S(2)}) collective-permute-start(f32[2,3584]{1,0:T(2,128)S(1)} %get-tuple-element.32.refs_1_), channel_id=1, source_target_pairs={{0,1},{1,0},{2,3},{3,2},{4,5},{5,4},{6,7},{7,6},{8,9},{9,8},{10,11... | collective-permute-start | bytes 86024 | tf_op jit(solution)/shard_map/ppermute | solution.py:31
  80.9 6.7 %collective-permute-start.5 = (f32[64,10752]{1,0:T(8,128)S(1)}, f32[64,10752]{1,0:T(8,128)S(1)}, u32[]{:S(2)}, u32[]{:S(2)}) collective-permute-start(f32[64,10752]{1,0:T(8,128)S(1)} %cross.3.own_ref), channel_id=1, source_target_pairs={{0,1},{1,0},{2,3},{3,2},{4,5},{5,4},{6,7},{7,6},{8,9},{9,8},{10,11... | collective-permute-start | bytes 8257544 | tf_op jit(solution)/shard_map/ppermute | solution.py:31
  87.0 2.7 %collective-permute-start.4 = (f32[64,3584]{1,0:T(8,128)S(1)}, f32[64,3584]{1,0:T(8,128)S(1)}, u32[]{:S(2)}, u32[]{:S(2)}) collective-permute-start(f32[64,3584]{1,0:T(8,128)S(1)} %cross.2.own_ref), channel_id=1, source_target_pairs={{0,1},{1,0},{2,3},{3,2},{4,5},{5,4},{6,7},{7,6},{8,9},{9,8},{10,11... | collective-permute-start | bytes 2752520 | tf_op jit(solution)/shard_map/ppermute | solution.py:31

commit v7 on v6

--- a/solution.py
+++ b/solution.py
@@ -14,12 +14,12 @@
 NT = (((1,), (1,)), ((), ()))
 ROWS = 256
 CHUNKS = 4
-KEEP = 3
+KEEP = 2
 DEPTH = 4
-SUB = 512
+SUB = 896
 FINAL = 2048
 LANES = 512
-DELAY = 2
+DELAY = 1
 SCOPED = 6 * MIB
 
 
@@ -40,11 +40,11 @@
     return pl.ds(j * ROWS if isinstance(j, int) else pl.multiple_of(j * ROWS, ROWS), ROWS)
 
 
-def stream_kernel(tokens, chunk, loads, at_chunk, starts, *refs):
+def stream_kernel(tokens, chunk, loads, at_chunk, starts, ahead, *refs):
     projects = at_chunk is not None
     refs = list(refs)
     take = refs.pop
-    if loads is not None:
+    if loads is not None or ahead:
         act_ref = take(0)
     if loads != 0:
         buf_ref = take(0)
@@ -58,6 +58,8 @@
     rows = tok_dev // ROWS
     if projects:
         proj_ref, stat_ref = take(0), take(0)
+    if ahead:
+        ahead_ref = take(0)
     if loads is not None:
         acc_ref, sem = take(0), take(0)
         into = loads % slots
@@ -73,6 +75,9 @@
             copy.start()
     if projects:
         scaled_ref = take(0)
+        if ahead:
+            early = pltpu.make_async_copy(act_ref.at[:, pl.ds(0, ahead)], ahead_ref, take(0))
+            early.start()
         held = at_chunk % slots
         sums = own_ref[...] + got_ref[...]
         mean = sums[0:1] / tokens
@@ -129,18 +134,21 @@
 
         gather(rows - 1)
         add_sums(rows - 1)
+    if ahead:
+        early.wait()
     if loads is not None:
         sums_ref[0:1] = jnp.sum(acc_ref[0:8], axis=0, keepdims=True)
         sums_ref[1:2] = jnp.sum(acc_ref[8:16], axis=0, keepdims=True)
 
 
-def stream(tokens, chunk, act, loads, buf, at, own, got, basis_t, part, last):
+def stream(tokens, chunk, act, loads, buf, at, own, got, basis_t, part, last, ahead):
     rows, cols = act.shape[0], basis_t.shape[0]
     vmem = pl.BlockSpec(memory_space=pltpu.VMEM)
     args, in_specs, outs, scratch, aliases = [], [], [], [], {}
-    if loads is not None:
+    if loads is not None or ahead:
         args.append(act)
         in_specs.append(pl.BlockSpec(memory_space=pl.ANY))
+    if loads is not None:
         outs += [pltpu.VMEM((KEEP, rows, chunk), BF16), jax.ShapeDtypeStruct((2, chunk), F32)]
         scratch += [pltpu.VMEM((16, chunk), F32), pltpu.SemaphoreType.DMA((rows // ROWS,))]
     if loads != 0:
@@ -159,8 +167,11 @@
             jax.ShapeDtypeStruct((2, chunk), F32),
         ]
         scratch.append(pltpu.VMEM((cols, chunk), BF16))
+    if ahead:
+        outs.append(pltpu.VMEM((rows, ahead), BF16))
+        scratch.append(pltpu.SemaphoreType.DMA)
     return list(pl.pallas_call(
-        functools.partial(stream_kernel, tokens, chunk, loads, at, part is None),
+        functools.partial(stream_kernel, tokens, chunk, loads, at, part is None, ahead),
         in_specs=in_specs,
         out_specs=[vmem] * len(outs),
         out_shape=outs,
@@ -174,49 +185,65 @@
     )(*args))
 
 
-def cross_kernel(start, sub, proj_ref, act_ref, *refs):
-    *stat_refs, out_ref, buf_ref, sem = refs
-    depth = buf_ref.shape[0]
+def cross_kernel(start, last, proj_ref, act_ref, ahead_ref, *refs):
+    if last:
+        *stat_refs, out_ref, buf_ref, sem = refs
+    else:
+        *stat_refs, out_ref, next_ref, buf_ref, sem, next_sem = refs
+    depth, _, sub = buf_ref.shape
     chunk = stat_refs[0].shape[1]
     blocks = out_ref.shape[1] // sub
     copies = [
         pltpu.make_async_copy(
             act_ref.at[:, pl.ds(start + s * sub, sub)], buf_ref.at[s % depth], sem.at[s % depth]
         )
-        for s in range(blocks)
+        for s in range(1, blocks)
     ]
+    if not last:
+        copies.append(
+            pltpu.make_async_copy(act_ref.at[:, pl.ds(start + blocks * sub, sub)], next_ref, next_sem)
+        )
     for copy in copies[:depth]:
         copy.start()
     proj = jnp.concatenate([proj_ref[r] for r in range(proj_ref.shape[0])], axis=1)
     total = jnp.sum(proj.astype(F32), axis=1, keepdims=True)
-    for s, copy in enumerate(copies):
+    for s in range(blocks):
         piece, at = divmod(s * sub, chunk)
         mean = stat_refs[piece][0:1, at : at + sub]
-        copy.wait()
-        prod = jnp.dot(proj, buf_ref[s % depth], preferred_element_type=F32)
-        if s + depth < blocks:
-            copies[s + depth].start()
+        if s:
+            copies[s - 1].wait()
+        act = buf_ref[s % depth] if s else ahead_ref[...]
+        prod = jnp.dot(proj, act, preferred_element_type=F32)
+        if s and s - 1 + depth < len(copies):
+            copies[s - 1 + depth].start()
         out_ref[:, s * sub : s * sub + sub] = prod - total * mean
-
-
-def cross(proj, act, stats, start):
+    if not last:
+        copies[-1].wait()
+
+
+def cross(proj, act, ahead, stats, start):
     cols, rows = proj.shape[1], act.shape[0]
-    chunk = stats[0].shape[1]
-    width = chunk * len(stats)
-    sub = block_of(chunk, SUB)
+    sub = ahead.shape[1]
+    width = stats[0].shape[1] * len(stats)
+    last = start + width == act.shape[1]
     vmem = pl.BlockSpec(memory_space=pltpu.VMEM)
+    outs = [jax.ShapeDtypeStruct((cols, width), F32)]
+    scratch = [pltpu.VMEM((DEPTH, rows, sub), BF16), pltpu.SemaphoreType.DMA((DEPTH,))]
+    if not last:
+        outs.append(pltpu.VMEM((rows, sub), BF16))
+        scratch.append(pltpu.SemaphoreType.DMA)
     return pl.pallas_call(
-        functools.partial(cross_kernel, start, sub),
-        in_specs=[vmem, pl.BlockSpec(memory_space=pl.ANY)] + [vmem] * len(stats),
-        out_specs=vmem,
-        out_shape=jax.ShapeDtypeStruct((cols, width), F32),
-        scratch_shapes=[pltpu.VMEM((DEPTH, rows, sub), BF16), pltpu.SemaphoreType.DMA((DEPTH,))],
+        functools.partial(cross_kernel, start, last),
+        in_specs=[vmem, pl.BlockSpec(memory_space=pl.ANY), vmem] + [vmem] * len(stats),
+        out_specs=[vmem] * len(outs),
+        out_shape=outs,
+        scratch_shapes=scratch,
         compiler_params=pltpu.CompilerParams(vmem_limit_bytes=40 * MIB),
         cost_estimate=pl.CostEstimate(
             flops=8 * rows * cols * width, bytes_accessed=2 * rows * width, transcendentals=0
         ),
         name="cross",
-    )(proj, act, *stats)
+    )(proj, act, ahead, *stats)
 
 
 def combine_kernel(start, pieces, last, tokens, own_ref, got_ref, *refs):
@@ -370,7 +397,8 @@
         at = step - DELAY if step >= DELAY else None
         sums = (None, None) if at is None else (own[at], got[at])
         results = stream(
-            tokens, chunk, activations, loads, buf, at, *sums, basis_t, part, at == chunks - 1
+            tokens, chunk, activations, loads, buf, at, *sums, basis_t, part,
+            at == chunks - 1, block_of(chunk, SUB) if at == chunks - 1 else 0,
         )
         if loads is not None:
             buf = results.pop(0)
@@ -379,6 +407,7 @@
         if at is not None:
             part = results.pop(0)
             stats.append(results.pop(0))
+    (ahead,) = results
 
     blocks = part
     if tok_dev // n != ROWS:
@@ -393,8 +422,12 @@
     split = chunks - max(1, chunks // 4)
     spans = [(0, split), (split, chunks)] if split else [(0, chunks)]
     spans = [(lo * chunk, stats[lo:hi]) for lo, hi in spans]
-    terms = [cross(proj, activations, stat, start) for start, stat in spans]
-    swapped = [swap_tokens(term) for term in terms]
+    terms, swapped = [], []
+    for start, stat in spans:
+        term, *rest = cross(proj, activations, ahead, stat, start)
+        ahead = rest[0] if rest else None
+        terms.append(term)
+        swapped.append(swap_tokens(term))
     both = gram = None
     for term, got, (start, stat) in zip(terms, swapped, spans):
         both, gram = combine(term, got, stat, start, neu_dev, tokens, n, both, gram)

time: 108 us -> 108 us (level)
  Pallas kernels: 65.3 us -> 61.4 us
  waiting for transfers between devices: 0.82 us -> 4.19 us
    ppermute x6, waiting for transfers between devices: 0.82 us -> 4.19 us  [swap_tokens(): return lax.ppermute(x, 'token', [(0, 1), (1, 0)])]
    pallas_call x6 -> x5, Pallas kernels: 35.8 us -> 33.3 us  [stream(): pl.pallas_call(functools.partial(stream_kernel, tokens, chunk, loads, at,...]
    pallas_call x2, Pallas kernels: 20.8 us -> 19.3 us  [cross(): pl.pallas_call(functools.partial(cross_kernel, start, last), in_specs=[vm...]
  transfers between devices with their start and end apart: 6 -> 6, of which waited for: 1 -> 5; matrix products, arithmetic and copies ran while one was open for 0% -> 0% of each run, Pallas kernels for 30% -> 6%
where the time goes in v7:
time: 108 us; the launch traced here: 107 us
  Pallas kernels  61.4 us (57%)
  blocking collectives  39.1 us (36%)
  waiting for transfers between devices  4.19 us (4%)
  starting transfers between devices  2.39 us (2%)
    pallas_call x5, Pallas kernels, stream(): pl.pallas_call(functools.partial(stream_kernel, tokens, chunk, loads, at,...  33.3 us
    pallas_call x2, Pallas kernels, cross(): pl.pallas_call(functools.partial(cross_kernel, start, last), in_specs=[vm...  19.3 us
    all_to_all x1, blocking collectives, local(): blocks = lax.all_to_all(blocks, 'neuron', 0, 0)  16.2 us
    all_to_all x1, blocking collectives, local(): proj = lax.all_to_all(blocks, 'neuron', 0, 0)  12 us
    all_to_all x1, blocking collectives, local(): grams = lax.all_to_all(gram, 'neuron', 0, 0)  10.9 us
    pallas_call x1, Pallas kernels, finish(): pl.pallas_call(functools.partial(finish_kernel, nb), in_specs=[vmem, vmem...  6.79 us
    ppermute x6, waiting for transfers between devices, swap_tokens(): return lax.ppermute(x, 'token', [(0, 1), (1, 0)])  4.19 us
    ppermute x6, starting transfers between devices, swap_tokens(): return lax.ppermute(x, 'token', [(0, 1), (1, 0)])  2.39 us
  transfers between devices with their start and end apart: 6, of which 5 were waited for; matrix products, arithmetic and copies ran while one was open for 0% of the time, Pallas kernels for 6%

profile of v7, /device:TPU:0, one launch (start us, length us, event | category | flops | bytes accessed | tf_op | source)
XLA Modules:
  0.0 107.4 jit_solution(14826677406872765324)
XLA Ops:
  0.0 5.8 %stream.5 = (bf16[2,2048,3584]{2,1,0:T(8,128)(2,1)S(1)}, f32[2,3584]{1,0:T(2,128)S(1)}) custom-call(bf16[2048,14336]{1,0:T(8,128)(2,1)} %act_ref.3), custom_call_target="tpu_custom_call" | custom-call | flops 3758096384 | bytes 14680064 | tf_op jit(solution)/shard_map/stream/pallas_call | solution.py:173
  5.8 0.5 collective-permute-start
  6.4 0.9 collective-permute-done.refs_3_
  7.2 7.6 %stream.6 = (bf16[2,2048,3584]{2,1,0:T(8,128)(2,1)S(1)}, f32[2,3584]{1,0:T(2,128)S(1)}, f32[8,64,256]{2,1,0:T(8,128)S(1)}, f32[2,3584]{1,0:T(2,128)S(1)}) custom-call(bf16[2048,14336]{1,0:T(8,128)(2,1)} %act_ref.3, bf16[2,2048,3584]{2,1,0:T(8,128)(2,1)S(1)} %get-tuple-element.28.refs_1_, ...), custom_call_target="tpu_custom_call", output_to_operand_aliasing={{0}: (1, {})} | custom-call | flops 3758096384 | bytes 14680064 | tf_op jit(solution)/shard_map/stream/pallas_call | solution.py:173
  14.9 0.4 collective-permute-start.1
  15.3 0.9 collective-permute-done.1.refs_3_
  16.1 7.7 %stream.7 = (bf16[2,2048,3584]{2,1,0:T(8,128)(2,1)S(1)}, f32[2,3584]{1,0:T(2,128)S(1)}, f32[8,64,256]{2,1,0:T(8,128)S(1)}, f32[2,3584]{1,0:T(2,128)S(1)}) custom-call(bf16[2048,14336]{1,0:T(8,128)(2,1)} %act_ref.3, bf16[2,2048,3584]{2,1,0:T(8,128)(2,1)S(1)} %get-tuple-element.30.refs_1_, ...), custom_call_target="tpu_custom_call", output_to_operand_aliasing={{0}: (1, {})} | custom-call | flops 3758096384 | bytes 14680064 | tf_op jit(solution)/shard_map/stream/pallas_call | solution.py:173
  23.8 0.4 collective-permute-start.2
  24.2 0.9 collective-permute-done.2.refs_3_
  25.1 7.7 %stream.8 = (bf16[2,2048,3584]{2,1,0:T(8,128)(2,1)S(1)}, f32[2,3584]{1,0:T(2,128)S(1)}, f32[8,64,256]{2,1,0:T(8,128)S(1)}, f32[2,3584]{1,0:T(2,128)S(1)}) custom-call(bf16[2048,14336]{1,0:T(8,128)(2,1)} %act_ref.3, bf16[2,2048,3584]{2,1,0:T(8,128)(2,1)S(1)} %get-tuple-element.33.refs_1_, ...), custom_call_target="tpu_custom_call", output_to_operand_aliasing={{0}: (1, {})} | custom-call | flops 3758096384 | bytes 14680064 | tf_op jit(solution)/shard_map/stream/pallas_call | solution.py:173
  32.7 0.4 collective-permute-start.3
  33.1 0.9 collective-permute-done.3.refs_3_
  34.0 4.5 %stream.9 = (bf16[8,64,256]{2,1,0:T(8,128)(2,1)S(1)}, f32[2,3584]{1,0:T(2,128)S(1)}, bf16[2048,896]{1,0:T(8,128)(2,1)S(1)}) custom-call(bf16[2048,14336]{1,0:T(8,128)(2,1)} %act_ref.3, bf16[2,2048,3584]{2,1,0:T(8,128)(2,1)S(1)} %get-tuple-element.36.refs_1_, f32[2,3584]{1,0:T(2,128)S(1)} %get-tuple-element.37.refs_2_, ...), custom_call_target="tpu_custom_call" | custom-call | flops 3758096384 | bytes 14680064 | tf_op jit(solution)/shard_map/stream/pallas_call | solution.py:173
  38.5 16.2 %all_to_all.15 = bf16[8,64,256]{2,1,0:T(8,128)(2,1)S(1)} all-to-all(bf16[8,64,256]{2,1,0:T(8,128)(2,1)S(1)} %get-tuple-element.39), channel_id=1, replica_groups=mesh['groups'=2,'neuron'=8,'token'=2] {'neuron'}, dimensions={0} | all-to-all | bytes 524288 | tf_op jit(solution)/shard_map/all_to_all | solution.py:415
  54.8 12.0 %all_to_all.16.proj_ref = bf16[8,64,256]{2,1,0:T(8,128)(2,1)S(1)} all-to-all(bf16[8,64,256]{2,1,0:T(8,128)(2,1)S(1)} %broadcast_in_dim.9), channel_id=1, replica_groups=mesh['groups'=2,'neuron'=8,'token'=2] {'neuron'}, dimensions={0} | all-to-all | bytes 524288 | tf_op jit(solution)/shard_map/all_to_all | solution.py:418
  66.8 14.1 %cross.2 = (f32[64,10752]{1,0:T(8,128)S(1)}, bf16[2048,896]{1,0:T(8,128)(2,1)S(1)}) custom-call(bf16[8,64,256]{2,1,0:T(8,128)(2,1)S(1)} %all_to_all.16.proj_ref, bf16[2048,14336]{1,0:T(8,128)(2,1)} %act_ref.3, bf16[2048,896]{1,0:T(8,128)(2,1)S(1)} %get-tuple-element.40.ahead_ref, f32[2,3584]{1,0:T(2,128)S(1)} %get-tuple-element.41.refs_0_, ...), custom_call_target="tpu_custom_call" | custom-call | flops 11274289152 | bytes 44040192 | tf_op jit(solution)/shard_map/cross/pallas_call | solution.py:235
  80.8 0.1 collective-permute-start.5
  80.9 5.2 %cross.3.own_ref = f32[64,3584]{1,0:T(8,128)S(1)} custom-call(bf16[8,64,256]{2,1,0:T(8,128)(2,1)S(1)} %all_to_all.16.proj_ref, bf16[2048,14336]{1,0:T(8,128)(2,1)} %act_ref.3, bf16[2048,896]{1,0:T(8,128)(2,1)S(1)} %get-tuple-element.44.ahead_ref, f32[2,3584]{1,0:T(2,128)S(1)} %get-tuple-element.45.refs_0_), custom_call_target="tpu_custom_call" | custom-call | flops 3758096384 | bytes 14680064 | tf_op jit(solution)/shard_map/cross/pallas_call | solution.py:235
  86.2 0.6 collective-permute-start.4
  86.7 1.3 %combine.2 = (bf16[128,14336]{1,0:T(8,128)(2,1)S(1)}, f32[32,128]{1,0:T(8,128)S(1)}) custom-call(f32[64,10752]{1,0:T(8,128)S(1)} %get-tuple-element.46.own_ref, f32[64,10752]{1,0:T(8,128)S(1)} %collective-permute-done.5.got_ref, f32[2,3584]{1,0:T(2,128)S(1)} %get-tuple-element.41.refs_0_, f32[2,3584]{1,0:T(2,128)S(1)} %get-tuple-element.42.refs_1_, ...), custom_call_target="tpu_custom_call" | custom-call | flops 352321536 | bytes 8257536 | tf_op jit(solution)/shard_map/combine/pallas_call | solution.py:283
  88.1 0.8 collective-permute-done.4.got_ref
  88.8 0.7 combine.3
  89.5 10.9 %all_to_all.17.gram_ref = f32[8,32,128]{2,1,0:T(8,128)S(1)} all-to-all(f32[8,32,128]{2,1,0:T(8,128)S(1)} %get-tuple-element.49), channel_id=1, replica_groups=mesh['groups'=2,'neuron'=8,'token'=2] {'neuron'}, dimensions={0} | all-to-all | bytes 262144 | tf_op jit(solution)/shard_map/all_to_all | solution.py:434
  100.4 6.8 %finish.1 = f32[64,14336]{1,0:T(8,128)} custom-call(f32[8,32,128]{2,1,0:T(8,128)S(1)} %all_to_all.17.gram_ref, bf16[128,14336]{1,0:T(8,128)(2,1)S(1)} %get-tuple-element.50.both_ref), custom_call_target="tpu_custom_call" | custom-call | tf_op jit(solution)/shard_map/finish/pallas_call | solution.py:373
  (5 shorter events, 0.1 us)
Async XLA Ops:
  0.0 7.2 %copy-start = (f32[14336,64]{0,1:T(8,128)S(1)}, f32[14336,64]{0,1:T(8,128)}, u32[]{:S(2)}) copy-start(f32[14336,64]{0,1:T(8,128)} %param.3) | copy-start | bytes 11010052
  5.8 1.4 %collective-permute-start = (f32[2,3584]{1,0:T(2,128)S(1)}, f32[2,3584]{1,0:T(2,128)S(1)}, u32[]{:S(2)}, u32[]{:S(2)}) collective-permute-start(f32[2,3584]{1,0:T(2,128)S(1)} %get-tuple-element.29.refs_2_), channel_id=1, source_target_pairs={{0,1},{1,0},{2,3},{3,2},{4,5},{5,4},{6,7},{7,6},{8,9},{9,8},{10,11... | collective-permute-start | bytes 86024 | tf_op jit(solution)/shard_map/ppermute | solution.py:31
  14.9 1.3 %collective-permute-start.1 = (f32[2,3584]{1,0:T(2,128)S(1)}, f32[2,3584]{1,0:T(2,128)S(1)}, u32[]{:S(2)}, u32[]{:S(2)}) collective-permute-start(f32[2,3584]{1,0:T(2,128)S(1)} %get-tuple-element.31.refs_2_), channel_id=1, source_target_pairs={{0,1},{1,0},{2,3},{3,2},{4,5},{5,4},{6,7},{7,6},{8,9},{9,8},{10,11... | collective-permute-start | bytes 86024 | tf_op jit(solution)/shard_map/ppermute | solution.py:31
  23.8 1.3 %collective-permute-start.2 = (f32[2,3584]{1,0:T(2,128)S(1)}, f32[2,3584]{1,0:T(2,128)S(1)}, u32[]{:S(2)}, u32[]{:S(2)}) collective-permute-start(f32[2,3584]{1,0:T(2,128)S(1)} %get-tuple-element.34.refs_2_), channel_id=1, source_target_pairs={{0,1},{1,0},{2,3},{3,2},{4,5},{5,4},{6,7},{7,6},{8,9},{9,8},{10,11... | collective-permute-start | bytes 86024 | tf_op jit(solution)/shard_map/ppermute | solution.py:31
  32.7 1.3 %collective-permute-start.3 = (f32[2,3584]{1,0:T(2,128)S(1)}, f32[2,3584]{1,0:T(2,128)S(1)}, u32[]{:S(2)}, u32[]{:S(2)}) collective-permute-start(f32[2,3584]{1,0:T(2,128)S(1)} %get-tuple-element.37.refs_2_), channel_id=1, source_target_pairs={{0,1},{1,0},{2,3},{3,2},{4,5},{5,4},{6,7},{7,6},{8,9},{9,8},{10,11... | collective-permute-start | bytes 86024 | tf_op jit(solution)/shard_map/ppermute | solution.py:31
  80.8 5.9 %collective-permute-start.5 = (f32[64,10752]{1,0:T(8,128)S(1)}, f32[64,10752]{1,0:T(8,128)S(1)}, u32[]{:S(2)}, u32[]{:S(2)}) collective-permute-start(f32[64,10752]{1,0:T(8,128)S(1)} %get-tuple-element.46.own_ref), channel_id=1, source_target_pairs={{0,1},{1,0},{2,3},{3,2},{4,5},{5,4},{6,7},{7,6},{8,9},{9,8},{10,11... | collective-permute-start | bytes 8257544 | tf_op jit(solution)/shard_map/ppermute | solution.py:31
  86.2 2.7 %collective-permute-start.4 = (f32[64,3584]{1,0:T(8,128)S(1)}, f32[64,3584]{1,0:T(8,128)S(1)}, u32[]{:S(2)}, u32[]{:S(2)}) collective-permute-start(f32[64,3584]{1,0:T(8,128)S(1)} %cross.3.own_ref), channel_id=1, source_target_pairs={{0,1},{1,0},{2,3},{3,2},{4,5},{5,4},{6,7},{7,6},{8,9},{9,8},{10,11... | collective-permute-start | bytes 2752520 | tf_op jit(solution)/shard_map/ppermute | solution.py:31

commit v8 on v7

--- a/solution.py
+++ b/solution.py
@@ -14,13 +14,14 @@
 NT = (((1,), (1,)), ((), ()))
 ROWS = 256
 CHUNKS = 4
-KEEP = 2
+KEEP = 3
+PEEK = 3
 DEPTH = 4
 SUB = 896
 FINAL = 2048
 LANES = 512
-DELAY = 1
-SCOPED = 6 * MIB
+DELAY = 2
+SCOPED = 3 * MIB
 
 
 def block_of(size, most):
@@ -40,7 +41,7 @@
     return pl.ds(j * ROWS if isinstance(j, int) else pl.multiple_of(j * ROWS, ROWS), ROWS)
 
 
-def stream_kernel(tokens, chunk, loads, at_chunk, starts, ahead, *refs):
+def stream_kernel(tokens, chunk, loads, at_chunk, starts, ahead, given, peek, *refs):
     projects = at_chunk is not None
     refs = list(refs)
     take = refs.pop
@@ -65,11 +66,12 @@
         into = loads % slots
         copies = [
             pltpu.make_async_copy(
-                act_ref.at[pl.ds(j * ROWS, ROWS), pl.ds(loads * chunk, chunk)],
-                buf_ref.at[into, pl.ds(j * ROWS, ROWS)],
-                sem.at[j],
+                act_ref.at[pl.ds(j * ROWS, ROWS), pl.ds(origin * chunk, chunk)],
+                buf_ref.at[origin % slots, pl.ds(j * ROWS, ROWS)],
+                sem.at[j + (rows if origin > loads else 0)],
             )
-            for j in range(rows)
+            for origin, lo, hi in ((loads, given, rows), (loads + 1, 0, peek))
+            for j in range(lo, hi)
         ]
         for copy in copies:
             copy.start()
@@ -117,11 +119,16 @@
         for j in range(rows):
             project(j)
     elif not projects:
-
-        @pl.loop(0, rows)
+        for j in range(given):
+            add_sums(j)
+
+        @pl.loop(given, rows)
         def _(j):
             gather(j)
             add_sums(j)
+
+        for copy in copies[rows - given :]:
+            copy.wait()
 
     else:
         project(0)
@@ -141,7 +148,7 @@
         sums_ref[1:2] = jnp.sum(acc_ref[8:16], axis=0, keepdims=True)
 
 
-def stream(tokens, chunk, act, loads, buf, at, own, got, basis_t, part, last, ahead):
+def stream(tokens, chunk, act, loads, buf, at, own, got, basis_t, part, last, ahead, given, peek):
     rows, cols = act.shape[0], basis_t.shape[0]
     vmem = pl.BlockSpec(memory_space=pltpu.VMEM)
     args, in_specs, outs, scratch, aliases = [], [], [], [], {}
@@ -150,7 +157,7 @@
         in_specs.append(pl.BlockSpec(memory_space=pl.ANY))
     if loads is not None:
         outs += [pltpu.VMEM((KEEP, rows, chunk), BF16), jax.ShapeDtypeStruct((2, chunk), F32)]
-        scratch += [pltpu.VMEM((16, chunk), F32), pltpu.SemaphoreType.DMA((rows // ROWS,))]
+        scratch += [pltpu.VMEM((16, chunk), F32), pltpu.SemaphoreType.DMA((rows // ROWS + peek,))]
     if loads != 0:
         if loads is not None:
             aliases = {len(args): 0}
@@ -171,7 +178,7 @@
         outs.append(pltpu.VMEM((rows, ahead), BF16))
         scratch.append(pltpu.SemaphoreType.DMA)
     return list(pl.pallas_call(
-        functools.partial(stream_kernel, tokens, chunk, loads, at, part is None, ahead),
+        functools.partial(stream_kernel, tokens, chunk, loads, at, part is None, ahead, given, peek),
         in_specs=in_specs,
         out_specs=[vmem] * len(outs),
         out_shape=outs,
@@ -316,23 +323,37 @@
     def line(x, i):
         return jnp.broadcast_to(x[i : i + 1], tile)
 
-    for k in range(0, cols, 2):
-        at, inner = divmod(k, 8)
-        first, second = line(tall[at], inner), line(tall[at], inner + 1)
-        left, right = column(tall[at], k), column(tall[at], k + 1)
-        a, b, c = line(left, inner), line(right, inner), line(right, inner + 1)
+    def factors_of(a, b, c):
         over = 1.0 / (a * c - b * b)
         a, b, c = a * over, b * over, c * over
-        for t in range(at, cols // 8):
-            if t > at:
-                left, right = column(tall[t], k), column(tall[t], k + 1)
-            by_first, by_second = c * left - b * right, a * right - b * left
-            if t == at:
-                if inner == 6:
-                    continue
-                below = within > inner + 1
-                by_first, by_second = jnp.where(below, by_first, 0.0), jnp.where(below, by_second, 0.0)
-            tall[t] = tall[t] - (by_first * first + by_second * second)
+        return lambda x, y: (c * x - b * y, a * y - b * x)
+
+    for at in range(cols // 8):
+        base = 8 * at
+        rows = [line(tall[at], j) for j in range(8)]
+        below = range(at, cols // 8)
+        columns = {t: [column(tall[t], base + j) for j in range(8)] for t in below}
+        pivots = {(i, j): line(columns[at][j], i) for i in range(8) for j in range(i + 1)}
+        change = {t: 0.0 for t in below}
+        for z in range(0, 8, 2):
+            factors = factors_of(pivots[z, z], pivots[z + 1, z], pivots[z + 1, z + 1])
+            later = range(z + 2, 8)
+            for t in below:
+                first, second = factors(columns[t][z], columns[t][z + 1])
+                for j in later:
+                    columns[t][j] = columns[t][j] - (first * pivots[j, z] + second * pivots[j, z + 1])
+                if t == at:
+                    first = jnp.where(within > z + 1, first, 0.0)
+                    second = jnp.where(within > z + 1, second, 0.0)
+                change[t] = change[t] + (first * rows[z] + second * rows[z + 1])
+            own = {i: factors(pivots[i, z], pivots[i, z + 1]) for i in later}
+            for i in later:
+                first, second = own[i]
+                for j in range(z + 2, i + 1):
+                    pivots[i, j] = pivots[i, j] - (first * pivots[j, z] + second * pivots[j, z + 1])
+                rows[i] = rows[i] - (first * rows[z] + second * rows[z + 1])
+        for t in below:
+            tall[t] = tall[t] - change[t]
     wide = jnp.concatenate(tall, axis=0)
     diag = jnp.sum(jnp.where(row == lane, wide[:, :cols], 0.0), axis=1, keepdims=True)
     odd = row % 2 == 1
@@ -392,6 +413,7 @@
 
     own, got, stats = [], [], []
     part = buf = None
+    peek = PEEK if DELAY > 1 and chunks > 1 else 0
     for step in range(chunks + DELAY):
         loads = step if step < chunks else None
         at = step - DELAY if step >= DELAY else None
@@ -399,6 +421,7 @@
         results = stream(
             tokens, chunk, activations, loads, buf, at, *sums, basis_t, part,
             at == chunks - 1, block_of(chunk, SUB) if at == chunks - 1 else 0,
+            peek if step == 1 else 0, peek if step == 0 else 0,
         )
         if loads is not None:
             buf = results.pop(0)

time: 108 us -> 105 us (0.972)
  waiting for transfers between devices: 4.19 us -> 0.78 us
    ppermute x6, waiting for transfers between devices: 4.19 us -> 0.78 us  [swap_tokens(): return lax.ppermute(x, 'token', [(0, 1), (1, 0)])]
    pallas_call x5 -> x6, Pallas kernels: 33.3 us -> 35.7 us  [stream(): pl.pallas_call(functools.partial(stream_kernel, tokens, chunk, loads, at,...]
    pallas_call x1, Pallas kernels: 6.79 us -> 4.51 us  [finish(): pl.pallas_call(functools.partial(finish_kernel, nb), in_specs=[vmem, vmem...]
  transfers between devices with their start and end apart: 6 -> 6, of which waited for: 5 -> 1; matrix products, arithmetic and copies ran while one was open for 0% -> 0% of each run, Pallas kernels for 6% -> 29%
where the time goes in v8:
time: 105 us; the launch traced here: 104 us
  Pallas kernels  61.5 us (59%)
  blocking collectives  39.5 us (38%)
  starting transfers between devices  1.91 us (2%)
    pallas_call x6, Pallas kernels, stream(): pl.pallas_call(functools.partial(stream_kernel, tokens, chunk, loads, at,...  35.7 us
    pallas_call x2, Pallas kernels, cross(): pl.pallas_call(functools.partial(cross_kernel, start, last), in_specs=[vm...  19.3 us
    all_to_all x1, blocking collectives, local(): blocks = lax.all_to_all(blocks, 'neuron', 0, 0)  16.2 us
    all_to_all x1, blocking collectives, local(): proj = lax.all_to_all(blocks, 'neuron', 0, 0)  12.4 us
    all_to_all x1, blocking collectives, local(): grams = lax.all_to_all(gram, 'neuron', 0, 0)  10.9 us
    pallas_call x1, Pallas kernels, finish(): pl.pallas_call(functools.partial(finish_kernel, nb), in_specs=[vmem, vmem...  4.51 us
  transfers between devices with their start and end apart: 6, of which 1 were waited for; matrix products, arithmetic and copies ran while one was open for 0% of the time, Pallas kernels for 29%

profile of v8, /device:TPU:0, one launch (start us, length us, event | category | flops | bytes accessed | tf_op | source)
XLA Modules:
  0.0 104.3 jit_solution(7251506020003658370)
XLA Ops:
  0.0 7.0 %stream.6 = (bf16[3,2048,3584]{2,1,0:T(8,128)(2,1)S(1)}, f32[2,3584]{1,0:T(2,128)S(1)}) custom-call(bf16[2048,14336]{1,0:T(8,128)(2,1)} %act_ref.3), custom_call_target="tpu_custom_call" | custom-call | flops 3758096384 | bytes 14680064 | tf_op jit(solution)/shard_map/stream/pallas_call | solution.py:180
  7.0 0.5 collective-permute-start
  7.6 4.3 %stream.7 = (bf16[3,2048,3584]{2,1,0:T(8,128)(2,1)S(1)}, f32[2,3584]{1,0:T(2,128)S(1)}) custom-call(bf16[2048,14336]{1,0:T(8,128)(2,1)} %act_ref.3, bf16[3,2048,3584]{2,1,0:T(8,128)(2,1)S(1)} %get-tuple-element.28.refs_1_), custom_call_target="tpu_custom_call", output_to_operand_aliasing={{0}: (1, {})} | custom-call | flops 3758096384 | bytes 14680064 | tf_op jit(solution)/shard_map/stream/pallas_call | solution.py:180
  11.8 0.1 collective-permute-start.1
  12.0 0.0 collective-permute-done.refs_3_
  12.0 0.3 copy-done
  12.3 7.6 %stream.8 = (bf16[3,2048,3584]{2,1,0:T(8,128)(2,1)S(1)}, f32[2,3584]{1,0:T(2,128)S(1)}, f32[8,64,256]{2,1,0:T(8,128)S(1)}, f32[2,3584]{1,0:T(2,128)S(1)}) custom-call(bf16[2048,14336]{1,0:T(8,128)(2,1)} %act_ref.3, bf16[3,2048,3584]{2,1,0:T(8,128)(2,1)S(1)} %get-tuple-element.29.refs_1_, ...), custom_call_target="tpu_custom_call", output_to_operand_aliasing={{0}: (1, {})} | custom-call | flops 3758096384 | bytes 14680064 | tf_op jit(solution)/shard_map/stream/pallas_call | solution.py:180
  19.9 0.2 collective-permute-start.3
  20.1 7.7 %stream.9 = (bf16[3,2048,3584]{2,1,0:T(8,128)(2,1)S(1)}, f32[2,3584]{1,0:T(2,128)S(1)}, f32[8,64,256]{2,1,0:T(8,128)S(1)}, f32[2,3584]{1,0:T(2,128)S(1)}) custom-call(bf16[2048,14336]{1,0:T(8,128)(2,1)} %act_ref.3, bf16[3,2048,3584]{2,1,0:T(8,128)(2,1)S(1)} %get-tuple-element.31.refs_1_, ...), custom_call_target="tpu_custom_call", output_to_operand_aliasing={{0}: (1, {})} | custom-call | flops 3758096384 | bytes 14680064 | tf_op jit(solution)/shard_map/stream/pallas_call | solution.py:180
  27.8 0.4 collective-permute-start.2
  28.3 4.5 %stream.10 = (f32[8,64,256]{2,1,0:T(8,128)S(1)}, f32[2,3584]{1,0:T(2,128)S(1)}) custom-call(bf16[3,2048,3584]{2,1,0:T(8,128)(2,1)S(1)} %get-tuple-element.34.refs_0_.refs_1_, f32[2,3584]{1,0:T(2,128)S(1)} %get-tuple-element.36.refs_1_, f32[2,3584]{1,0:T(2,128)S(1)} %collective-permute-done.3.refs_2_, f32[64,14336]{1,0:T(8,128)S(1)} %bitcast.6, ...), custom_call_target="tpu_custom_call" | custom-call | flops 3758096384 | bytes 14680064 | tf_op jit(solution)/shard_map/stream/pallas_call | solution.py:180
  32.8 4.5 %stream.11 = (bf16[8,64,256]{2,1,0:T(8,128)(2,1)S(1)}, f32[2,3584]{1,0:T(2,128)S(1)}, bf16[2048,896]{1,0:T(8,128)(2,1)S(1)}) custom-call(bf16[2048,14336]{1,0:T(8,128)(2,1)} %act_ref.3, bf16[3,2048,3584]{2,1,0:T(8,128)(2,1)S(1)} %get-tuple-element.34.refs_0_.refs_1_, f32[2,3584]{1,0:T(2,128)S(1)} %get-tuple-element.35.refs_2_, ...), custom_call_target="tpu_custom_call" | custom-call | flops 3758096384 | bytes 14680064 | tf_op jit(solution)/shard_map/stream/pallas_call | solution.py:180
  37.3 16.2 %all_to_all.15 = bf16[8,64,256]{2,1,0:T(8,128)(2,1)S(1)} all-to-all(bf16[8,64,256]{2,1,0:T(8,128)(2,1)S(1)} %get-tuple-element.39), channel_id=1, replica_groups=mesh['groups'=2,'neuron'=8,'token'=2] {'neuron'}, dimensions={0} | all-to-all | bytes 524288 | tf_op jit(solution)/shard_map/all_to_all | solution.py:438
  53.6 12.4 %all_to_all.16.proj_ref = bf16[8,64,256]{2,1,0:T(8,128)(2,1)S(1)} all-to-all(bf16[8,64,256]{2,1,0:T(8,128)(2,1)S(1)} %broadcast_in_dim.9), channel_id=1, replica_groups=mesh['groups'=2,'neuron'=8,'token'=2] {'neuron'}, dimensions={0} | all-to-all | bytes 524288 | tf_op jit(solution)/shard_map/all_to_all | solution.py:441
  66.0 14.1 %cross.2 = (f32[64,10752]{1,0:T(8,128)S(1)}, bf16[2048,896]{1,0:T(8,128)(2,1)S(1)}) custom-call(bf16[8,64,256]{2,1,0:T(8,128)(2,1)S(1)} %all_to_all.16.proj_ref, bf16[2048,14336]{1,0:T(8,128)(2,1)} %act_ref.3, bf16[2048,896]{1,0:T(8,128)(2,1)S(1)} %get-tuple-element.40.ahead_ref, f32[2,3584]{1,0:T(2,128)S(1)} %get-tuple-element.41.refs_0_, ...), custom_call_target="tpu_custom_call" | custom-call | flops 11274289152 | bytes 44040192 | tf_op jit(solution)/shard_map/cross/pallas_call | solution.py:242
  80.1 0.1 collective-permute-start.5
  80.1 5.2 %cross.3.own_ref = f32[64,3584]{1,0:T(8,128)S(1)} custom-call(bf16[8,64,256]{2,1,0:T(8,128)(2,1)S(1)} %all_to_all.16.proj_ref, bf16[2048,14336]{1,0:T(8,128)(2,1)} %act_ref.3, bf16[2048,896]{1,0:T(8,128)(2,1)S(1)} %get-tuple-element.44.ahead_ref, f32[2,3584]{1,0:T(2,128)S(1)} %get-tuple-element.45.refs_0_), custom_call_target="tpu_custom_call" | custom-call | flops 3758096384 | bytes 14680064 | tf_op jit(solution)/shard_map/cross/pallas_call | solution.py:242
  85.4 0.6 collective-permute-start.4
  86.0 0.0 collective-permute-done.5.got_ref
  86.0 1.3 %combine.2 = (bf16[128,14336]{1,0:T(8,128)(2,1)S(1)}, f32[32,128]{1,0:T(8,128)S(1)}) custom-call(f32[64,10752]{1,0:T(8,128)S(1)} %get-tuple-element.46.own_ref, f32[64,10752]{1,0:T(8,128)S(1)} %collective-permute-done.5.got_ref, f32[2,3584]{1,0:T(2,128)S(1)} %get-tuple-element.41.refs_0_, f32[2,3584]{1,0:T(2,128)S(1)} %get-tuple-element.42.refs_1_, ...), custom_call_target="tpu_custom_call" | custom-call | flops 352321536 | bytes 8257536 | tf_op jit(solution)/shard_map/combine/pallas_call | solution.py:290
  87.3 0.8 collective-permute-done.4.got_ref
  88.1 0.7 combine.3
  88.7 10.9 %all_to_all.17.gram_ref = f32[8,32,128]{2,1,0:T(8,128)S(1)} all-to-all(f32[8,32,128]{2,1,0:T(8,128)S(1)} %get-tuple-element.49), channel_id=1, replica_groups=mesh['groups'=2,'neuron'=8,'token'=2] {'neuron'}, dimensions={0} | all-to-all | bytes 262144 | tf_op jit(solution)/shard_map/all_to_all | solution.py:457
  99.6 4.5 %finish.1 = f32[64,14336]{1,0:T(8,128)} custom-call(f32[8,32,128]{2,1,0:T(8,128)S(1)} %all_to_all.17.gram_ref, bf16[128,14336]{1,0:T(8,128)(2,1)S(1)} %get-tuple-element.50.both_ref), custom_call_target="tpu_custom_call" | custom-call | tf_op jit(solution)/shard_map/finish/pallas_call | solution.py:394
  (6 shorter events, 0.1 us)
Async XLA Ops:
  7.0 4.9 %collective-permute-start = (f32[2,3584]{1,0:T(2,128)S(1)}, f32[2,3584]{1,0:T(2,128)S(1)}, u32[]{:S(2)}, u32[]{:S(2)}) collective-permute-start(f32[2,3584]{1,0:T(2,128)S(1)} %get-tuple-element.30.refs_2_), channel_id=1, source_target_pairs={{0,1},{1,0},{2,3},{3,2},{4,5},{5,4},{6,7},{7,6},{8,9},{9,8},{10,11... | collective-permute-start | bytes 86024 | tf_op jit(solution)/shard_map/ppermute | solution.py:32
  7.6 4.7 %copy-start = (f32[14336,64]{0,1:T(8,128)S(1)}, f32[14336,64]{0,1:T(8,128)}, u32[]{:S(2)}) copy-start(f32[14336,64]{0,1:T(8,128)} %param.3) | copy-start | bytes 11010052
  11.8 8.3 %collective-permute-start.1 = (f32[2,3584]{1,0:T(2,128)S(1)}, f32[2,3584]{1,0:T(2,128)S(1)}, u32[]{:S(2)}, u32[]{:S(2)}) collective-permute-start(f32[2,3584]{1,0:T(2,128)S(1)} %get-tuple-element.32.refs_2_), channel_id=1, source_target_pairs={{0,1},{1,0},{2,3},{3,2},{4,5},{5,4},{6,7},{7,6},{8,9},{9,8},{10,11... | collective-permute-start | bytes 86024 | tf_op jit(solution)/shard_map/ppermute | solution.py:32
  19.9 8.3 %collective-permute-start.3 = (f32[2,3584]{1,0:T(2,128)S(1)}, f32[2,3584]{1,0:T(2,128)S(1)}, u32[]{:S(2)}, u32[]{:S(2)}) collective-permute-start(f32[2,3584]{1,0:T(2,128)S(1)} %get-tuple-element.36.refs_1_), channel_id=1, source_target_pairs={{0,1},{1,0},{2,3},{3,2},{4,5},{5,4},{6,7},{7,6},{8,9},{9,8},{10,11... | collective-permute-start | bytes 86024 | tf_op jit(solution)/shard_map/ppermute | solution.py:32
  27.8 5.0 %collective-permute-start.2 = (f32[2,3584]{1,0:T(2,128)S(1)}, f32[2,3584]{1,0:T(2,128)S(1)}, u32[]{:S(2)}, u32[]{:S(2)}) collective-permute-start(f32[2,3584]{1,0:T(2,128)S(1)} %get-tuple-element.35.refs_2_), channel_id=1, source_target_pairs={{0,1},{1,0},{2,3},{3,2},{4,5},{5,4},{6,7},{7,6},{8,9},{9,8},{10,11... | collective-permute-start | bytes 86024 | tf_op jit(solution)/shard_map/ppermute | solution.py:32
  80.1 5.9 %collective-permute-start.5 = (f32[64,10752]{1,0:T(8,128)S(1)}, f32[64,10752]{1,0:T(8,128)S(1)}, u32[]{:S(2)}, u32[]{:S(2)}) collective-permute-start(f32[64,10752]{1,0:T(8,128)S(1)} %get-tuple-element.46.own_ref), channel_id=1, source_target_pairs={{0,1},{1,0},{2,3},{3,2},{4,5},{5,4},{6,7},{7,6},{8,9},{9,8},{10,11... | collective-permute-start | bytes 8257544 | tf_op jit(solution)/shard_map/ppermute | solution.py:32
  85.4 2.7 %collective-permute-start.4 = (f32[64,3584]{1,0:T(8,128)S(1)}, f32[64,3584]{1,0:T(8,128)S(1)}, u32[]{:S(2)}, u32[]{:S(2)}) collective-permute-start(f32[64,3584]{1,0:T(8,128)S(1)} %cross.3.own_ref), channel_id=1, source_target_pairs={{0,1},{1,0},{2,3},{3,2},{4,5},{5,4},{6,7},{7,6},{8,9},{9,8},{10,11... | collective-permute-start | bytes 2752520 | tf_op jit(solution)/shard_map/ppermute | solution.py:32

commit v9 on v8

--- a/solution.py
+++ b/solution.py
@@ -16,6 +16,7 @@
 CHUNKS = 4
 KEEP = 3
 PEEK = 3
+TURN = 1
 DEPTH = 4
 SUB = 896
 FINAL = 2048
@@ -39,6 +40,10 @@
 
 def rows_at(j):
     return pl.ds(j * ROWS if isinstance(j, int) else pl.multiple_of(j * ROWS, ROWS), ROWS)
+
+
+def turned(origin, chunk):
+    return origin < TURN and chunk % ROWS == 0
 
 
 def stream_kernel(tokens, chunk, loads, at_chunk, starts, ahead, given, peek, *refs):
@@ -104,11 +109,25 @@
             acc_ref[0:8, here] += jnp.sum(x.reshape(wide), axis=0)
             acc_ref[8:16, here] += jnp.sum((x * x).reshape(wide), axis=0)
 
+    def turn(j):
+        at = rows_at(j)
+        for lo in range(0, chunk, ROWS):
+            buf_ref[into, at, lo : lo + ROWS] = buf_ref[into, at, lo : lo + ROWS].T
+
     def project(j):
         at = rows_at(j)
-        part_here = lax.dot_general(
-            scaled_ref[...], buf_ref[held, at, :], NT, preferred_element_type=F32
-        ) - offset
+        if turned(at_chunk, chunk):
+            part_here = -offset
+            for lo in range(0, chunk, ROWS):
+                part_here = part_here + jnp.dot(
+                    scaled_ref[:, lo : lo + ROWS],
+                    buf_ref[held, at, lo : lo + ROWS],
+                    preferred_element_type=F32,
+                )
+        else:
+            part_here = lax.dot_general(
+                scaled_ref[...], buf_ref[held, at, :], NT, preferred_element_type=F32
+            ) - offset
         if not starts:
             part_here = part_here + part_ref[j]
         proj_ref[j] = part_here.astype(proj_ref.dtype)
@@ -121,11 +140,15 @@
     elif not projects:
         for j in range(given):
             add_sums(j)
+            if turned(loads, chunk):
+                turn(j)
 
         @pl.loop(given, rows)
         def _(j):
             gather(j)
             add_sums(j)
+            if turned(loads, chunk):
+                turn(j)
 
         for copy in copies[rows - given :]:
             copy.wait()

time: 105 us -> 103 us (0.981)
  Pallas kernels: 61.5 us -> 60.2 us
    pallas_call x6, Pallas kernels: 35.7 us -> 34.4 us  [stream(): pl.pallas_call(functools.partial(stream_kernel, tokens, chunk, loads, at,...]
  transfers between devices with their start and end apart: 6 -> 6, of which waited for: 1 -> 1; matrix products, arithmetic and copies ran while one was open for 0% -> 0% of each run, Pallas kernels for 29% -> 28%
where the time goes in v9:
time: 103 us
  Pallas kernels  60.2 us (58%)
  blocking collectives  39.5 us (38%)
  starting transfers between devices  1.91 us (2%)
    pallas_call x6, Pallas kernels, stream(): pl.pallas_call(functools.partial(stream_kernel, tokens, chunk, loads, at,...  34.4 us
    pallas_call x2, Pallas kernels, cross(): pl.pallas_call(functools.partial(cross_kernel, start, last), in_specs=[vm...  19.3 us
    all_to_all x1, blocking collectives, local(): blocks = lax.all_to_all(blocks, 'neuron', 0, 0)  16.2 us
    all_to_all x1, blocking collectives, local(): proj = lax.all_to_all(blocks, 'neuron', 0, 0)  12.4 us
    all_to_all x1, blocking collectives, local(): grams = lax.all_to_all(gram, 'neuron', 0, 0)  10.9 us
    pallas_call x1, Pallas kernels, finish(): pl.pallas_call(functools.partial(finish_kernel, nb), in_specs=[vmem, vmem...  4.51 us
  transfers between devices with their start and end apart: 6, of which 1 were waited for; matrix products, arithmetic and copies ran while one was open for 0% of the time, Pallas kernels for 28%

profile of v9, /device:TPU:0, one launch (start us, length us, event | category | flops | bytes accessed | tf_op | source)
XLA Modules:
  0.0 103.0 jit_solution(14551327385772459054)
XLA Ops:
  0.0 7.3 %stream.6 = (bf16[3,2048,3584]{2,1,0:T(8,128)(2,1)S(1)}, f32[2,3584]{1,0:T(2,128)S(1)}) custom-call(bf16[2048,14336]{1,0:T(8,128)(2,1)} %act_ref.3), custom_call_target="tpu_custom_call" | custom-call | flops 3758096384 | bytes 14680064 | tf_op jit(solution)/shard_map/stream/pallas_call | solution.py:203
  7.4 0.5 collective-permute-start
  7.9 4.3 %stream.7 = (bf16[3,2048,3584]{2,1,0:T(8,128)(2,1)S(1)}, f32[2,3584]{1,0:T(2,128)S(1)}) custom-call(bf16[2048,14336]{1,0:T(8,128)(2,1)} %act_ref.3, bf16[3,2048,3584]{2,1,0:T(8,128)(2,1)S(1)} %get-tuple-element.28.refs_1_), custom_call_target="tpu_custom_call", output_to_operand_aliasing={{0}: (1, {})} | custom-call | flops 3758096384 | bytes 14680064 | tf_op jit(solution)/shard_map/stream/pallas_call | solution.py:203
  12.1 0.1 collective-permute-start.1
  12.3 0.0 collective-permute-done.refs_3_
  12.3 0.3 copy-done
  12.6 6.1 %stream.8 = (bf16[3,2048,3584]{2,1,0:T(8,128)(2,1)S(1)}, f32[2,3584]{1,0:T(2,128)S(1)}, f32[8,64,256]{2,1,0:T(8,128)S(1)}, f32[2,3584]{1,0:T(2,128)S(1)}) custom-call(bf16[2048,14336]{1,0:T(8,128)(2,1)} %act_ref.3, bf16[3,2048,3584]{2,1,0:T(8,128)(2,1)S(1)} %get-tuple-element.29.refs_1_, ...), custom_call_target="tpu_custom_call", output_to_operand_aliasing={{0}: (1, {})} | custom-call | flops 3758096384 | bytes 14680064 | tf_op jit(solution)/shard_map/stream/pallas_call | solution.py:203
  18.7 0.2 collective-permute-start.3
  18.9 0.0 collective-permute-done.1.refs_3_
  18.9 7.7 %stream.9 = (bf16[3,2048,3584]{2,1,0:T(8,128)(2,1)S(1)}, f32[2,3584]{1,0:T(2,128)S(1)}, f32[8,64,256]{2,1,0:T(8,128)S(1)}, f32[2,3584]{1,0:T(2,128)S(1)}) custom-call(bf16[2048,14336]{1,0:T(8,128)(2,1)} %act_ref.3, bf16[3,2048,3584]{2,1,0:T(8,128)(2,1)S(1)} %get-tuple-element.31.refs_1_, ...), custom_call_target="tpu_custom_call", output_to_operand_aliasing={{0}: (1, {})} | custom-call | flops 3758096384 | bytes 14680064 | tf_op jit(solution)/shard_map/stream/pallas_call | solution.py:203
  26.5 0.4 collective-permute-start.2
  27.0 4.5 %stream.10 = (f32[8,64,256]{2,1,0:T(8,128)S(1)}, f32[2,3584]{1,0:T(2,128)S(1)}) custom-call(bf16[3,2048,3584]{2,1,0:T(8,128)(2,1)S(1)} %get-tuple-element.34.refs_0_.refs_1_, f32[2,3584]{1,0:T(2,128)S(1)} %get-tuple-element.36.refs_1_, f32[2,3584]{1,0:T(2,128)S(1)} %collective-permute-done.3.refs_2_, f32[64,14336]{1,0:T(8,128)S(1)} %bitcast.6, ...), custom_call_target="tpu_custom_call" | custom-call | flops 3758096384 | bytes 14680064 | tf_op jit(solution)/shard_map/stream/pallas_call | solution.py:203
  31.5 4.5 %stream.11 = (bf16[8,64,256]{2,1,0:T(8,128)(2,1)S(1)}, f32[2,3584]{1,0:T(2,128)S(1)}, bf16[2048,896]{1,0:T(8,128)(2,1)S(1)}) custom-call(bf16[2048,14336]{1,0:T(8,128)(2,1)} %act_ref.3, bf16[3,2048,3584]{2,1,0:T(8,128)(2,1)S(1)} %get-tuple-element.34.refs_0_.refs_1_, f32[2,3584]{1,0:T(2,128)S(1)} %get-tuple-element.35.refs_2_, ...), custom_call_target="tpu_custom_call" | custom-call | flops 3758096384 | bytes 14680064 | tf_op jit(solution)/shard_map/stream/pallas_call | solution.py:203
  36.1 16.2 %all_to_all.15 = bf16[8,64,256]{2,1,0:T(8,128)(2,1)S(1)} all-to-all(bf16[8,64,256]{2,1,0:T(8,128)(2,1)S(1)} %get-tuple-element.39), channel_id=1, replica_groups=mesh['groups'=2,'neuron'=8,'token'=2] {'neuron'}, dimensions={0} | all-to-all | bytes 524288 | tf_op jit(solution)/shard_map/all_to_all | solution.py:461
  52.3 12.4 %all_to_all.16.proj_ref = bf16[8,64,256]{2,1,0:T(8,128)(2,1)S(1)} all-to-all(bf16[8,64,256]{2,1,0:T(8,128)(2,1)S(1)} %broadcast_in_dim.9), channel_id=1, replica_groups=mesh['groups'=2,'neuron'=8,'token'=2] {'neuron'}, dimensions={0} | all-to-all | bytes 524288 | tf_op jit(solution)/shard_map/all_to_all | solution.py:464
  64.7 14.1 %cross.2 = (f32[64,10752]{1,0:T(8,128)S(1)}, bf16[2048,896]{1,0:T(8,128)(2,1)S(1)}) custom-call(bf16[8,64,256]{2,1,0:T(8,128)(2,1)S(1)} %all_to_all.16.proj_ref, bf16[2048,14336]{1,0:T(8,128)(2,1)} %act_ref.3, bf16[2048,896]{1,0:T(8,128)(2,1)S(1)} %get-tuple-element.40.ahead_ref, f32[2,3584]{1,0:T(2,128)S(1)} %get-tuple-element.41.refs_0_, ...), custom_call_target="tpu_custom_call" | custom-call | flops 11274289152 | bytes 44040192 | tf_op jit(solution)/shard_map/cross/pallas_call | solution.py:265
  78.8 0.1 collective-permute-start.5
  78.9 5.2 %cross.3.own_ref = f32[64,3584]{1,0:T(8,128)S(1)} custom-call(bf16[8,64,256]{2,1,0:T(8,128)(2,1)S(1)} %all_to_all.16.proj_ref, bf16[2048,14336]{1,0:T(8,128)(2,1)} %act_ref.3, bf16[2048,896]{1,0:T(8,128)(2,1)S(1)} %get-tuple-element.44.ahead_ref, f32[2,3584]{1,0:T(2,128)S(1)} %get-tuple-element.45.refs_0_), custom_call_target="tpu_custom_call" | custom-call | flops 3758096384 | bytes 14680064 | tf_op jit(solution)/shard_map/cross/pallas_call | solution.py:265
  84.1 0.6 collective-permute-start.4
  84.7 1.3 %combine.2 = (bf16[128,14336]{1,0:T(8,128)(2,1)S(1)}, f32[32,128]{1,0:T(8,128)S(1)}) custom-call(f32[64,10752]{1,0:T(8,128)S(1)} %get-tuple-element.46.own_ref, f32[64,10752]{1,0:T(8,128)S(1)} %collective-permute-done.5.got_ref, f32[2,3584]{1,0:T(2,128)S(1)} %get-tuple-element.41.refs_0_, f32[2,3584]{1,0:T(2,128)S(1)} %get-tuple-element.42.refs_1_, ...), custom_call_target="tpu_custom_call" | custom-call | flops 352321536 | bytes 8257536 | tf_op jit(solution)/shard_map/combine/pallas_call | solution.py:313
  86.0 0.8 collective-permute-done.4.got_ref
  86.8 0.7 combine.3
  87.5 10.9 %all_to_all.17.gram_ref = f32[8,32,128]{2,1,0:T(8,128)S(1)} all-to-all(f32[8,32,128]{2,1,0:T(8,128)S(1)} %get-tuple-element.49), channel_id=1, replica_groups=mesh['groups'=2,'neuron'=8,'token'=2] {'neuron'}, dimensions={0} | all-to-all | bytes 262144 | tf_op jit(solution)/shard_map/all_to_all | solution.py:480
  98.4 4.5 %finish.1 = f32[64,14336]{1,0:T(8,128)} custom-call(f32[8,32,128]{2,1,0:T(8,128)S(1)} %all_to_all.17.gram_ref, bf16[128,14336]{1,0:T(8,128)(2,1)S(1)} %get-tuple-element.50.both_ref), custom_call_target="tpu_custom_call" | custom-call | tf_op jit(solution)/shard_map/finish/pallas_call | solution.py:417
  (6 shorter events, 0.1 us)
Async XLA Ops:
  7.4 4.9 %collective-permute-start = (f32[2,3584]{1,0:T(2,128)S(1)}, f32[2,3584]{1,0:T(2,128)S(1)}, u32[]{:S(2)}, u32[]{:S(2)}) collective-permute-start(f32[2,3584]{1,0:T(2,128)S(1)} %get-tuple-element.30.refs_2_), channel_id=1, source_target_pairs={{0,1},{1,0},{2,3},{3,2},{4,5},{5,4},{6,7},{7,6},{8,9},{9,8},{10,11... | collective-permute-start | bytes 86024 | tf_op jit(solution)/shard_map/ppermute | solution.py:33
  7.9 4.7 %copy-start = (f32[14336,64]{0,1:T(8,128)S(1)}, f32[14336,64]{0,1:T(8,128)}, u32[]{:S(2)}) copy-start(f32[14336,64]{0,1:T(8,128)} %param.3) | copy-start | bytes 11010052
  12.1 6.7 %collective-permute-start.1 = (f32[2,3584]{1,0:T(2,128)S(1)}, f32[2,3584]{1,0:T(2,128)S(1)}, u32[]{:S(2)}, u32[]{:S(2)}) collective-permute-start(f32[2,3584]{1,0:T(2,128)S(1)} %get-tuple-element.32.refs_2_), channel_id=1, source_target_pairs={{0,1},{1,0},{2,3},{3,2},{4,5},{5,4},{6,7},{7,6},{8,9},{9,8},{10,11... | collective-permute-start | bytes 86024 | tf_op jit(solution)/shard_map/ppermute | solution.py:33
  18.7 8.3 %collective-permute-start.3 = (f32[2,3584]{1,0:T(2,128)S(1)}, f32[2,3584]{1,0:T(2,128)S(1)}, u32[]{:S(2)}, u32[]{:S(2)}) collective-permute-start(f32[2,3584]{1,0:T(2,128)S(1)} %get-tuple-element.36.refs_1_), channel_id=1, source_target_pairs={{0,1},{1,0},{2,3},{3,2},{4,5},{5,4},{6,7},{7,6},{8,9},{9,8},{10,11... | collective-permute-start | bytes 86024 | tf_op jit(solution)/shard_map/ppermute | solution.py:33
  26.5 5.0 %collective-permute-start.2 = (f32[2,3584]{1,0:T(2,128)S(1)}, f32[2,3584]{1,0:T(2,128)S(1)}, u32[]{:S(2)}, u32[]{:S(2)}) collective-permute-start(f32[2,3584]{1,0:T(2,128)S(1)} %get-tuple-element.35.refs_2_), channel_id=1, source_target_pairs={{0,1},{1,0},{2,3},{3,2},{4,5},{5,4},{6,7},{7,6},{8,9},{9,8},{10,11... | collective-permute-start | bytes 86024 | tf_op jit(solution)/shard_map/ppermute | solution.py:33
  78.8 5.9 %collective-permute-start.5 = (f32[64,10752]{1,0:T(8,128)S(1)}, f32[64,10752]{1,0:T(8,128)S(1)}, u32[]{:S(2)}, u32[]{:S(2)}) collective-permute-start(f32[64,10752]{1,0:T(8,128)S(1)} %get-tuple-element.46.own_ref), channel_id=1, source_target_pairs={{0,1},{1,0},{2,3},{3,2},{4,5},{5,4},{6,7},{7,6},{8,9},{9,8},{10,11... | collective-permute-start | bytes 8257544 | tf_op jit(solution)/shard_map/ppermute | solution.py:33
  84.1 2.7 %collective-permute-start.4 = (f32[64,3584]{1,0:T(8,128)S(1)}, f32[64,3584]{1,0:T(8,128)S(1)}, u32[]{:S(2)}, u32[]{:S(2)}) collective-permute-start(f32[64,3584]{1,0:T(8,128)S(1)} %cross.3.own_ref), channel_id=1, source_target_pairs={{0,1},{1,0},{2,3},{3,2},{4,5},{5,4},{6,7},{7,6},{8,9},{9,8},{10,11... | collective-permute-start | bytes 2752520 | tf_op jit(solution)/shard_map/ppermute | solution.py:33

commit v10 on v9

--- a/solution.py
+++ b/solution.py
@@ -15,9 +15,9 @@
 ROWS = 256
 CHUNKS = 4
 KEEP = 3
-PEEK = 3
+PEEK = 4
 TURN = 1
-DEPTH = 4
+DEPTH = 3
 SUB = 896
 FINAL = 2048
 LANES = 512

time: 103 us -> 103 us (level)
  no operation moved by 1% of the time
where the time goes in v10:
time: 103 us
  Pallas kernels  60 us (58%)
  blocking collectives  39.6 us (38%)
  starting transfers between devices  1.92 us (2%)
    pallas_call x6, Pallas kernels, stream(): pl.pallas_call(functools.partial(stream_kernel, tokens, chunk, loads, at,...  34.2 us
    pallas_call x2, Pallas kernels, cross(): pl.pallas_call(functools.partial(cross_kernel, start, last), in_specs=[vm...  19.3 us
    all_to_all x1, blocking collectives, local(): blocks = lax.all_to_all(blocks, 'neuron', 0, 0)  16.2 us
    all_to_all x1, blocking collectives, local(): proj = lax.all_to_all(blocks, 'neuron', 0, 0)  12.5 us
    all_to_all x1, blocking collectives, local(): grams = lax.all_to_all(gram, 'neuron', 0, 0)  10.9 us
    pallas_call x1, Pallas kernels, finish(): pl.pallas_call(functools.partial(finish_kernel, nb), in_specs=[vmem, vmem...  4.51 us
  transfers between devices with their start and end apart: 6, of which 1 were waited for; matrix products, arithmetic and copies ran while one was open for 0% of the time, Pallas kernels for 28%

profile of v10, /device:TPU:0, one launch (start us, length us, event | category | flops | bytes accessed | tf_op | source)
XLA Modules:
  0.0 102.9 jit_solution(8881535935374272947)
XLA Ops:
  0.0 7.6 %stream.6 = (bf16[3,2048,3584]{2,1,0:T(8,128)(2,1)S(1)}, f32[2,3584]{1,0:T(2,128)S(1)}) custom-call(bf16[2048,14336]{1,0:T(8,128)(2,1)} %act_ref.3), custom_call_target="tpu_custom_call" | custom-call | flops 3758096384 | bytes 14680064 | tf_op jit(solution)/shard_map/stream/pallas_call | solution.py:203
  7.6 0.5 collective-permute-start
  8.2 3.7 %stream.7 = (bf16[3,2048,3584]{2,1,0:T(8,128)(2,1)S(1)}, f32[2,3584]{1,0:T(2,128)S(1)}) custom-call(bf16[2048,14336]{1,0:T(8,128)(2,1)} %act_ref.3, bf16[3,2048,3584]{2,1,0:T(8,128)(2,1)S(1)} %get-tuple-element.28.refs_1_), custom_call_target="tpu_custom_call", output_to_operand_aliasing={{0}: (1, {})} | custom-call | flops 3758096384 | bytes 14680064 | tf_op jit(solution)/shard_map/stream/pallas_call | solution.py:203
  11.9 0.1 collective-permute-start.1
  12.0 0.0 collective-permute-done.refs_3_
  12.0 0.3 copy-done
  12.4 6.1 %stream.8 = (bf16[3,2048,3584]{2,1,0:T(8,128)(2,1)S(1)}, f32[2,3584]{1,0:T(2,128)S(1)}, f32[8,64,256]{2,1,0:T(8,128)S(1)}, f32[2,3584]{1,0:T(2,128)S(1)}) custom-call(bf16[2048,14336]{1,0:T(8,128)(2,1)} %act_ref.3, bf16[3,2048,3584]{2,1,0:T(8,128)(2,1)S(1)} %get-tuple-element.29.refs_1_, ...), custom_call_target="tpu_custom_call", output_to_operand_aliasing={{0}: (1, {})} | custom-call | flops 3758096384 | bytes 14680064 | tf_op jit(solution)/shard_map/stream/pallas_call | solution.py:203
  18.4 0.2 collective-permute-start.3
  18.6 0.0 collective-permute-done.1.refs_3_
  18.6 7.7 %stream.9 = (bf16[3,2048,3584]{2,1,0:T(8,128)(2,1)S(1)}, f32[2,3584]{1,0:T(2,128)S(1)}, f32[8,64,256]{2,1,0:T(8,128)S(1)}, f32[2,3584]{1,0:T(2,128)S(1)}) custom-call(bf16[2048,14336]{1,0:T(8,128)(2,1)} %act_ref.3, bf16[3,2048,3584]{2,1,0:T(8,128)(2,1)S(1)} %get-tuple-element.31.refs_1_, ...), custom_call_target="tpu_custom_call", output_to_operand_aliasing={{0}: (1, {})} | custom-call | flops 3758096384 | bytes 14680064 | tf_op jit(solution)/shard_map/stream/pallas_call | solution.py:203
  26.3 0.5 collective-permute-start.2
  26.8 4.5 %stream.10 = (f32[8,64,256]{2,1,0:T(8,128)S(1)}, f32[2,3584]{1,0:T(2,128)S(1)}) custom-call(bf16[3,2048,3584]{2,1,0:T(8,128)(2,1)S(1)} %get-tuple-element.34.refs_0_.refs_1_, f32[2,3584]{1,0:T(2,128)S(1)} %get-tuple-element.36.refs_1_, f32[2,3584]{1,0:T(2,128)S(1)} %collective-permute-done.3.refs_2_, f32[64,14336]{1,0:T(8,128)S(1)} %bitcast.6, ...), custom_call_target="tpu_custom_call" | custom-call | flops 3758096384 | bytes 14680064 | tf_op jit(solution)/shard_map/stream/pallas_call | solution.py:203
  31.3 4.5 %stream.11 = (bf16[8,64,256]{2,1,0:T(8,128)(2,1)S(1)}, f32[2,3584]{1,0:T(2,128)S(1)}, bf16[2048,896]{1,0:T(8,128)(2,1)S(1)}) custom-call(bf16[2048,14336]{1,0:T(8,128)(2,1)} %act_ref.3, bf16[3,2048,3584]{2,1,0:T(8,128)(2,1)S(1)} %get-tuple-element.34.refs_0_.refs_1_, f32[2,3584]{1,0:T(2,128)S(1)} %get-tuple-element.35.refs_2_, ...), custom_call_target="tpu_custom_call" | custom-call | flops 3758096384 | bytes 14680064 | tf_op jit(solution)/shard_map/stream/pallas_call | solution.py:203
  35.8 16.2 %all_to_all.15 = bf16[8,64,256]{2,1,0:T(8,128)(2,1)S(1)} all-to-all(bf16[8,64,256]{2,1,0:T(8,128)(2,1)S(1)} %get-tuple-element.39), channel_id=1, replica_groups=mesh['groups'=2,'neuron'=8,'token'=2] {'neuron'}, dimensions={0} | all-to-all | bytes 524288 | tf_op jit(solution)/shard_map/all_to_all | solution.py:461
  52.1 12.5 %all_to_all.16.proj_ref = bf16[8,64,256]{2,1,0:T(8,128)(2,1)S(1)} all-to-all(bf16[8,64,256]{2,1,0:T(8,128)(2,1)S(1)} %broadcast_in_dim.9), channel_id=1, replica_groups=mesh['groups'=2,'neuron'=8,'token'=2] {'neuron'}, dimensions={0} | all-to-all | bytes 524288 | tf_op jit(solution)/shard_map/all_to_all | solution.py:464
  64.6 14.1 %cross.2 = (f32[64,10752]{1,0:T(8,128)S(1)}, bf16[2048,896]{1,0:T(8,128)(2,1)S(1)}) custom-call(bf16[8,64,256]{2,1,0:T(8,128)(2,1)S(1)} %all_to_all.16.proj_ref, bf16[2048,14336]{1,0:T(8,128)(2,1)} %act_ref.3, bf16[2048,896]{1,0:T(8,128)(2,1)S(1)} %get-tuple-element.40.ahead_ref, f32[2,3584]{1,0:T(2,128)S(1)} %get-tuple-element.41.refs_0_, ...), custom_call_target="tpu_custom_call" | custom-call | flops 11274289152 | bytes 44040192 | tf_op jit(solution)/shard_map/cross/pallas_call | solution.py:265
  78.7 0.1 collective-permute-start.5
  78.7 5.2 %cross.3.own_ref = f32[64,3584]{1,0:T(8,128)S(1)} custom-call(bf16[8,64,256]{2,1,0:T(8,128)(2,1)S(1)} %all_to_all.16.proj_ref, bf16[2048,14336]{1,0:T(8,128)(2,1)} %act_ref.3, bf16[2048,896]{1,0:T(8,128)(2,1)S(1)} %get-tuple-element.44.ahead_ref, f32[2,3584]{1,0:T(2,128)S(1)} %get-tuple-element.45.refs_0_), custom_call_target="tpu_custom_call" | custom-call | flops 3758096384 | bytes 14680064 | tf_op jit(solution)/shard_map/cross/pallas_call | solution.py:265
  84.0 0.6 collective-permute-start.4
  84.5 1.3 %combine.2 = (bf16[128,14336]{1,0:T(8,128)(2,1)S(1)}, f32[32,128]{1,0:T(8,128)S(1)}) custom-call(f32[64,10752]{1,0:T(8,128)S(1)} %get-tuple-element.46.own_ref, f32[64,10752]{1,0:T(8,128)S(1)} %collective-permute-done.5.got_ref, f32[2,3584]{1,0:T(2,128)S(1)} %get-tuple-element.41.refs_0_, f32[2,3584]{1,0:T(2,128)S(1)} %get-tuple-element.42.refs_1_, ...), custom_call_target="tpu_custom_call" | custom-call | flops 352321536 | bytes 8257536 | tf_op jit(solution)/shard_map/combine/pallas_call | solution.py:313
  85.9 0.8 collective-permute-done.4.got_ref
  86.6 0.7 combine.3
  87.3 10.9 %all_to_all.17.gram_ref = f32[8,32,128]{2,1,0:T(8,128)S(1)} all-to-all(f32[8,32,128]{2,1,0:T(8,128)S(1)} %get-tuple-element.49), channel_id=1, replica_groups=mesh['groups'=2,'neuron'=8,'token'=2] {'neuron'}, dimensions={0} | all-to-all | bytes 262144 | tf_op jit(solution)/shard_map/all_to_all | solution.py:480
  98.2 4.5 %finish.1 = f32[64,14336]{1,0:T(8,128)} custom-call(f32[8,32,128]{2,1,0:T(8,128)S(1)} %all_to_all.17.gram_ref, bf16[128,14336]{1,0:T(8,128)(2,1)S(1)} %get-tuple-element.50.both_ref), custom_call_target="tpu_custom_call" | custom-call | tf_op jit(solution)/shard_map/finish/pallas_call | solution.py:417
  (6 shorter events, 0.1 us)
Async XLA Ops:
  7.6 4.4 %collective-permute-start = (f32[2,3584]{1,0:T(2,128)S(1)}, f32[2,3584]{1,0:T(2,128)S(1)}, u32[]{:S(2)}, u32[]{:S(2)}) collective-permute-start(f32[2,3584]{1,0:T(2,128)S(1)} %get-tuple-element.30.refs_2_), channel_id=1, source_target_pairs={{0,1},{1,0},{2,3},{3,2},{4,5},{5,4},{6,7},{7,6},{8,9},{9,8},{10,11... | collective-permute-start | bytes 86024 | tf_op jit(solution)/shard_map/ppermute | solution.py:33
  8.2 4.2 %copy-start = (f32[14336,64]{0,1:T(8,128)S(1)}, f32[14336,64]{0,1:T(8,128)}, u32[]{:S(2)}) copy-start(f32[14336,64]{0,1:T(8,128)} %param.3) | copy-start | bytes 11010052
  11.9 6.7 %collective-permute-start.1 = (f32[2,3584]{1,0:T(2,128)S(1)}, f32[2,3584]{1,0:T(2,128)S(1)}, u32[]{:S(2)}, u32[]{:S(2)}) collective-permute-start(f32[2,3584]{1,0:T(2,128)S(1)} %get-tuple-element.32.refs_2_), channel_id=1, source_target_pairs={{0,1},{1,0},{2,3},{3,2},{4,5},{5,4},{6,7},{7,6},{8,9},{9,8},{10,11... | collective-permute-start | bytes 86024 | tf_op jit(solution)/shard_map/ppermute | solution.py:33
  18.4 8.3 %collective-permute-start.3 = (f32[2,3584]{1,0:T(2,128)S(1)}, f32[2,3584]{1,0:T(2,128)S(1)}, u32[]{:S(2)}, u32[]{:S(2)}) collective-permute-start(f32[2,3584]{1,0:T(2,128)S(1)} %get-tuple-element.36.refs_1_), channel_id=1, source_target_pairs={{0,1},{1,0},{2,3},{3,2},{4,5},{5,4},{6,7},{7,6},{8,9},{9,8},{10,11... | collective-permute-start | bytes 86024 | tf_op jit(solution)/shard_map/ppermute | solution.py:33
  26.3 5.0 %collective-permute-start.2 = (f32[2,3584]{1,0:T(2,128)S(1)}, f32[2,3584]{1,0:T(2,128)S(1)}, u32[]{:S(2)}, u32[]{:S(2)}) collective-permute-start(f32[2,3584]{1,0:T(2,128)S(1)} %get-tuple-element.35.refs_2_), channel_id=1, source_target_pairs={{0,1},{1,0},{2,3},{3,2},{4,5},{5,4},{6,7},{7,6},{8,9},{9,8},{10,11... | collective-permute-start | bytes 86024 | tf_op jit(solution)/shard_map/ppermute | solution.py:33
  78.7 5.9 %collective-permute-start.5 = (f32[64,10752]{1,0:T(8,128)S(1)}, f32[64,10752]{1,0:T(8,128)S(1)}, u32[]{:S(2)}, u32[]{:S(2)}) collective-permute-start(f32[64,10752]{1,0:T(8,128)S(1)} %get-tuple-element.46.own_ref), channel_id=1, source_target_pairs={{0,1},{1,0},{2,3},{3,2},{4,5},{5,4},{6,7},{7,6},{8,9},{9,8},{10,11... | collective-permute-start | bytes 8257544 | tf_op jit(solution)/shard_map/ppermute | solution.py:33
  84.0 2.7 %collective-permute-start.4 = (f32[64,3584]{1,0:T(8,128)S(1)}, f32[64,3584]{1,0:T(8,128)S(1)}, u32[]{:S(2)}, u32[]{:S(2)}) collective-permute-start(f32[64,3584]{1,0:T(8,128)S(1)} %cross.3.own_ref), channel_id=1, source_target_pairs={{0,1},{1,0},{2,3},{3,2},{4,5},{5,4},{6,7},{7,6},{8,9},{9,8},{10,11... | collective-permute-start | bytes 2752520 | tf_op jit(solution)/shard_map/ppermute | solution.py:33
